TPU v7x, 32 devices: a whole 2x2x4 slice. The times are simulated.
32 devices in a mesh: dp: 4 (over z), seq: 8 (over y, x, core).
Axes of the slice: x: 2, y: 2, z: 4, core: 2. Of those that a mesh axis runs over, the one named last changes fastest.
Arguments:
- tokens: bfloat16 [8192, 768], P(('dp', 'seq')), may hold values from -6 to 6
- doc_ids: int32 [8192], P(('dp', 'seq')), may hold values from 0 to 1, as said below
- cotangent: bfloat16 [8192, 768], P(('dp', 'seq')), may hold values from -6 to 6
- w_qkv: bfloat16 [768, 2304], P(('dp', 'seq')), may hold values from -0.3125 to 0.3125
- bias_qv: bfloat16 [2, 768], P(None, ('dp', 'seq')), may hold values from -3 to 3
- w_o: bfloat16 [768, 768], P(('dp', 'seq')), may hold values from -0.875 to 0.875
- bias_o: bfloat16 [768], P(('dp', 'seq')), may hold values from -2 to 2
- ln_gain: bfloat16 [2, 768], P(None, ('dp', 'seq')), may hold values from 0.25 to 1.75
- ln_bias: bfloat16 [2, 768], P(None, ('dp', 'seq')), may hold values from -2 to 2
- w_in: bfloat16 [768, 3072], P(('dp', 'seq')), may hold values from -0.21875 to 0.21875
- bias_in: bfloat16 [3072], P(('dp', 'seq')), may hold values from -3 to 3
- w_out: bfloat16 [3072, 768], P(('dp', 'seq')), may hold values from -0.109375 to 0.109375
- bias_out: bfloat16 [768], P(('dp', 'seq')), may hold values from -2 to 2
Outputs:
- block_out: bfloat16 [8192, 768], P(('dp', 'seq'))
- input_grad: float32 [8192, 768], P(('dp', 'seq'))
- grad_w_qkv: float32 [768, 2304], P(('dp', 'seq'))
- grad_bias_qv: float32 [2, 768], P(None, ('dp', 'seq'))
- grad_w_o: float32 [768, 768], P(('dp', 'seq'))
- grad_bias_o: float32 [768], P(('dp', 'seq'))
- grad_ln_gain: float32 [2, 768], P(None, ('dp', 'seq'))
- grad_ln_bias: float32 [2, 768], P(None, ('dp', 'seq'))
- grad_w_in: float32 [768, 3072], P(('dp', 'seq'))
- grad_bias_in: float32 [3072], P(('dp', 'seq'))
- grad_w_out: float32 [3072, 768], P(('dp', 'seq'))
- grad_bias_out: float32 [768], P(('dp', 'seq'))
Inputs may be any that keep to these rules, and one draw needn't show every extreme that they name: `doc_ids`: each stream holds exactly two sequences: ids 0 then 1, never falling; the first covers b whole aligned blocks of 256 positions, with 1 <= b <= 2, and the second the rest of the stream.
All inputs are finite; a program needn't handle non-finite values.
Results may differ from a plain program's by a relative error of at most 0.02.
The roundings to bfloat16 on the way count: a program that leaves them out, or rounds other values in their place, can miss the bound.
Values may be sent and summed in bfloat16 or wider, within the bound.
No kernel may reach another device: no remote copies, remote signals or barrier semaphores. Data moves between devices by JAX's collectives and lax.ppermute only.
A program may use at most 192 MiB of HBM per device.

v0:
```python
import math

import jax
import jax.numpy as jnp
from jax import lax
from jax.sharding import PartitionSpec as P

HEADS = 12
HDIM = 64
BLK = 256


EPSILON = 1e-12
NEG_LARGE = -1e30


def layer_norm(resid, gain, shift):
    center = resid - jnp.mean(resid, axis=-1, keepdims=True)
    spread = jnp.mean(center * center, axis=-1, keepdims=True)
    return center * lax.rsqrt(spread + EPSILON) * gain + shift


def exact_gelu(value):
    return jax.nn.gelu(value, approximate=False)


def split_heads(matrix):
    return matrix.reshape(matrix.shape[0], HEADS, HDIM)


def allowed_pairs(query_doc, query_block, key_doc, key_block):
    return (query_doc[:, None] == key_doc[None, :]) & (key_block[None, :] <= query_block[:, None])


def over_parts(carry, arrays, update):
    count = arrays[0].shape[0]
    span = math.gcd(count, 1024)
    steps = count // span
    offsets = jnp.arange(steps, dtype=jnp.int32) * span
    parts = tuple((a.reshape((steps, span) + a.shape[1:]) for a in arrays))

    def inner(state, items):
        return (update(state, items[:-1], items[-1]), None)

    carry, unused = lax.scan(inner, carry, parts + (offsets,))
    return carry


def score_grads(query_heads, grad_heads, log_total, delta, allowed, key_heads, value_heads):
    raw = (
        jnp.einsum("qhd,khd->hqk", query_heads, key_heads, preferred_element_type=jnp.float32)
        * 0.125
    )
    probs = jnp.where(allowed[None], jnp.exp(raw - log_total[:, :, None]), 0.0)
    grad_probs = jnp.einsum(
        "qhd,khd->hqk", grad_heads, value_heads, preferred_element_type=jnp.float32
    )
    grad_scores = (probs * (grad_probs - delta[:, :, None]) * 0.125).astype(jnp.bfloat16)
    grad_query = jnp.einsum(
        "hqk,khd->qhd", grad_scores, key_heads, preferred_element_type=jnp.float32
    )
    grad_key = jnp.einsum(
        "hqk,qhd->khd", grad_scores, query_heads, preferred_element_type=jnp.float32
    )
    grad_value = jnp.einsum(
        "hqk,qhd->khd", probs.astype(jnp.bfloat16), grad_heads, preferred_element_type=jnp.float32
    )
    return (grad_query, grad_key, grad_value)


def on_device(
    tokens,
    doc_ids,
    cotangent,
    w_qkv,
    bias_qv,
    w_o,
    bias_o,
    ln_gain,
    ln_bias,
    w_in,
    bias_in,
    w_out,
    bias_out,
):
    rows = tokens.shape[0]
    width = tokens.shape[1]
    full = (
        lax.all_gather(w_qkv, ("dp", "seq"), axis=0, tiled=True),
        lax.all_gather(bias_qv, ("dp", "seq"), axis=1, tiled=True),
        lax.all_gather(w_o, ("dp", "seq"), axis=0, tiled=True),
        lax.all_gather(bias_o, ("dp", "seq"), axis=0, tiled=True),
        lax.all_gather(ln_gain, ("dp", "seq"), axis=1, tiled=True),
        lax.all_gather(ln_bias, ("dp", "seq"), axis=1, tiled=True),
        lax.all_gather(w_in, ("dp", "seq"), axis=0, tiled=True),
        lax.all_gather(bias_in, ("dp", "seq"), axis=0, tiled=True),
        lax.all_gather(w_out, ("dp", "seq"), axis=0, tiled=True),
        lax.all_gather(bias_out, ("dp", "seq"), axis=0, tiled=True),
    )
    (
        full_qkv,
        full_bias_qv,
        full_o,
        full_bias_o,
        full_gain,
        full_shift,
        full_in,
        full_bias_in,
        full_out,
        full_bias_out,
    ) = full
    positions = lax.axis_index("seq") * rows + jnp.arange(rows, dtype=jnp.int32)
    query_block = positions // BLK
    bias_three = jnp.concatenate(
        [
            full_bias_qv[0].astype(jnp.float32),
            jnp.zeros((width,), jnp.float32),
            full_bias_qv[1].astype(jnp.float32),
        ]
    )
    projected = (jnp.dot(tokens, full_qkv, preferred_element_type=jnp.float32) + bias_three).astype(
        jnp.bfloat16
    )
    queries = projected[:, :width]
    keys = projected[:, width : 2 * width]
    values = projected[:, 2 * width :]
    query_heads = split_heads(queries)

    def forward_update(state, parts, first):
        key_rows, value_rows, key_doc = parts
        count = key_rows.shape[0]
        key_block = (first + jnp.arange(count, dtype=jnp.int32)) // BLK
        allowed = allowed_pairs(doc_ids, query_block, key_doc, key_block)
        raw = (
            jnp.einsum(
                "qhd,khd->hqk",
                query_heads,
                split_heads(key_rows),
                preferred_element_type=jnp.float32,
            )
            * 0.125
        )
        masked = jnp.where(allowed[None], raw, NEG_LARGE)
        top, total, summed = state
        new_top = jnp.maximum(top, jnp.max(masked, axis=-1))
        weights = jnp.where(allowed[None], jnp.exp(masked - new_top[:, :, None]), 0.0)
        factor = jnp.exp(top - new_top)
        total = total * factor + jnp.sum(weights, axis=-1)
        summed = summed * factor[:, :, None] + jnp.einsum(
            "hqk,khd->hqd",
            weights.astype(jnp.bfloat16),
            split_heads(value_rows),
            preferred_element_type=jnp.float32,
        )
        return (new_top, total, summed)

    start_state = (
        jnp.full((HEADS, rows), NEG_LARGE, jnp.float32),
        jnp.zeros((HEADS, rows), jnp.float32),
        jnp.zeros((HEADS, rows, HDIM), jnp.float32),
    )
    top, total, summed = over_parts(
        start_state,
        (
            lax.all_gather(keys, "seq", axis=0, tiled=True),
            lax.all_gather(values, "seq", axis=0, tiled=True),
            lax.all_gather(doc_ids, "seq", axis=0, tiled=True),
        ),
        forward_update,
    )
    attn_heads = summed / total[:, :, None]
    log_total = top + jnp.log(total)
    attended_low = attn_heads.transpose(1, 0, 2).reshape(rows, width).astype(jnp.bfloat16)
    resid_one = (
        tokens.astype(jnp.float32)
        + jnp.dot(attended_low, full_o, preferred_element_type=jnp.float32)
        + full_bias_o.astype(jnp.float32)
    )
    hidden_one, norm_one_pull = jax.vjp(
        layer_norm, resid_one, full_gain[0].astype(jnp.float32), full_shift[0].astype(jnp.float32)
    )
    hidden_low = hidden_one.astype(jnp.bfloat16)
    pre_act = jnp.dot(
        hidden_low, full_in, preferred_element_type=jnp.float32
    ) + full_bias_in.astype(jnp.float32)
    activated, gelu_pull = jax.vjp(exact_gelu, pre_act)
    act_low = activated.astype(jnp.bfloat16)
    resid_two = (
        hidden_one
        + jnp.dot(act_low, full_out, preferred_element_type=jnp.float32)
        + full_bias_out.astype(jnp.float32)
    )
    normed, norm_two_pull = jax.vjp(
        layer_norm, resid_two, full_gain[1].astype(jnp.float32), full_shift[1].astype(jnp.float32)
    )
    block_out = normed.astype(jnp.bfloat16)
    again = (
        lax.all_gather(w_qkv, ("dp", "seq"), axis=0, tiled=True),
        lax.all_gather(bias_qv, ("dp", "seq"), axis=1, tiled=True),
        lax.all_gather(w_o, ("dp", "seq"), axis=0, tiled=True),
        lax.all_gather(bias_o, ("dp", "seq"), axis=0, tiled=True),
        lax.all_gather(ln_gain, ("dp", "seq"), axis=1, tiled=True),
        lax.all_gather(ln_bias, ("dp", "seq"), axis=1, tiled=True),
        lax.all_gather(w_in, ("dp", "seq"), axis=0, tiled=True),
        lax.all_gather(bias_in, ("dp", "seq"), axis=0, tiled=True),
        lax.all_gather(w_out, ("dp", "seq"), axis=0, tiled=True),
        lax.all_gather(bias_out, ("dp", "seq"), axis=0, tiled=True),
    )
    back_qkv = again[0]
    back_o = again[2]
    back_in = again[6]
    back_out = again[8]
    grad_resid_two, grad_gain_two, grad_shift_two = norm_two_pull(cotangent.astype(jnp.float32))
    grad_two_low = grad_resid_two.astype(jnp.bfloat16)
    grad_w_out = jnp.einsum("tf,td->fd", act_low, grad_two_low, preferred_element_type=jnp.float32)
    grad_bias_out = jnp.sum(grad_resid_two, axis=0)
    grad_act = jnp.einsum("td,fd->tf", grad_two_low, back_out, preferred_element_type=jnp.float32)
    (grad_pre,) = gelu_pull(grad_act)
    grad_pre_low = grad_pre.astype(jnp.bfloat16)
    grad_w_in = jnp.einsum(
        "td,tf->df", hidden_low, grad_pre_low, preferred_element_type=jnp.float32
    )
    grad_bias_in = jnp.sum(grad_pre, axis=0)
    grad_hidden = (
        jnp.einsum("tf,df->td", grad_pre_low, back_in, preferred_element_type=jnp.float32)
        + grad_resid_two
    )
    grad_resid_one, grad_gain_one, grad_shift_one = norm_one_pull(grad_hidden)
    grad_one_low = grad_resid_one.astype(jnp.bfloat16)
    grad_w_o = jnp.einsum(
        "te,td->ed", attended_low, grad_one_low, preferred_element_type=jnp.float32
    )
    grad_bias_o = jnp.sum(grad_resid_one, axis=0)
    grad_attn_low = jnp.einsum(
        "td,ed->te", grad_one_low, back_o, preferred_element_type=jnp.float32
    ).astype(jnp.bfloat16)
    grad_heads = split_heads(grad_attn_low)
    delta = jnp.sum(grad_heads.astype(jnp.float32).transpose(1, 0, 2) * attn_heads, axis=-1)
    keys_all, values_all, docs_all = (
        lax.all_gather(keys, "seq", axis=0, tiled=True),
        lax.all_gather(values, "seq", axis=0, tiled=True),
        lax.all_gather(doc_ids, "seq", axis=0, tiled=True),
    )
    length = keys_all.shape[0]
    span = math.gcd(length, 1024)
    steps = length // span
    offsets = jnp.arange(steps, dtype=jnp.int32) * span

    def back_step(grad_query, items):
        key_rows, value_rows, key_doc, first = items
        key_block = (first + jnp.arange(span, dtype=jnp.int32)) // BLK
        allowed = allowed_pairs(doc_ids, query_block, key_doc, key_block)
        part_query, part_key, part_value = score_grads(
            query_heads,
            grad_heads,
            log_total,
            delta,
            allowed,
            split_heads(key_rows),
            split_heads(value_rows),
        )
        return (
            grad_query + part_query,
            (part_key.reshape(span, width), part_value.reshape(span, width)),
        )

    grad_query, (key_terms, value_terms) = lax.scan(
        back_step,
        jnp.zeros((rows, HEADS, HDIM), jnp.float32),
        (
            keys_all.reshape(steps, span, width),
            values_all.reshape(steps, span, width),
            docs_all.reshape(steps, span),
            offsets,
        ),
    )
    grad_keys, grad_values = (
        lax.psum_scatter(
            key_terms.reshape(length, width).astype(jnp.bfloat16),
            "seq",
            scatter_dimension=0,
            tiled=True,
        ).astype(jnp.float32),
        lax.psum_scatter(
            value_terms.reshape(length, width).astype(jnp.bfloat16),
            "seq",
            scatter_dimension=0,
            tiled=True,
        ).astype(jnp.float32),
    )
    grad_queries = grad_query.reshape(rows, width)
    grad_qkv_low = jnp.concatenate([grad_queries, grad_keys, grad_values], axis=1).astype(
        jnp.bfloat16
    )
    grad_w_qkv = jnp.einsum("td,te->de", tokens, grad_qkv_low, preferred_element_type=jnp.float32)
    grad_bias_qv = jnp.stack([jnp.sum(grad_queries, axis=0), jnp.sum(grad_values, axis=0)])
    input_grad = (
        jnp.einsum("te,de->td", grad_qkv_low, back_qkv, preferred_element_type=jnp.float32)
        + grad_resid_one
    )
    grad_gain = jnp.stack([grad_gain_one, grad_gain_two])
    grad_shift = jnp.stack([grad_shift_one, grad_shift_two])
    owned = (
        lax.psum_scatter(grad_w_qkv, ("dp", "seq"), scatter_dimension=0, tiled=True),
        lax.psum_scatter(grad_bias_qv, ("dp", "seq"), scatter_dimension=1, tiled=True),
        lax.psum_scatter(grad_w_o, ("dp", "seq"), scatter_dimension=0, tiled=True),
        lax.psum_scatter(grad_bias_o, ("dp", "seq"), scatter_dimension=0, tiled=True),
        lax.psum_scatter(grad_gain, ("dp", "seq"), scatter_dimension=1, tiled=True),
        lax.psum_scatter(grad_shift, ("dp", "seq"), scatter_dimension=1, tiled=True),
        lax.psum_scatter(grad_w_in, ("dp", "seq"), scatter_dimension=0, tiled=True),
        lax.psum_scatter(grad_bias_in, ("dp", "seq"), scatter_dimension=0, tiled=True),
        lax.psum_scatter(grad_w_out, ("dp", "seq"), scatter_dimension=0, tiled=True),
        lax.psum_scatter(grad_bias_out, ("dp", "seq"), scatter_dimension=0, tiled=True),
    )
    return (
        block_out,
        input_grad,
        owned[0],
        owned[1],
        owned[2],
        owned[3],
        owned[4],
        owned[5],
        owned[6],
        owned[7],
        owned[8],
        owned[9],
    )


def solution(mesh):
    placed = (
        P(("dp", "seq"), None),
        P(("dp", "seq")),
        P(("dp", "seq"), None),
        P(("dp", "seq"), None),
        P(None, ("dp", "seq")),
        P(("dp", "seq"), None),
        P(("dp", "seq")),
        P(None, ("dp", "seq")),
        P(None, ("dp", "seq")),
        P(("dp", "seq"), None),
        P(("dp", "seq")),
        P(("dp", "seq"), None),
        P(("dp", "seq")),
    )
    return jax.shard_map(
        on_device,
        mesh=mesh,
        in_specs=placed,
        out_specs=(
            P(("dp", "seq"), None),
            P(("dp", "seq"), None),
            P(("dp", "seq"), None),
            P(None, ("dp", "seq")),
            P(("dp", "seq"), None),
            P(("dp", "seq")),
            P(None, ("dp", "seq")),
            P(None, ("dp", "seq")),
            P(("dp", "seq"), None),
            P(("dp", "seq")),
            P(("dp", "seq"), None),
            P(("dp", "seq")),
        ),
        check_vma=False,
    )
```

profile of v0, /device:TPU:0, one launch (start us, length us, event | category | flops | bytes accessed | tf_op | source)
XLA Modules:
  0.0 1045.0 jit_solution(12160134699010066056)
XLA Ops:
  8.0 43.3 %all-gather.1 = bf16[32,24,2]{1,2,0:T(2,128)(2,1)S(1)} all-gather(bf16[1,24,2]{1,2,0:T(2,128)(2,1)} %bitcast.194), channel_id=1, replica_groups=mesh['dp'=4,'seq'=8] {'dp','seq'}, dimensions={0}, use_global_device_ids=true | all-gather | bytes 3168 | tf_op jit(solution)/shard_map/all_gather | solution.py:90
  51.4 22.3 %all-gather.11.cloned.1.call-done = bf16[768,2304]{1,0:T(8,128)(2,1)} async-done(((bf16[24,2304]{1,0:T(8,128)(2,1)}), bf16[768,2304]{1,0:T(8,128)(2,1)}) %all-gather.11.cloned.1.call-update) | async-done | bytes 3538960 | tf_op jit(solution)/shard_map/all_gather | solution.py:89
  80.6 8.9 all-gather
  90.3 39.0 %all-reduce.10 = (bf16[3072]{0:T(1024)(128)(2,1)S(1)}, bf16[768]{0:T(1024)(128)(2,1)S(1)}, bf16[768]{0:T(1024)(128)(2,1)S(1)}) all-reduce(bf16[3072]{0:T(1024)(128)(2,1)S(1)} %dynamic-update-slice.1, bf16[768]{0:T(1024)(128)(2,1)S(1)} %dynamic-update-slice, ...), channel_id=1, replica_groups=mesh['dp'=4,'seq'=8] {'dp','seq'}, use_global_device_ids=true, to_apply=%add.1 | all-reduce | flops 4608 | bytes 18432
  129.3 39.5 %all-gather.2 = bf16[32,24,2]{1,2,0:T(2,128)(2,1)S(1)} all-gather(bf16[1,24,2]{1,2,0:T(2,128)(2,1)S(1)} %bitcast.195), channel_id=1, replica_groups=mesh['dp'=4,'seq'=8] {'dp','seq'}, dimensions={0}, use_global_device_ids=true | all-gather | bytes 3168 | tf_op jit(solution)/shard_map/all_gather | solution.py:93
  169.0 37.0 %all-gather.3 = bf16[32,24,2]{1,2,0:T(2,128)(2,1)S(1)} all-gather(bf16[1,24,2]{1,2,0:T(2,128)(2,1)S(1)} %bitcast.196), channel_id=1, replica_groups=mesh['dp'=4,'seq'=8] {'dp','seq'}, dimensions={0}, use_global_device_ids=true | all-gather | bytes 3168 | tf_op jit(solution)/shard_map/all_gather | solution.py:94
  215.8 44.6 %while.34 = (s32[]{:T(128)}, f32[12,256]{1,0:T(8,128)S(1)}, f32[12,256]{1,0:T(8,128)S(1)}, f32[12,256,64]{1,2,0:T(8,128)S(1)}, s32[256]{0:T(256)S(1)}, /*index=5...) while((s32[]{:T(128)}, f32[12,256]{1,0:T(8,128)S(1)}, ...), condition=%wide.region_3.4_spmd.clone, body=%wide.region_0.3_spmd.clone.sunk | while | flops 847612928 | bytes 100752568 | solution.py:45
  219.6 6.7 fusion.131
  226.3 7.7 fusion.132
  241.8 7.0 fusion.131
  248.8 7.8 fusion.132
  267.0 11.8 %multiply_convert_fusion = (bf16[256,3072]{1,0:T(8,128)(2,1)}, f32[256,3072]{1,0:T(8,128)}, f32[256,3072]{1,0:T(8,128)}) fusion(f32[3072]{0:T(1024)S(1)} %convert_element_type.115, bf16[768,3072]{1,0:T(8,128)(2,1)} %all-gather.19.cloned.1.call-done, f32[256,768]{1,0:T(8,128)S(1)} %get-tuple-element.661, f32[768]{0:T(1024)S(1)} %get-tuple-element.578, ...), kind=kOutput, calls=%fused_computation.72 | convolution fusion | flops 1260847104 | bytes 13389824 | tf_op jit(solution)/shard_map/dot_general | solution.py:183
  278.7 53.5 %all-gather.21.cloned.1.call-done = bf16[3072,768]{1,0:T(8,128)(2,1)} async-done(((bf16[96,768]{1,0:T(8,128)(2,1)}), bf16[3072,768]{1,0:T(8,128)(2,1)}) %all-gather.21.cloned.1.call-update) | async-done | bytes 4718608 | tf_op jit(solution)/shard_map/all_gather | solution.py:97
  349.2 75.6 %while.35 = (s32[]{:T(128)}, f32[256,12,64]{0,2,1:T(8,128)}, bf16[2,1024,768]{2,1,0:T(8,128)(2,1)}, bf16[2,1024,768]{2,1,0:T(8,128)(2,1)}, bf16[2,1024,768]{1,2,...) while((s32[]{:T(128)}, f32[256,12,64]{0,2,1:T(8,128)}, ...), condition=%wide.region_14.15_spmd.clone, body=%wide.region_13.14_spmd.clone.sunk | while | flops 2049069056 | bytes 163999568 | solution.py:267
  368.0 8.3 fusion.148
  405.7 8.4 fusion.148
  453.8 21.0 %reduce-scatter.14.cloned.1.call-done = bf16[256,768]{0,1:T(8,128)(2,1)} async-done(((bf16[2048,768]{0,1:T(8,128)(2,1)}), bf16[256,768]{0,1:T(8,128)(2,1)}) %reduce-scatter.14.cloned.1.call-update) | async-done | bytes 393232 | tf_op jit(solution)/shard_map/reduce_scatter | solution.py:284
  474.8 50.0 %reduce-scatter.12.cloned.1.call-done = bf16[256,768]{0,1:T(8,128)(2,1)} async-done(((bf16[2048,768]{0,1:T(8,128)(2,1)}), bf16[256,768]{0,1:T(8,128)(2,1)}) %reduce-scatter.12.cloned.1.call-update) | async-done | bytes 393232 | tf_op jit(solution)/shard_map/reduce_scatter | solution.py:278
  529.9 8.1 copy.95
  539.2 40.1 %all-reduce.9 = (f32[2,768]{1,0:T(2,128)S(1)}, f32[768]{0:T(1024)S(1)}, f32[2,768]{1,0:T(2,128)S(1)}, f32[2,768]{1,0:T(2,128)S(1)}, f32[3072]{0:T(1024)S(1)}, /*index=5*/f32[768]{0:T(1024)S(1)}) all-reduce(f32[2,768]{1,0:T(2,128)S(1)} %pad_maximum_fusion.4, ...), channel_id=5, replica_groups=mesh['dp'=4,'seq'=8] {'dp','seq'}, use_global_device_ids=true, to_apply=%region_20.21.clone | all-reduce | flops 9216 | bytes 73728
  587.0 42.7 %reduce-scatter.16.cloned.1.call-done = f32[24,768]{1,0:T(8,128)} async-done(((f32[768,768]{1,0:T(8,128)}), f32[24,768]{1,0:T(8,128)}) %reduce-scatter.16.cloned.1.call-update) | async-done | bytes 73744 | tf_op jit(solution)/shard_map/reduce_scatter | solution.py:306
  629.8 142.1 %reduce-scatter.20.cloned.1.call-done = f32[96,768]{1,0:T(8,128)} async-done(((f32[3072,768]{1,0:T(8,128)}), f32[96,768]{1,0:T(8,128)}) %reduce-scatter.20.cloned.1.call-update) | async-done | bytes 294928 | tf_op jit(solution)/shard_map/reduce_scatter | solution.py:312
  771.8 141.1 %reduce-scatter.18.cloned.1.call-done = f32[24,3072]{1,0:T(8,128)} async-done(((f32[768,3072]{1,0:T(8,128)}), f32[24,3072]{1,0:T(8,128)}) %reduce-scatter.18.cloned.1.call-update) | async-done | bytes 294928 | tf_op jit(solution)/shard_map/reduce_scatter | solution.py:310
  912.9 125.0 %reduce-scatter.22.cloned.1.call-done = f32[24,2304]{1,0:T(8,128)} async-done(((f32[768,2304]{1,0:T(8,128)}), f32[24,2304]{1,0:T(8,128)}) %reduce-scatter.22.cloned.1.call-update) | async-done | bytes 221200
  (277 shorter events, 158.1 us)
Async XLA Ops:
  7.2 66.5 %all-gather.11.cloned.1.call-start = ((), (), s32[]{:S(2)}) async-start(), calls=%async_computation.6 | async-start | bytes 3649536 | tf_op jit(solution)/shard_map/all_gather | solution.py:89
  7.9 198.4 %all-gather.13.cloned.1.call-start = ((), (), s32[]{:S(2)}) async-start(), calls=%async_computation.7 | async-start | bytes 3538944 | tf_op jit(solution)/shard_map/all_gather | solution.py:165
  77.0 13.0 %copy-start.46 = (bf16[96]{0:T(256)(128)(2,1)S(1)}, bf16[96]{0:T(256)(128)(2,1)}, u32[]{:S(2)}) copy-start(bf16[96]{0:T(256)(128)(2,1)} %param.27) | copy-start | bytes 580
  77.0 52.3 %copy-start.42 = (bf16[2,24]{1,0:T(2,128)(2,1)S(1)}, bf16[2,24]{1,0:T(2,128)(2,1)}, u32[]{:S(2)}) copy-start(bf16[2,24]{1,0:T(2,128)(2,1)} %param.24) | copy-start | bytes 292
  77.0 92.0 %copy-start.43 = (bf16[2,24]{1,0:T(2,128)(2,1)S(1)}, bf16[2,24]{1,0:T(2,128)(2,1)}, u32[]{:S(2)}) copy-start(bf16[2,24]{1,0:T(2,128)(2,1)} %param.25) | copy-start | bytes 292
  78.0 133.1 %all-gather.15.cloned.1.call-start = ((), (), s32[]{:S(2)}) async-start(), calls=%async_computation.8 | async-start | bytes 3538944 | tf_op jit(solution)/shard_map/all_gather | solution.py:166
  78.7 181.8 %all-gather.17.cloned.1.call-start = ((), (), s32[]{:S(2)}) async-start(), calls=%async_computation.9 | async-start | bytes 1216512 | tf_op jit(solution)/shard_map/all_gather | solution.py:91
  79.3 187.7 %all-gather.19.cloned.1.call-start = ((), (), s32[]{:S(2)}) async-start(), calls=%async_computation.10 | async-start | bytes 4866048 | tf_op jit(solution)/shard_map/all_gather | solution.py:95
  79.9 252.3 %all-gather.21.cloned.1.call-start = ((), (), s32[]{:S(2)}) async-start(), calls=%async_computation.11 | async-start | bytes 4866048 | tf_op jit(solution)/shard_map/all_gather | solution.py:97
  80.5 394.4 %reduce-scatter.14.cloned.1.call-start = ((), (), s32[]{:S(2)}) async-start(), calls=%async_computation.13 | async-start | bytes 3538944 | tf_op jit(solution)/shard_map/reduce_scatter | solution.py:284
  206.1 126.1 %copy-start.25 = (f32[768]{0:T(1024)}, f32[768]{0:T(1024)S(1)}, u32[]{:S(2)}) copy-start(f32[768]{0:T(1024)S(1)} %get-tuple-element.578) | copy-start | bytes 9220
  206.1 138.0 %copy-start.22 = (f32[768]{0:T(1024)}, f32[768]{0:T(1024)S(1)}, u32[]{:S(2)}) copy-start(f32[768]{0:T(1024)S(1)} %get-tuple-element.668) | copy-start | bytes 9220
  260.4 18.3 %copy-start.15 = (f32[12,256,64]{1,2,0:T(8,128)}, f32[12,256,64]{1,2,0:T(8,128)S(1)}, u32[]{:S(2)}) copy-start(f32[12,256,64]{1,2,0:T(8,128)S(1)} %get-tuple-element.328) | copy-start | bytes 2359300
  260.5 18.2 %copy-start.12 = (bf16[12,256,64]{1,2,0:T(8,128)(2,1)}, bf16[12,256,64]{1,2,0:T(8,128)(2,1)S(1)}, u32[]{:S(2)}) copy-start(bf16[12,256,64]{1,2,0:T(8,128)(2,1)S(1)} %fusion.50) | copy-start | bytes 1179652
  262.8 81.3 %copy-start.6 = (f32[256,768]{1,0:T(8,128)}, f32[256,768]{1,0:T(8,128)S(1)}, u32[]{:S(2)}) copy-start(f32[256,768]{1,0:T(8,128)S(1)} %get-tuple-element.661) | copy-start | bytes 2359300
  262.8 81.3 %copy-start.27 = (f32[256]{0:T(256)}, f32[256]{0:T(256)S(1)}, u32[]{:S(2)}) copy-start(f32[256]{0:T(256)S(1)} %broadcast_multiply_fusion.1) | copy-start | bytes 3076
  263.1 81.1 %copy-start.35 = (f32[256]{0:T(256)}, f32[256]{0:T(256)S(1)}, u32[]{:S(2)}) copy-start(f32[256]{0:T(256)S(1)} %fusion.57) | copy-start | bytes 3076
  429.6 95.2 %reduce-scatter.12.cloned.1.call-start = ((), (), s32[]{:S(2)}) async-start(), calls=%async_computation.12 | async-start | bytes 3538944 | tf_op jit(solution)/shard_map/reduce_scatter | solution.py:278
  434.5 195.2 %reduce-scatter.16.cloned.1.call-start = ((), (), s32[]{:S(2)}) async-start(), calls=%async_computation.14 | async-start | bytes 2433024 | tf_op jit(solution)/shard_map/reduce_scatter | solution.py:306
  437.7 334.1 %reduce-scatter.20.cloned.1.call-start = ((), (), s32[]{:S(2)}) async-start(), calls=%async_computation.16 | async-start | bytes 9732096 | tf_op jit(solution)/shard_map/reduce_scatter | solution.py:312
  444.8 468.2 %reduce-scatter.18.cloned.1.call-start = ((), (), s32[]{:S(2)}) async-start(), calls=%async_computation.15 | async-start | bytes 9732096 | tf_op jit(solution)/shard_map/reduce_scatter | solution.py:310
  452.5 72.3 %copy-start.17 = (bf16[256,768]{1,0:T(8,128)(2,1)S(1)}, bf16[256,768]{1,0:T(8,128)(2,1)}, u32[]{:S(2)}) copy-start(bf16[256,768]{1,0:T(8,128)(2,1)} %param.17) | copy-start | bytes 1179652
  452.5 585.3 %reduce-scatter.22.cloned.1.call-start = ((), (), s32[]{:S(2)}) async-start(), calls=%async_computation.17 | async-start | bytes 7299072
  538.0 45.0 %copy-start.21 = (bf16[256,768]{0,1:T(8,128)(2,1)S(1)}, bf16[256,768]{0,1:T(8,128)(2,1)}, u32[]{:S(2)}) copy-start(bf16[256,768]{0,1:T(8,128)(2,1)} %reduce-scatter.12.cloned.1.call-done) | copy-start | bytes 1179652
  (47 other events, 172.0 us)
Sparse Core Ops, SparseCore 0:
  10.9 62.7 all-gather.10
  78.1 31.2 all-gather.12
  111.9 32.8 all-gather.14
  147.6 53.9 all-gather.16
  204.3 62.6 all-gather.18
  269.7 62.4 all-gather.20
  429.7 45.0 reduce-scatter.13
  478.6 46.1 reduce-scatter.11
  530.7 99.0 reduce-scatter.15
  637.1 134.6 reduce-scatter.19
  778.3 134.5 reduce-scatter.17
  920.0 117.8 reduce-scatter.21
where the time goes:
time: 1050 us; the launch traced here: 1040 us
  waiting for transfers between devices  605 us (58%)
  blocking collectives  208 us (20%)
  matrix products  120 us (11%)
  local copies, waits for them, and re-layouts  70.8 us (7%)
  other arithmetic  25.6 us (2%)
  between operations  15.2 us (1%)
    reduce_scatter x1, waiting for transfers between devices, on_device(): lax.psum_scatter(grad_w_out, ('dp', 'seq'), scatter_dimension=0, tiled=True)  142 us
    reduce_scatter x1, waiting for transfers between devices, on_device(): lax.psum_scatter(grad_w_in, ('dp', 'seq'), scatter_dimension=0, tiled=True)  141 us
    unnamed x13, waiting for transfers between devices  128 us
    unnamed x2, blocking collectives  79.2 us
    all_gather x1, waiting for transfers between devices, on_device(): lax.all_gather(w_out, ('dp', 'seq'), axis=0, tiled=True)  53.5 us
    reduce_scatter x1, waiting for transfers between devices, on_device(): lax.psum_scatter(key_terms.reshape(length, width).astype(jnp.bfloat16), '...  50 us
    all_gather x1, blocking collectives, on_device(): lax.all_gather(bias_qv, ('dp', 'seq'), axis=1, tiled=True)  43.3 us
    reduce_scatter x1, waiting for transfers between devices, on_device(): lax.psum_scatter(grad_w_o, ('dp', 'seq'), scatter_dimension=0, tiled=True)  42.7 us
  transfers between devices with their start and end apart: 12, of which 9 were waited for; matrix products, arithmetic and copies ran while one was open for 10% of the time, Pallas kernels for 0%

commit v1 on v0

--- a/solution.py
+++ b/solution.py
@@ -3,6 +3,8 @@
 import jax
 import jax.numpy as jnp
 from jax import lax
+from jax.experimental import pallas as pl
+from jax.experimental.pallas import tpu as pltpu
 from jax.sharding import PartitionSpec as P
 
 HEADS = 12
@@ -12,6 +14,725 @@
 
 EPSILON = 1e-12
 NEG_LARGE = -1e30
+
+F32 = jnp.float32
+BF16 = jnp.bfloat16
+LOG2E = 1.4426950408889634
+NT = (((1,), (1,)), ((), ()))
+TN = (((0,), (0,)), ((), ()))
+NN = (((1,), (0,)), ((), ()))
+
+
+def dot(left, right, dims=NN):
+    return lax.dot_general(left, right, dims, preferred_element_type=F32)
+
+
+def sds(shape, dtype):
+    return jax.ShapeDtypeStruct(shape, dtype)
+
+
+def call(kernel, args, outs, scratch=(), smem_in=(0,), smem_out=(), flops=0, name=None):
+    space = lambda inside: pl.BlockSpec(memory_space=pltpu.SMEM if inside else pltpu.VMEM)
+    nbytes = sum(math.prod(a.shape) * a.dtype.itemsize for a in tuple(args) + tuple(outs))
+    return pl.pallas_call(
+        kernel,
+        out_shape=tuple(outs),
+        in_specs=[space(i in smem_in) for i in range(len(args))],
+        out_specs=tuple(space(i in smem_out) for i in range(len(outs))),
+        scratch_shapes=list(scratch),
+        compiler_params=pltpu.CompilerParams(vmem_limit_bytes=60 * 1024 * 1024),
+        cost_estimate=pl.CostEstimate(
+            flops=int(flops), transcendentals=0, bytes_accessed=int(nbytes)
+        ),
+        name=name,
+    )(*args)
+
+
+def place(pos):
+    d = pos[0]
+    return d >> 3, (d >> 1) & 3, d & 1
+
+
+def row_of(start, size=8):
+    return pl.multiple_of(start, size)
+
+
+def pack_kernel(pos, wqkv, win, wout, smalls, p0, p1, p2, p3, wx):
+    z, p, c = place(pos)
+    rows = lax.broadcasted_iota(jnp.int32, (96, 96), 0)
+    cols = lax.broadcasted_iota(jnp.int32, (96, 96), 1)
+    eye = (rows == cols).astype(BF16)
+    side = dot(eye, smalls[...], NT).astype(BF16)
+    wx[...] = jnp.concatenate([wout[...], side, jnp.zeros((96, 112), BF16)], axis=1)
+    small = jnp.concatenate([side[:24], jnp.zeros((24, 48), BF16)], axis=1)
+
+    def piece(chip):
+        parts = [wqkv[:, 768 * i + 192 * chip : 768 * i + 192 * chip + 192] for i in range(3)]
+        parts.append(small)
+        parts += [win[:, 768 * i + 192 * chip : 768 * i + 192 * chip + 192] for i in range(4)]
+        return jnp.concatenate(parts, axis=1)
+
+    for own in range(4):
+
+        @pl.when(p == own)
+        def _(own=own):
+            for k, out in enumerate((p0, p1, p2, p3)):
+                out[...] = piece(own ^ k)
+
+
+def interleave(pos, mine, other, lanes, out, order):
+    z, p, c = place(pos)
+
+    def run(first, second):
+        for j in range(4):
+            for k in range(4):
+                at = (j, slice(24 * k, 24 * k + 24), lanes) if order == "jk" else (
+                    k, slice(24 * j, 24 * j + 24), lanes)
+                block = jnp.concatenate([first[at], second[at]], axis=0)
+                start = ((z ^ j) * 4 + (p ^ k)) * 48
+                out[pl.ds(row_of(start, 16), 48), :] = block
+
+    @pl.when(c == 0)
+    def _():
+        run(mine, other)
+
+    @pl.when(c == 1)
+    def _():
+        run(other, mine)
+
+
+def qkv_kernel(pos, am, ao, x0, x1, x2, x3, q, kv, wq, vecs, nb, bias):
+    z, p, c = place(pos)
+    interleave(pos, am, ao, slice(None), wq, "jk")
+    flipped = jnp.transpose(wq[:, 512:640].astype(F32))
+    vecs[...] = flipped[64:80]
+    for own in range(4):
+
+        @pl.when(p == own)
+        def _(own=own):
+            at = slice(192 * own, 192 * own + 192)
+            bias[0:1, :] = jnp.concatenate(
+                [vecs[0:1, at], jnp.zeros((1, 192), F32), vecs[1:2, at], jnp.zeros((1, 64), F32)],
+                axis=1,
+            )
+
+    lane = lax.broadcasted_iota(jnp.int32, (1, 768), 1)
+    mask = (lane >= 192 * z) & (lane < 192 * z + 192) & (lane % 24 == 0)
+    second = jnp.sum(jnp.where(mask, vecs[8:9, :], 0.0))
+    nb[0] = 8 - second.astype(jnp.int32)
+    for k, x in enumerate((x0, x1, x2, x3)):
+        got = (dot(x[...], wq[...]) + bias[0:1, :]).astype(BF16)
+        q[k] = got[:, :192]
+        kv[k] = got[:, 192:576]
+
+
+def weights_kernel(pos, mm, mo, wi, wx, bin_):
+    z, p, c = place(pos)
+    interleave(pos, mm, mo, slice(0, 768), wi, "jk")
+    for j in range(4):
+        base = (z ^ j) * 192
+        wx[pl.ds(row_of(base + c * 96, 32), 96), :] = mm[j, :, 768:1664]
+        wx[pl.ds(row_of(base + (1 - c) * 96, 32), 96), :] = mo[j, :, 768:1664]
+    flipped = jnp.transpose(wx[:, 768:896].astype(F32))
+    bin_[...] = flipped[8:16]
+
+
+def wo_kernel(pos, om, oo, wo):
+    interleave(pos, om, oo, slice(None), wo, "kj")
+
+
+def absolute_kv(pos, mine, other, kv):
+    z, p, c = place(pos)
+    for k in range(4):
+        first = 2 * (p ^ k)
+        kv[first + c] = mine[k]
+        kv[first + 1 - c] = other[k]
+
+
+def key_range(pos, nb, k):
+    z, p, c = place(pos)
+    block = 2 * (p ^ k) + c
+    return jnp.where(block < nb[0], 0, nb[0]), block + 1
+
+
+def attention_kernel(pos, nb, q, mine, other, a0, a1, a2, a3, ot, lse, kv):
+    scale = 0.125 * LOG2E
+    absolute_kv(pos, mine, other, kv)
+    for k, out in enumerate((a0, a1, a2, a3)):
+        low, high = key_range(pos, nb, k)
+        heads = [q[k, :, 64 * h : 64 * h + 64] for h in range(3)]
+
+        def step(kb, state):
+            new = []
+            for h in range(3):
+                top, total, acc = state[h]
+                keys = kv[kb, :, 64 * h : 64 * h + 64]
+                values = kv[kb, :, 192 + 64 * h : 256 + 64 * h]
+                scores = dot(keys, heads[h], NT)
+                next_top = jnp.maximum(top, jnp.max(scores, axis=0, keepdims=True))
+                weights = jnp.exp2((scores - next_top) * scale)
+                factor = jnp.exp2((top - next_top) * scale)
+                total = total * factor + jnp.sum(weights, axis=0, keepdims=True)
+                acc = acc * factor + dot(values, weights.astype(BF16), TN)
+                new.append((next_top, total, acc))
+            return tuple(new)
+
+        start = tuple(
+            (jnp.full((1, BLK), NEG_LARGE, F32), jnp.zeros((1, BLK), F32), jnp.zeros((HDIM, BLK), F32))
+            for _ in range(3)
+        )
+        state = lax.fori_loop(low, high, step, start)
+        done = []
+        for h in range(3):
+            top, total, acc = state[h]
+            mixed = acc / total
+            ot[k, 64 * h : 64 * h + 64, :] = mixed
+            lse[k, h : h + 1, :] = top * scale + jnp.log(total) * LOG2E
+            done.append(mixed)
+        out[...] = jnp.transpose(jnp.concatenate(done, axis=0)).astype(BF16)
+
+
+def attention_back_kernel(
+    pos, nb, q, mine, other, g0, g1, g2, g3, ot, lse, dq, dmine, dother, kv, dkv
+):
+    z, p, c = place(pos)
+    scale = 0.125 * LOG2E
+    absolute_kv(pos, mine, other, kv)
+    dkv[...] = jnp.zeros(dkv.shape, F32)
+    for k, grad in enumerate((g0, g1, g2, g3)):
+        low, high = key_range(pos, nb, k)
+        heads = [q[k, :, 64 * h : 64 * h + 64] for h in range(3)]
+        grads = [grad[:, 64 * h : 64 * h + 64] for h in range(3)]
+        flipped = jnp.transpose(grad[...].astype(F32))
+        product = flipped * ot[k]
+        deltas = [
+            jnp.sum(product[64 * h : 64 * h + 64], axis=0, keepdims=True) for h in range(3)
+        ]
+        logs = [lse[k, h : h + 1, :] for h in range(3)]
+
+        def step(kb, state):
+            new = []
+            for h in range(3):
+                keys = kv[kb, :, 64 * h : 64 * h + 64]
+                values = kv[kb, :, 192 + 64 * h : 256 + 64 * h]
+                probs = jnp.exp2(dot(keys, heads[h], NT) * scale - logs[h])
+                dprobs = dot(values, grads[h], NT)
+                low_scores = (probs * (dprobs - deltas[h]) * 0.125).astype(BF16)
+                dkv[h, kb] += dot(low_scores, heads[h])
+                dkv[3 + h, kb] += dot(probs.astype(BF16), grads[h])
+                new.append(state[h] + dot(keys, low_scores, TN))
+            return tuple(new)
+
+        state = lax.fori_loop(
+            low, high, step, tuple(jnp.zeros((HDIM, BLK), F32) for _ in range(3))
+        )
+        dq[k] = jnp.transpose(jnp.concatenate(state, axis=0))
+    for k in range(4):
+        first = 2 * (p ^ k)
+        dmine[k] = jnp.concatenate([dkv[i, first + c] for i in range(6)], axis=1)
+        dother[k] = jnp.concatenate([dkv[i, first + 1 - c] for i in range(6)], axis=1).astype(BF16)
+
+
+def norm_kernel(pos, tokens, a0, a1, a2, a3, wo, vecs, low, xhat, rstd):
+    z, p, c = place(pos)
+    resid = tokens[...].astype(F32) + vecs[2:3, :]
+    for k, a in enumerate((a0, a1, a2, a3)):
+        start = (p ^ k) * 192
+        resid += dot(a[...], wo[pl.ds(row_of(start, 64), 192), :])
+    center = resid - jnp.mean(resid, axis=-1, keepdims=True)
+    scale = lax.rsqrt(jnp.mean(center * center, axis=-1, keepdims=True) + EPSILON)
+    hat = center * scale
+    xhat[...] = hat
+    rstd[...] = scale
+    low[...] = (hat * vecs[3:4, :] + vecs[5:6, :]).astype(BF16)
+
+
+def norm_grad(grad, gain, hat, scale):
+    e = grad * gain
+    mean_e = jnp.mean(e, axis=-1, keepdims=True)
+    mean_x = jnp.mean(e * hat, axis=-1, keepdims=True)
+    return scale * (e - mean_e - hat * mean_x)
+
+
+def total(values):
+    return jnp.sum(values, axis=0, keepdims=True)
+
+
+def norm_two_kernel(vecs, xhat, own, r1, r2, r3, cot, block_out, low, grad_two, sums):
+    acc = [jnp.zeros((1, 768), F32) for _ in range(3)]
+    for i in range(8):
+        at = slice(32 * i, 32 * i + 32)
+        hidden = xhat[at, :] * vecs[3:4, :] + vecs[5:6, :]
+        resid = hidden + own[at, :] + vecs[7:8, :]
+        for r in (r1, r2, r3):
+            resid += r[at, :].astype(F32)
+        center = resid - jnp.mean(resid, axis=-1, keepdims=True)
+        scale = lax.rsqrt(jnp.mean(center * center, axis=-1, keepdims=True) + EPSILON)
+        hat = center * scale
+        block_out[at, :] = (hat * vecs[4:5, :] + vecs[6:7, :]).astype(BF16)
+        grad = cot[at, :].astype(F32)
+        back = norm_grad(grad, vecs[4:5, :], hat, scale)
+        grad_two[at, :] = back
+        low[at, :] = back.astype(BF16)
+        acc = [acc[0] + total(grad * hat), acc[1] + total(grad), acc[2] + total(back)]
+    sums[...] = jnp.concatenate(acc + [jnp.zeros((5, 768), F32)], axis=0)
+
+
+def norm_one_kernel(
+    pos, own, r1, r2, r3, grad_two, xhat, rstd, vecs, wo, o0, o1, o2, o3, low, grad_one, sums
+):
+    z, p, c = place(pos)
+    acc = [jnp.zeros((1, 768), F32) for _ in range(3)]
+    for i in range(8):
+        at = slice(32 * i, 32 * i + 32)
+        grad = own[at, :] + grad_two[at, :]
+        for r in (r1, r2, r3):
+            grad += r[at, :].astype(F32)
+        hat = xhat[at, :]
+        back = norm_grad(grad, vecs[3:4, :], hat, rstd[at, :])
+        grad_one[at, :] = back
+        low[at, :] = back.astype(BF16)
+        acc = [acc[0] + total(grad * hat), acc[1] + total(grad), acc[2] + total(back)]
+    sums[...] = jnp.concatenate(acc + [jnp.zeros((5, 768), F32)], axis=0)
+    for k, out in enumerate((o0, o1, o2, o3)):
+        start = (p ^ k) * 192
+        out[...] = dot(low[...], wo[pl.ds(row_of(start, 64), 192), :], NT).astype(BF16)
+
+
+def ff_kernel(count):
+    def kernel(*refs):
+        hs = refs[:count]
+        wi, wx, bias = refs[count : count + 3]
+        outs = refs[count + 3 :]
+        for i, h in enumerate(hs):
+            part, act, slope = outs[3 * i : 3 * i + 3]
+            acc = jnp.zeros((256, 768), F32)
+            for f in range(3):
+                at = slice(256 * f, 256 * f + 256)
+                u = dot(h[...], wi[:, at]) + bias[1:2, at]
+                cdf = 0.5 * (1.0 + lax.erf(u * 0.7071067811865476))
+                low = (u * cdf).astype(BF16)
+                act[:, at] = low
+                slope[:, at] = cdf + u * jnp.exp2(u * u * (-0.5 * LOG2E)) * 0.3989422804014327
+                acc += dot(low, wx[at, :768])
+            part[...] = acc.astype(part.dtype)
+
+    return kernel
+
+
+def ff_back_kernel(count):
+    def kernel(*refs):
+        gs = refs[:count]
+        slopes = refs[count : 2 * count]
+        wi, wx = refs[2 * count : 2 * count + 2]
+        sums = refs[2 * count + 2]
+        outs = refs[2 * count + 3 :]
+        for f in range(3):
+            at = slice(256 * f, 256 * f + 256)
+            acc = jnp.zeros((1, 256), F32)
+            for i in range(count):
+                pre = dot(gs[i][...], wx[at, :768], NT) * slopes[i][:, at]
+                outs[2 * i + 1][:, at] = pre.astype(BF16)
+                acc += total(pre)
+            sums[:, at] = jnp.broadcast_to(acc, (8, 256))
+        for i in range(count):
+            back = dot(outs[2 * i + 1][...], wi[...], NT)
+            outs[2 * i][...] = back.astype(outs[2 * i].dtype)
+
+    return kernel
+
+
+def column_of(row):
+    n = row.shape[1]
+    first = lax.broadcasted_iota(jnp.int32, (128, n), 0) == 0
+    return jnp.transpose(jnp.where(first, jnp.broadcast_to(row, (128, n)), 0.0))
+
+
+def ff_grad_kernel(*refs):
+    pos = refs[0]
+    hs, pres, acts, gs = refs[1:5], refs[5:9], refs[9:13], refs[13:17]
+    sum_a, sum_b = refs[17:19]
+    keep, send, gi, go = refs[19:]
+    z, p, c = place(pos)
+    gi[...] = sum(dot(hs[k][...], pres[k][...], TN) for k in range(4))
+    go[:, :768] = sum(dot(acts[k][...], gs[k][...], TN) for k in range(4))
+    go[:, 768:] = column_of(sum_a[0:1, :] + sum_b[0:1, :])
+    for j in range(4):
+        for out, core in ((keep, c), (send, 1 - c)):
+            for k in range(4):
+                start = ((z ^ j) * 4 + (p ^ k)) * 48 + core * 24
+                out[j, 24 * k : 24 * k + 24, 0:768] = gi[pl.ds(row_of(start), 24), :].astype(BF16)
+            start = (z ^ j) * 192 + core * 96
+            out[j, :, 768:1664] = go[pl.ds(row_of(start), 96), :].astype(BF16)
+
+
+def wo_grad_kernel(pos, a0, a1, a2, a3, low, sum_one, sum_two, keep, send, acc):
+    z, p, c = place(pos)
+    for k, a in enumerate((a0, a1, a2, a3)):
+        start = (p ^ k) * 192
+        acc[pl.ds(row_of(start), 192), 0:768] = dot(a[...], low[...], TN)
+    rows = jnp.concatenate(
+        [
+            sum_one[2:3, :],
+            sum_one[0:1, :],
+            sum_two[0:1, :],
+            sum_one[1:2, :],
+            sum_two[1:2, :],
+            sum_two[2:3, :],
+            jnp.zeros((122, 768), F32),
+        ],
+        axis=0,
+    )
+    acc[:, 768:896] = jnp.transpose(rows)
+    for k in range(4):
+        for j in range(4):
+            for out, core in ((keep, c), (send, 1 - c)):
+                start = ((z ^ j) * 4 + (p ^ k)) * 48 + core * 24
+                out[k, 24 * j : 24 * j + 24, :] = acc[pl.ds(row_of(start), 24), :].astype(BF16)
+
+
+def qkv_back_kernel(dq, dmine, dother, wq, i0, i1, i2, i3, low, sums):
+    bias_q = jnp.zeros((1, 192), F32)
+    bias_v = jnp.zeros((1, 192), F32)
+    for k, out in enumerate((i0, i1, i2, i3)):
+        grad_q = dq[k]
+        grad_kv = dmine[k] + dother[k].astype(F32)
+        bias_q += total(grad_q)
+        bias_v += total(grad_kv[:, 192:])
+        whole = jnp.concatenate([grad_q, grad_kv, jnp.zeros((256, 64), F32)], axis=1).astype(BF16)
+        low[k] = whole
+        out[...] = dot(whole, wq[...], NT).astype(out.dtype)
+    sums[...] = jnp.concatenate(
+        [
+            jnp.concatenate([bias_q, jnp.zeros((1, 64), F32)], axis=1),
+            jnp.concatenate([bias_v, jnp.zeros((1, 64), F32)], axis=1),
+            jnp.zeros((6, 256), F32),
+        ],
+        axis=0,
+    )
+
+
+def qkv_grad_kernel(pos, x0, x1, x2, x3, low, sums, keep, send, acc):
+    z, p, c = place(pos)
+    acc[...] = sum(dot(x[...], low[k], TN) for k, x in enumerate((x0, x1, x2, x3)))
+    rows = jnp.concatenate(
+        [jnp.zeros((64, 256), F32), sums[...], jnp.zeros((56, 256), F32)], axis=0
+    )
+    extra = jnp.transpose(rows)[:192]
+    for i in range(4):
+        acc[192 * i : 192 * i + 192, 512:640] += extra
+    for j in range(4):
+        for k in range(4):
+            for out, core in ((keep, c), (send, 1 - c)):
+                start = ((z ^ j) * 4 + (p ^ k)) * 48 + core * 24
+                out[j, 24 * k : 24 * k + 24, :] = acc[pl.ds(row_of(start), 24), :].astype(BF16)
+
+
+def turned(block):
+    n = block.shape[0]
+    return jnp.transpose(jnp.concatenate([block, jnp.zeros((128 - n, 128), F32)], axis=0))
+
+
+def finish_kernel(
+    pos, tq, tm, f1, f2, f3, uo, gqkv, gbqv, gwo, gbo, gain, shift, gwin, gbin, gwout, gbout
+):
+    z, p, c = place(pos)
+    gwout[...] = tm[:, 768:1536]
+    gbin[...] = turned(tm[:, 1536:1664])[0:1, 0:96]
+    gwo[...] = uo[:, 0:768]
+    side = turned(uo[:, 768:896])
+    gbo[...] = side[0:1, 0:24]
+    gain[...] = side[1:3, 0:24]
+    shift[...] = side[3:5, 0:24]
+    gbout[...] = side[5:6, 0:24]
+    for own in range(4):
+
+        @pl.when(p == own)
+        def _(own=own):
+            biases = jnp.zeros((24, 128), F32)
+            for k in range(4):
+                chip = own ^ k
+                if k == 0:
+                    qkv, win = tq[0:24, :], tm[0:24, 0:768]
+                else:
+                    got = (f1, f2, f3)[k - 1][...].astype(F32)
+                    qkv, win = got[:, 0:640], got[:, 640:1408]
+                for i in range(3):
+                    gqkv[:, 768 * i + 192 * chip : 768 * i + 192 * chip + 192] = qkv[
+                        :, 192 * i : 192 * i + 192
+                    ]
+                for i in range(4):
+                    gwin[:, 768 * i + 192 * chip : 768 * i + 192 * chip + 192] = win[
+                        :, 192 * i : 192 * i + 192
+                    ]
+                biases += jnp.where(z == chip, qkv[:, 512:640], 0.0)
+            gbqv[...] = turned(biases)[64:66, 0:24]
+
+
+def chip_swap(value, k):
+    return lax.ppermute(value, "seq", [(s, s ^ (2 * k)) for s in range(8)])
+
+
+def core_swap(value):
+    return lax.ppermute(value, "seq", [(s, s ^ 1) for s in range(8)])
+
+
+def z_swap(value, j):
+    return lax.ppermute(value, "dp", [(s, s ^ j) for s in range(4)])
+
+
+def low_add(*terms):
+    return sum(t.astype(F32) for t in terms)
+
+
+def fast_device(
+    tokens,
+    doc_ids,
+    cotangent,
+    w_qkv,
+    bias_qv,
+    w_o,
+    bias_o,
+    ln_gain,
+    ln_bias,
+    w_in,
+    bias_in,
+    w_out,
+    bias_out,
+):
+    pos = lax.axis_index(("dp", "seq")).astype(jnp.int32).reshape(1)
+    others = (1, 2, 3)
+    narrow = jnp.concatenate(
+        [
+            bias_qv,
+            bias_o[None],
+            ln_gain,
+            ln_bias,
+            bias_out[None],
+            doc_ids[None, :24].astype(BF16),
+        ],
+        axis=0,
+    )
+    smalls = jnp.concatenate(
+        [
+            jnp.pad(narrow, ((0, 0), (0, 72))),
+            bias_in[None],
+            jnp.zeros((6, 96), BF16),
+        ],
+        axis=0,
+    )
+    p0, p1, p2, p3, wx_own = call(
+        pack_kernel,
+        (pos, w_qkv, w_in, w_out, smalls),
+        [sds((24, 1408), BF16)] * 4 + [sds((96, 896), BF16)],
+        name="pack",
+    )
+    got = [p0] + [chip_swap(v, k) for v, k in zip((p1, p2, p3), others)]
+    xs = [tokens] + [chip_swap(tokens, k) for k in others]
+    first = jnp.concatenate([g[:, :640] for g in got], axis=0)
+    first_all = jnp.stack([first] + [z_swap(first, j) for j in others])
+    first_other = core_swap(first_all)
+    wo_z = jnp.concatenate([w_o] + [z_swap(w_o, j) for j in others], axis=0)
+    bulk = jnp.concatenate(
+        [jnp.concatenate([g[:, 640:] for g in got], axis=0), wx_own], axis=1
+    )
+    bulk_all = jnp.stack([bulk] + [z_swap(bulk, j) for j in others])
+    bulk_other = core_swap(bulk_all)
+    wo_all = jnp.stack([wo_z] + [chip_swap(wo_z, k) for k in others])
+    wo_other = core_swap(wo_all)
+
+    q, kv, wq, vecs, nb = call(
+        qkv_kernel,
+        (pos, first_all, first_other, *xs),
+        [
+            sds((4, 256, 192), BF16),
+            sds((4, 256, 384), BF16),
+            sds((768, 640), BF16),
+            sds((16, 768), F32),
+            sds((1,), jnp.int32),
+        ],
+        scratch=[pltpu.VMEM((8, 640), F32)],
+        smem_out=(4,),
+        flops=2 * 1024 * 768 * 640,
+        name="qkv",
+    )
+    kv_other = core_swap(kv)
+    *attended, ot, lse = call(
+        attention_kernel,
+        (pos, nb, q, kv, kv_other),
+        [sds((256, 192), BF16)] * 4 + [sds((4, 192, 256), F32), sds((4, 8, 256), F32)],
+        scratch=[pltpu.VMEM((8, 256, 384), BF16)],
+        smem_in=(0, 1),
+        flops=6e9,
+        name="attention",
+    )
+    pieces = [attended[0]] + [chip_swap(attended[k], k) for k in others]
+    (wo,) = call(wo_kernel, (pos, wo_all, wo_other), [sds((768, 768), BF16)], name="join_wo")
+    hidden, xhat, rstd = call(
+        norm_kernel,
+        (pos, tokens, *pieces, wo, vecs),
+        [sds((256, 768), BF16), sds((256, 768), F32), sds((256, 1), F32)],
+        flops=2 * 256 * 768 * 768,
+        name="norm_one",
+    )
+    hs = [hidden] + [chip_swap(hidden, k) for k in others]
+    wi, wx, bin_ = call(
+        weights_kernel,
+        (pos, bulk_all, bulk_other),
+        [sds((768, 768), BF16), sds((768, 896), BF16), sds((8, 768), F32)],
+        name="join_ff",
+    )
+
+    def ff(blocks, dtype):
+        per = [sds((256, 768), dtype), sds((256, 768), BF16), sds((256, 768), F32)]
+        out = call(
+            ff_kernel(len(blocks)),
+            (*blocks, wi, wx, bin_),
+            per * len(blocks),
+            smem_in=(),
+            flops=len(blocks) * 4 * 256 * 768 * 768,
+            name="ff",
+        )
+        return [out[3 * i : 3 * i + 3] for i in range(len(blocks))]
+
+    made = ff(hs[:1], F32) + ff(hs[1:], BF16)
+    parts = [made[0][0]] + [chip_swap(made[k][0], k) for k in others]
+    block_out, grad_two_low, grad_two, sums_two = call(
+        norm_two_kernel,
+        (vecs, xhat, *parts, cotangent),
+        [sds((256, 768), BF16), sds((256, 768), BF16), sds((256, 768), F32), sds((8, 768), F32)],
+        smem_in=(),
+        flops=1e7,
+        name="norm_two",
+    )
+    gs = [grad_two_low] + [chip_swap(grad_two_low, k) for k in others]
+
+    def ff_back(blocks, slopes, dtype):
+        n = len(blocks)
+        out = call(
+            ff_back_kernel(n),
+            (*blocks, *slopes, wi, wx),
+            [sds((8, 768), F32)] + [sds((256, 768), dtype), sds((256, 768), BF16)] * n,
+            smem_in=(),
+            flops=n * 4 * 256 * 768 * 768,
+            name="ff_back",
+        )
+        return out[0], [out[1 + 2 * i : 3 + 2 * i] for i in range(n)]
+
+    sum_a, back_a = ff_back(gs[:1], [made[0][2]], F32)
+    sum_b, back_b = ff_back(gs[1:], [m[2] for m in made[1:]], BF16)
+    backs = back_a + back_b
+    grad_parts = [backs[0][0]] + [chip_swap(backs[k][0], k) for k in others]
+    ff_keep, ff_send = call(
+        ff_grad_kernel,
+        (pos, *hs, *[b[1] for b in backs], *[m[1] for m in made], *gs, sum_a, sum_b),
+        [sds((4, 96, 1664), BF16)] * 2,
+        scratch=[pltpu.VMEM((768, 768), F32), pltpu.VMEM((768, 896), F32)],
+        flops=16 * 256 * 768 * 768,
+        name="ff_grad",
+    )
+    ff_got = core_swap(ff_send)
+    ff_sum = [low_add(ff_keep[j], ff_got[j]) for j in range(4)]
+    ff_z = [z_swap(ff_sum[j].astype(BF16), j) for j in others]
+    tm = low_add(ff_sum[0], *ff_z)
+
+    *grad_att, low_one, grad_one, sums_one = call(
+        norm_one_kernel,
+        (pos, *grad_parts, grad_two, xhat, rstd, vecs, wo),
+        [sds((256, 192), BF16)] * 4
+        + [sds((256, 768), BF16), sds((256, 768), F32), sds((8, 768), F32)],
+        flops=2 * 256 * 768 * 768,
+        name="norm_one_back",
+    )
+    grad_pieces = [grad_att[0]] + [chip_swap(grad_att[k], k) for k in others]
+    wo_keep, wo_send = call(
+        wo_grad_kernel,
+        (pos, *pieces, low_one, sums_one, sums_two),
+        [sds((4, 96, 896), BF16)] * 2,
+        scratch=[pltpu.VMEM((768, 896), F32)],
+        flops=2 * 256 * 768 * 768,
+        name="wo_grad",
+    )
+    wo_got = core_swap(wo_send)
+    wo_sum = [low_add(wo_keep[k], wo_got[k]) for k in range(4)]
+    to = low_add(wo_sum[0], *[chip_swap(wo_sum[k].astype(BF16), k) for k in others])
+    uo = low_add(
+        to[:24], *[z_swap(to[24 * j : 24 * j + 24].astype(BF16), j) for j in others]
+    )
+
+    dq, dmine, dother = call(
+        attention_back_kernel,
+        (pos, nb, q, kv, kv_other, *grad_pieces, ot, lse),
+        [sds((4, 256, 192), F32), sds((4, 256, 384), F32), sds((4, 256, 384), BF16)],
+        scratch=[pltpu.VMEM((8, 256, 384), BF16), pltpu.VMEM((6, 8, 256, 64), F32)],
+        smem_in=(0, 1),
+        flops=15e9,
+        name="attention_back",
+    )
+    dgot = core_swap(dother)
+    *in_parts, low, sums_qv = call(
+        qkv_back_kernel,
+        (dq, dmine, dgot, wq),
+        [sds((256, 768), F32)]
+        + [sds((256, 768), BF16)] * 3
+        + [sds((4, 256, 640), BF16), sds((8, 256), F32)],
+        smem_in=(),
+        flops=2 * 1024 * 768 * 640,
+        name="qkv_back",
+    )
+    in_got = [chip_swap(in_parts[k], k) for k in others]
+    input_grad = low_add(in_parts[0], grad_one, *in_got)
+    q_keep, q_send = call(
+        qkv_grad_kernel,
+        (pos, *xs, low, sums_qv),
+        [sds((4, 96, 640), BF16)] * 2,
+        scratch=[pltpu.VMEM((768, 640), F32)],
+        flops=2 * 1024 * 768 * 640,
+        name="qkv_grad",
+    )
+    q_got = core_swap(q_send)
+    q_sum = [low_add(q_keep[j], q_got[j]) for j in range(4)]
+    tq = low_add(q_sum[0], *[z_swap(q_sum[j].astype(BF16), j) for j in others])
+    final = [
+        chip_swap(
+            jnp.concatenate(
+                [tq[24 * k : 24 * k + 24], tm[24 * k : 24 * k + 24, :768]], axis=1
+            ).astype(BF16),
+            k,
+        )
+        for k in others
+    ]
+    gqkv, gbqv, gwo, gbo, gain, shift, gwin, gbin, gwout, gbout = call(
+        finish_kernel,
+        (pos, tq, tm, *final, uo),
+        [
+            sds((24, 2304), F32),
+            sds((2, 24), F32),
+            sds((24, 768), F32),
+            sds((1, 24), F32),
+            sds((2, 24), F32),
+            sds((2, 24), F32),
+            sds((24, 3072), F32),
+            sds((1, 96), F32),
+            sds((96, 768), F32),
+            sds((1, 24), F32),
+        ],
+        name="finish",
+    )
+    return (
+        block_out,
+        input_grad,
+        gqkv,
+        gbqv,
+        gwo,
+        gbo.reshape(24),
+        gain,
+        shift,
+        gwin,
+        gbin.reshape(96),
+        gwout,
+        gbout.reshape(24),
+    )
 
 
 def layer_norm(resid, gain, shift):
@@ -344,8 +1065,10 @@
         P(("dp", "seq"), None),
         P(("dp", "seq")),
     )
+    sizes = dict(mesh.shape)
+    fast = sizes["dp"] == 4 and sizes["seq"] == 8
     return jax.shard_map(
-        on_device,
+        fast_device if fast else on_device,
         mesh=mesh,
         in_specs=placed,
         out_specs=(

time: 1050 us -> 306 us (0.29)
  waiting for transfers between devices: 605 us -> 106 us
  blocking collectives: 208 us -> 0 us
  matrix products: 120 us -> 0 us
  Pallas kernels: 0 us -> 94 us
  starting transfers between devices: 0.73 us -> 82.3 us
  local copies, waits for them, and re-layouts: 70.8 us -> 10.5 us
  other arithmetic: 25.6 us -> 11.1 us
  between operations: 15.2 us -> 1.11 us
    reduce_scatter x5 -> x0, waiting for transfers between devices: 397 us -> none  [the longest x1 142 us: on_device(): lax.psum_scatter(grad_w_out, ('dp', 'seq'), scatter_dimension=0, tiled=True)]
    all_gather x4 -> x0, blocking collectives: 129 us -> none  [the longest x1 43.3 us: on_device(): lax.all_gather(bias_qv, ('dp', 'seq'), axis=1, tiled=True)]
    unnamed x13 -> x0, waiting for transfers between devices: 128 us -> none
    dot_general x26 -> x0, matrix products: 120 us -> none  [the longest x2 16.7 us: score_grads(): jnp.einsum('hqk,qhd->khd', probs.astype(jnp.bfloat16), grad_heads, prefer...]
    ppermute x0 -> x62, waiting for transfers between devices: none -> 106 us  [the longest x36 75.5 us: chip_swap(): return lax.ppermute(value, 'seq', [(s, s ^ 2 * k) for s in range(8)])]
    pallas_call x0 -> x18, Pallas kernels: none -> 94 us  [call(): pl.pallas_call(kernel, out_shape=tuple(outs), in_specs=[space(i in smem_i...]
    ppermute x0 -> x62, starting transfers between devices: none -> 82.3 us  [the longest x36 44.6 us: chip_swap(): return lax.ppermute(value, 'seq', [(s, s ^ 2 * k) for s in range(8)])]
    all_gather x6 -> x0, waiting for transfers between devices: 79.6 us -> none  [the longest x1 53.5 us: on_device(): lax.all_gather(w_out, ('dp', 'seq'), axis=0, tiled=True)]
  transfers between devices with their start and end apart: 12 -> 62, of which waited for: 9 -> 29; matrix products, arithmetic and copies ran while one was open for 10% -> 3% of each run, Pallas kernels for 0% -> 22%
where the time goes in v1:
time: 306 us; the launch traced here: 305 us
  waiting for transfers between devices  106 us (35%)
  Pallas kernels  94 us (31%)
  starting transfers between devices  82.3 us (27%)
  other arithmetic  11.1 us (4%)
  local copies, waits for them, and re-layouts  10.5 us (3%)
    pallas_call x18, Pallas kernels, call(): pl.pallas_call(kernel, out_shape=tuple(outs), in_specs=[space(i in smem_i...  94 us
    ppermute x36, waiting for transfers between devices, chip_swap(): return lax.ppermute(value, 'seq', [(s, s ^ 2 * k) for s in range(8)])  75.5 us
    ppermute x36, starting transfers between devices, chip_swap(): return lax.ppermute(value, 'seq', [(s, s ^ 2 * k) for s in range(8)])  44.6 us
    ppermute x18, starting transfers between devices, z_swap(): return lax.ppermute(value, 'dp', [(s, s ^ j) for s in range(4)])  35.9 us
    ppermute x18, waiting for transfers between devices, z_swap(): return lax.ppermute(value, 'dp', [(s, s ^ j) for s in range(4)])  30.8 us
    unnamed x91, local copies, waits for them, and re-layouts  8.21 us
  transfers between devices with their start and end apart: 62, of which 29 were waited for; matrix products, arithmetic and copies ran while one was open for 3% of the time, Pallas kernels for 22%

profile of v1, /device:TPU:0, one launch (start us, length us, event | category | flops | bytes accessed | tf_op | source)
XLA Modules:
  0.0 305.5 jit_solution(17821063907297840903)
XLA Ops:
  29.7 5.0 %collective-permute-start.16 = (bf16[24,768]{1,0:T(8,128)(2,1)S(1)}, bf16[24,768]{1,0:T(8,128)(2,1)S(1)}, u32[]{:S(2)}, u32[]{:S(2)}) collective-permute-start(bf16[24,768]{1,0:T(8,128)(2,1)S(1)} %copy-done.27), channel_id=1, source_target_pairs={{0,24},{8,16},{16,8},{24,0},{1,25},{9,17},{17,9},{25,1},{2,26},{10... | collective-permute-start | bytes 110600 | tf_op jit(solution)/shard_map/ppermute | solution.py:481
  48.1 4.6 %qkv.1 = (bf16[4,256,192]{2,1,0:T(8,128)(2,1)}, bf16[4,256,384]{2,1,0:T(8,128)(2,1)}, bf16[768,640]{1,0:T(8,128)(2,1)}, f32[16,768]{1,0:T(8,128)}, s32[1]{0:T(128)}) custom-call(s32[1]{0:T(128)} %bitcast.pos.refs_0_, bf16[4,96,640]{2,1,0:T(8,128)(2,1)} %copy-done.12, bf16[4,96,640]{2,1,0:T(8,128)(2,1)} %copy-done.28, bf16[256,768]{1,0:T(8,128)(2,1)} %x0.3, ...), custom_call_target="tpu_custom_call" | custom-call | flops 1006632960 | bytes 4767752 | tf_op jit(solution)/shard_map/qkv/pallas_call | solution.py:37
  54.7 5.3 %collective-permute-done.22 = bf16[96,1664]{1,0:T(8,128)(2,1)S(1)} collective-permute-done((bf16[96,1664]{1,0:T(8,128)(2,1)S(1)}, bf16[96,1664]{1,0:T(8,128)(2,1)S(1)}, u32[]{:S(2)}, u32[]{:S(2)}) %collective-permute-start.22) | collective-permute-done | bytes 319520 | tf_op jit(solution)/shard_map/ppermute | solution.py:481
  65.9 13.7 %attention.1 = (bf16[256,192]{1,0:T(8,128)(2,1)}, bf16[256,192]{1,0:T(8,128)(2,1)}, bf16[256,192]{1,0:T(8,128)(2,1)}, bf16[256,192]{1,0:T(8,128)(2,1)}, f32[4,192,256]{2,1,0:T(8,128)}, /*index=5*/f32[4,8,256]{2,1,0:T(8,128)}) custom-call(s32[1]{0:T(128)} %bitcast.pos.refs_0_, s32[1]{0:T(128)} %get-tuple-element.97.nb, ...), custom_call_target="tpu_custom_call" | custom-call | flops 6000000000 | bytes 3178504 | tf_op jit(solution)/shard_map/attention/pallas_call | solution.py:37
  102.5 10.3 %collective-permute-done.26.refs_1_.refs_3_ = bf16[256,768]{1,0:T(8,128)(2,1)S(1)} collective-permute-done((bf16[256,768]{1,0:T(8,128)(2,1)}, bf16[256,768]{1,0:T(8,128)(2,1)S(1)}, u32[]{:S(2)}, u32[]{:S(2)}) %collective-permute-start.26) | collective-permute-done | bytes 393248 | tf_op jit(solution)/shard_map/ppermute | solution.py:473
  113.7 5.9 %ff.3 = (bf16[256,768]{1,0:T(8,128)(2,1)}, bf16[256,768]{1,0:T(8,128)(2,1)}, f32[256,768]{1,0:T(8,128)}, bf16[256,768]{1,0:T(8,128)(2,1)}, bf16[256,768]{1,0:T(8...) custom-call(bf16[256,768]{1,0:T(8,128)(2,1)} %copy-done.32, ...), custom_call_target="tpu_custom_call" | custom-call | flops 1811939328 | bytes 8478720 | tf_op jit(solution)/shard_map/ff/pallas_call | solution.py:37
  123.1 4.1 %ff.2 = (f32[256,768]{1,0:T(8,128)}, bf16[256,768]{1,0:T(8,128)(2,1)}, f32[256,768]{1,0:T(8,128)}) custom-call(bf16[256,768]{1,0:T(8,128)(2,1)} %get-tuple-element.105.refs_0_.refs_1_, bf16[768,768]{1,0:T(8,128)(2,1)} %get-tuple-element.107.refs_1_.refs_3_.refs_2_.refs_6_, bf16[768,896]{1,0:T(8,128)(2,1)} %get-tuple-element.108.refs_2_.refs_4_.refs_3_.refs_7_, ...), custom_call_target="tpu_custom_call" | custom-call | flops 603979776 | bytes 4939776 | tf_op jit(solution)/shard_map/ff/pallas_call | solution.py:37
  127.2 4.5 %collective-permute-done.28.r1 = bf16[256,768]{1,0:T(8,128)(2,1)S(1)} collective-permute-done((bf16[256,768]{1,0:T(8,128)(2,1)}, bf16[256,768]{1,0:T(8,128)(2,1)S(1)}, u32[]{:S(2)}, u32[]{:S(2)}) %collective-permute-start.28) | collective-permute-done | bytes 393248 | tf_op jit(solution)/shard_map/ppermute | solution.py:473
  131.7 9.4 %collective-permute-done.29.r2 = bf16[256,768]{1,0:T(8,128)(2,1)S(1)} collective-permute-done((bf16[256,768]{1,0:T(8,128)(2,1)}, bf16[256,768]{1,0:T(8,128)(2,1)S(1)}, u32[]{:S(2)}, u32[]{:S(2)}) %collective-permute-start.29) | collective-permute-done | bytes 393248 | tf_op jit(solution)/shard_map/ppermute | solution.py:473
  142.0 3.8 %norm_two.1 = (bf16[256,768]{1,0:T(8,128)(2,1)}, bf16[256,768]{1,0:T(8,128)(2,1)}, f32[256,768]{1,0:T(8,128)}, f32[8,768]{1,0:T(8,128)}) custom-call(f32[16,768]{1,0:T(8,128)} %get-tuple-element.96.vecs, f32[256,768]{1,0:T(8,128)} %get-tuple-element.104.xhat, f32[256,768]{1,0:T(8,128)} %get-tuple-element.110.own, bf16[256,768]{1,0:T(8,128)(2,1)} %copy-done.17, ...), custom_call_target="tpu_custom_call" | custom-call | flops 10000000 | bytes 4792320 | tf_op jit(solution)/shard_map/norm_two/pallas_call | solution.py:37
  149.3 9.7 %collective-permute-done.33.refs_2_.refs_16_ = bf16[256,768]{1,0:T(8,128)(2,1)S(1)} collective-permute-done((bf16[256,768]{1,0:T(8,128)(2,1)}, bf16[256,768]{1,0:T(8,128)(2,1)S(1)}, u32[]{:S(2)}, u32[]{:S(2)}) %collective-permute-start.33) | collective-permute-done | bytes 393248 | tf_op jit(solution)/shard_map/ppermute | solution.py:473
  159.0 7.2 %collective-permute-done.32.refs_1_.refs_15_ = bf16[256,768]{1,0:T(8,128)(2,1)S(1)} collective-permute-done((bf16[256,768]{1,0:T(8,128)(2,1)}, bf16[256,768]{1,0:T(8,128)(2,1)S(1)}, u32[]{:S(2)}, u32[]{:S(2)}) %collective-permute-start.32) | collective-permute-done | bytes 393248 | tf_op jit(solution)/shard_map/ppermute | solution.py:473
  167.1 5.8 %ff_back.3 = (f32[8,768]{1,0:T(8,128)}, bf16[256,768]{1,0:T(8,128)(2,1)}, bf16[256,768]{1,0:T(8,128)(2,1)}, bf16[256,768]{1,0:T(8,128)(2,1)}, bf16[256,768]{1,0:...) custom-call(bf16[256,768]{1,0:T(8,128)(2,1)} %copy-done.37, bf16[256,768]{1,0:T(8,128)(2,1)} %copy-done.36, ...), custom_call_target="tpu_custom_call" | custom-call | flops 1811939328 | bytes 8478720 | tf_op jit(solution)/shard_map/ff_back/pallas_call | solution.py:37
  176.3 4.0 %ff_back.2 = (f32[8,768]{1,0:T(8,128)}, f32[256,768]{1,0:T(8,128)}, bf16[256,768]{1,0:T(8,128)(2,1)}) custom-call(bf16[256,768]{1,0:T(8,128)(2,1)} %get-tuple-element.115.refs_0_.refs_13_, f32[256,768]{1,0:T(8,128)} %get-tuple-element.116.refs_1_, bf16[768,768]{1,0:T(8,128)(2,1)} %get-tuple-element.107.refs_1_.refs_3_.refs_2_.refs_6_, ...), custom_call_target="tpu_custom_call" | custom-call | flops 603979776 | bytes 4939776 | tf_op jit(solution)/shard_map/ff_back/pallas_call | solution.py:37
  180.4 4.7 %collective-permute-done.34.r1 = bf16[256,768]{1,0:T(8,128)(2,1)S(1)} collective-permute-done((bf16[256,768]{1,0:T(8,128)(2,1)}, bf16[256,768]{1,0:T(8,128)(2,1)S(1)}, u32[]{:S(2)}, u32[]{:S(2)}) %collective-permute-start.34) | collective-permute-done | bytes 393248 | tf_op jit(solution)/shard_map/ppermute | solution.py:473
  185.7 7.5 %collective-permute-done.36.r3 = bf16[256,768]{1,0:T(8,128)(2,1)S(1)} collective-permute-done((bf16[256,768]{1,0:T(8,128)(2,1)}, bf16[256,768]{1,0:T(8,128)(2,1)S(1)}, u32[]{:S(2)}, u32[]{:S(2)}) %collective-permute-start.36) | collective-permute-done | bytes 393248 | tf_op jit(solution)/shard_map/ppermute | solution.py:473
  193.9 4.5 %norm_one_back.1 = (bf16[256,192]{1,0:T(8,128)(2,1)}, bf16[256,192]{1,0:T(8,128)(2,1)}, bf16[256,192]{1,0:T(8,128)(2,1)}, bf16[256,192]{1,0:T(8,128)(2,1)}, bf16...) custom-call(s32[1]{0:T(128)} %bitcast.pos.refs_0_, f32[256,768]{1,0:T(8,128)} %get-tuple-element.117.own, ...), custom_call_target="tpu_custom_call" | custom-call | flops 301989888 | bytes 6366212 | tf_op jit(solution)/shard_map/norm_one_back/pallas_call | solution.py:37
  201.4 7.3 %ff_grad.1 = (bf16[4,96,1664]{2,1,0:T(8,128)(2,1)}, bf16[4,96,1664]{2,1,0:T(8,128)(2,1)}) custom-call(s32[1]{0:T(128)} %bitcast.pos.refs_0_, bf16[256,768]{1,0:T(8,128)(2,1)} %get-tuple-element.105.refs_0_.refs_1_, bf16[256,768]{1,0:T(8,128)(2,1)} %copy-done.32, bf16[256,768]{1,0:T(8,128)(2,1)} %copy-done.31, bf16[256,768]{1,0:T(8,128)(2,1)} %copy-done.30, ...), custom_call_target="tpu_custom_call" | custom-call | flops 2415919104 | bytes 8896516 | tf_op jit(solution)/shard_map/ff_grad/pallas_call | solution.py:37
  219.9 14.3 %attention_back.1 = (f32[4,256,192]{2,1,0:T(8,128)}, f32[4,256,384]{2,1,0:T(8,128)}, bf16[4,256,384]{2,1,0:T(8,128)(2,1)}) custom-call(s32[1]{0:T(128)} %bitcast.pos.refs_0_, s32[1]{0:T(128)} %get-tuple-element.97.nb, bf16[4,256,192]{2,1,0:T(8,128)(2,1)} %get-tuple-element.98.q, bf16[4,256,384]{2,1,0:T(8,128)(2,1)} %get-tuple-element.99.mine, ...), custom_call_target="tpu_custom_call" | custom-call | flops 15000000512 | bytes 6324232 | tf_op jit(solution)/shard_map/attention_back/pallas_call | solution.py:37
  237.9 4.8 %collective-permute-start.59 = (bf16[24,896]{1,0:T(8,128)(2,1)S(1)}, bf16[24,896]{1,0:T(8,128)(2,1)S(1)}, u32[]{:S(2)}, u32[]{:S(2)}) collective-permute-start(bf16[24,896]{1,0:T(8,128)(2,1)S(1)} %get-tuple-element.190), channel_id=1, source_target_pairs={{0,8},{8,0},{16,24},{24,16},{1,9},{9,1},{17,25},{25,17},{2,10},{10... | collective-permute-start | bytes 129032 | tf_op jit(solution)/shard_map/ppermute | solution.py:481
  251.3 4.9 %qkv_back.1 = (f32[256,768]{1,0:T(8,128)}, bf16[256,768]{1,0:T(8,128)(2,1)}, bf16[256,768]{1,0:T(8,128)(2,1)}, bf16[256,768]{1,0:T(8,128)(2,1)}, bf16[4,256,640]{2,1,0:T(8,128)(2,1)}, /*index=5*/f32[8,256]{1,0:T(8,128)}) custom-call(f32[4,256,192]{2,1,0:T(8,128)} %get-tuple-element.132.dq, f32[4,256,384]{2,1,0:T(8,128)} %get-tuple-element.133.dmine, ...), custom_call_target="tpu_custom_call" | custom-call | flops 1006632960 | bytes 7413760 | tf_op jit(solution)/shard_map/qkv_back/pallas_call | solution.py:37
  256.7 4.3 %qkv_grad.1 = (bf16[4,96,640]{2,1,0:T(8,128)(2,1)}, bf16[4,96,640]{2,1,0:T(8,128)(2,1)}) custom-call(s32[1]{0:T(128)} %bitcast.pos.refs_0_, bf16[256,768]{1,0:T(8,128)(2,1)} %x0.3, bf16[256,768]{1,0:T(8,128)(2,1)} %copy-done.29, bf16[256,768]{1,0:T(8,128)(2,1)} %collective-permute-done.8.x2, bf16[256,768]{1,0:T(8,128)(2,1)} %collective-permute-done.9.x3, ...), custom_call_target="tpu_custom_call" | custom-call | flops 1006632960 | bytes 3874820 | tf_op jit(solution)/shard_map/qkv_grad/pallas_call | solution.py:37
  266.9 12.0 %collective-permute-done.50 = bf16[96,1664]{1,0:T(8,128)(2,1)S(1)} collective-permute-done((bf16[96,1664]{1,0:T(8,128)(2,1)}, bf16[96,1664]{1,0:T(8,128)(2,1)S(1)}, u32[]{:S(2)}, u32[]{:S(2)}) %collective-permute-start.50) | collective-permute-done | bytes 319520 | tf_op jit(solution)/shard_map/ppermute | solution.py:481
  288.6 5.5 %collective-permute-done.46 = bf16[96,640]{1,0:T(8,128)(2,1)S(1)} collective-permute-done((bf16[96,640]{1,0:T(8,128)(2,1)S(1)}, bf16[96,640]{1,0:T(8,128)(2,1)S(1)}, u32[]{:S(2)}, u32[]{:S(2)}) %collective-permute-start.46) | collective-permute-done | bytes 122912 | tf_op jit(solution)/shard_map/ppermute | solution.py:481
  (244 shorter events, 141.3 us)
Async XLA Ops:
  27.9 19.4 %collective-permute-start.6 = (bf16[4,96,640]{2,1,0:T(8,128)(2,1)S(1)}, bf16[4,96,640]{2,1,0:T(8,128)(2,1)S(1)}, u32[]{:S(2)}, u32[]{:S(2)}) collective-permute-start(bf16[4,96,640]{2,1,0:T(8,128)(2,1)S(1)} %pad_maximum_fusion.2.am), channel_id=1, source_target_pairs={{0,1},{1,0},{2,3},{3,2},{4,5},{5,4},{6,7},{7,6},{8,9},{9,8},{10,11... | collective-permute-start | bytes 1474568 | tf_op jit(solution)/shard_map/ppermute | solution.py:477
  29.7 23.1 %collective-permute-start.16 = (bf16[24,768]{1,0:T(8,128)(2,1)S(1)}, bf16[24,768]{1,0:T(8,128)(2,1)S(1)}, u32[]{:S(2)}, u32[]{:S(2)}) collective-permute-start(bf16[24,768]{1,0:T(8,128)(2,1)S(1)} %copy-done.27), channel_id=1, source_target_pairs={{0,24},{8,16},{16,8},{24,0},{1,25},{9,17},{17,9},{25,1},{2,26},{10... | collective-permute-start | bytes 110600 | tf_op jit(solution)/shard_map/ppermute | solution.py:481
  38.4 21.5 %collective-permute-start.22 = (bf16[96,1664]{1,0:T(8,128)(2,1)S(1)}, bf16[96,1664]{1,0:T(8,128)(2,1)S(1)}, u32[]{:S(2)}, u32[]{:S(2)}) collective-permute-start(bf16[96,1664]{1,0:T(8,128)(2,1)S(1)} %pad_maximum_fusion.3), channel_id=1, source_target_pairs={{0,16},{8,24},{16,0},{24,8},{1,17},{9,25},{17,1},{25,9},{2,18},{10... | collective-permute-start | bytes 958472 | tf_op jit(solution)/shard_map/ppermute | solution.py:481
  41.4 19.2 %collective-permute-start.21 = (bf16[96,1664]{1,0:T(8,128)(2,1)S(1)}, bf16[96,1664]{1,0:T(8,128)(2,1)S(1)}, u32[]{:S(2)}, u32[]{:S(2)}) collective-permute-start(bf16[96,1664]{1,0:T(8,128)(2,1)S(1)} %pad_maximum_fusion.3), channel_id=1, source_target_pairs={{0,8},{8,0},{16,24},{24,16},{1,9},{9,1},{17,25},{25,17},{2,10},{10... | collective-permute-start | bytes 958472 | tf_op jit(solution)/shard_map/ppermute | solution.py:481
  43.9 17.6 %collective-permute-start.23 = (bf16[96,1664]{1,0:T(8,128)(2,1)S(1)}, bf16[96,1664]{1,0:T(8,128)(2,1)S(1)}, u32[]{:S(2)}, u32[]{:S(2)}) collective-permute-start(bf16[96,1664]{1,0:T(8,128)(2,1)S(1)} %pad_maximum_fusion.3), channel_id=1, source_target_pairs={{0,24},{8,16},{16,8},{24,0},{1,25},{9,17},{17,9},{25,1},{2,26},{10... | collective-permute-start | bytes 958472 | tf_op jit(solution)/shard_map/ppermute | solution.py:481
  61.6 34.3 %collective-permute-start.24 = (bf16[4,96,1664]{2,1,0:T(8,128)(2,1)S(1)}, bf16[4,96,1664]{2,1,0:T(8,128)(2,1)S(1)}, u32[]{:S(2)}, u32[]{:S(2)}) collective-permute-start(bf16[4,96,1664]{2,1,0:T(8,128)(2,1)S(1)} %pad_maximum_fusion.mm), channel_id=1, source_target_pairs={{0,1},{1,0},{2,3},{3,2},{4,5},{5,4},{6,7},{7,6},{8,9},{9,8},{10,11... | collective-permute-start | bytes 3833864 | tf_op jit(solution)/shard_map/ppermute | solution.py:477
  65.8 17.4 %collective-permute-start.20 = (bf16[4,96,768]{2,1,0:T(8,128)(2,1)S(1)}, bf16[4,96,768]{2,1,0:T(8,128)(2,1)S(1)}, u32[]{:S(2)}, u32[]{:S(2)}) collective-permute-start(bf16[4,96,768]{2,1,0:T(8,128)(2,1)S(1)} %pad_maximum_fusion.1.om), channel_id=1, source_target_pairs={{0,1},{1,0},{2,3},{3,2},{4,5},{5,4},{6,7},{7,6},{8,9},{9,8},{10,11... | collective-permute-start | bytes 1769480 | tf_op jit(solution)/shard_map/ppermute | solution.py:477
  94.1 18.7 %collective-permute-start.26 = (bf16[256,768]{1,0:T(8,128)(2,1)}, bf16[256,768]{1,0:T(8,128)(2,1)S(1)}, u32[]{:S(2)}, u32[]{:S(2)}) collective-permute-start(bf16[256,768]{1,0:T(8,128)(2,1)} %get-tuple-element.105.refs_0_.refs_1_), channel_id=1, source_target_pairs={{0,4},{1,5},{2,6},{3,7},{4,0},{5,1},{6,2},{7,3},{8,12},{9,13},{10,... | collective-permute-start | bytes 1179656 | tf_op jit(solution)/shard_map/ppermute | solution.py:473
  120.8 20.2 %collective-permute-start.29 = (bf16[256,768]{1,0:T(8,128)(2,1)}, bf16[256,768]{1,0:T(8,128)(2,1)S(1)}, u32[]{:S(2)}, u32[]{:S(2)}) collective-permute-start(bf16[256,768]{1,0:T(8,128)(2,1)} %get-tuple-element.112), channel_id=1, source_target_pairs={{0,4},{1,5},{2,6},{3,7},{4,0},{5,1},{6,2},{7,3},{8,12},{9,13},{10,... | collective-permute-start | bytes 1179656 | tf_op jit(solution)/shard_map/ppermute | solution.py:473
  122.4 18.7 %collective-permute-start.30 = (bf16[256,768]{1,0:T(8,128)(2,1)}, bf16[256,768]{1,0:T(8,128)(2,1)S(1)}, u32[]{:S(2)}, u32[]{:S(2)}) collective-permute-start(bf16[256,768]{1,0:T(8,128)(2,1)} %get-tuple-element.113), channel_id=1, source_target_pairs={{0,6},{1,7},{2,4},{3,5},{4,2},{5,3},{6,0},{7,1},{8,14},{9,15},{10,... | collective-permute-start | bytes 1179656 | tf_op jit(solution)/shard_map/ppermute | solution.py:473
  146.9 19.3 %collective-permute-start.32 = (bf16[256,768]{1,0:T(8,128)(2,1)}, bf16[256,768]{1,0:T(8,128)(2,1)S(1)}, u32[]{:S(2)}, u32[]{:S(2)}) collective-permute-start(bf16[256,768]{1,0:T(8,128)(2,1)} %get-tuple-element.115.refs_0_.refs_13_), channel_id=1, source_target_pairs={{0,4},{1,5},{2,6},{3,7},{4,0},{5,1},{6,2},{7,3},{8,12},{9,13},{10,... | collective-permute-start | bytes 1179656 | tf_op jit(solution)/shard_map/ppermute | solution.py:473
  148.2 18.0 %collective-permute-start.31 = (bf16[256,768]{1,0:T(8,128)(2,1)}, bf16[256,768]{1,0:T(8,128)(2,1)S(1)}, u32[]{:S(2)}, u32[]{:S(2)}) collective-permute-start(bf16[256,768]{1,0:T(8,128)(2,1)} %get-tuple-element.115.refs_0_.refs_13_), channel_id=1, source_target_pairs={{0,2},{1,3},{2,0},{3,1},{4,6},{5,7},{6,4},{7,5},{8,10},{9,11},{10,... | collective-permute-start | bytes 1179656 | tf_op jit(solution)/shard_map/ppermute | solution.py:473
  174.7 18.5 %collective-permute-start.36 = (bf16[256,768]{1,0:T(8,128)(2,1)}, bf16[256,768]{1,0:T(8,128)(2,1)S(1)}, u32[]{:S(2)}, u32[]{:S(2)}) collective-permute-start(bf16[256,768]{1,0:T(8,128)(2,1)} %get-tuple-element.123), channel_id=1, source_target_pairs={{0,6},{1,7},{2,4},{3,5},{4,2},{5,3},{6,0},{7,1},{8,14},{9,15},{10,... | collective-permute-start | bytes 1179656 | tf_op jit(solution)/shard_map/ppermute | solution.py:473
  208.7 37.6 %collective-permute-start.48 = (bf16[4,96,1664]{2,1,0:T(8,128)(2,1)}, bf16[4,96,1664]{2,1,0:T(8,128)(2,1)S(1)}, u32[]{:S(2)}, u32[]{:S(2)}) collective-permute-start(bf16[4,96,1664]{2,1,0:T(8,128)(2,1)} %get-tuple-element.156), channel_id=1, source_target_pairs={{0,1},{1,0},{2,3},{3,2},{4,5},{5,4},{6,7},{7,6},{8,9},{9,8},{10,11... | collective-permute-start | bytes 3833864 | tf_op jit(solution)/shard_map/ppermute | solution.py:477
  213.7 21.5 %collective-permute-start.56 = (bf16[96,896]{1,0:T(8,128)(2,1)}, bf16[96,896]{1,0:T(8,128)(2,1)}, u32[]{:S(2)}, u32[]{:S(2)}) collective-permute-start(bf16[96,896]{1,0:T(8,128)(2,1)} %get-tuple-element.181), channel_id=1, source_target_pairs={{0,2},{1,3},{2,0},{3,1},{4,6},{5,7},{6,4},{7,5},{8,10},{9,11},{10,... | collective-permute-start | bytes 516104 | tf_op jit(solution)/shard_map/ppermute | solution.py:473
  215.3 19.9 %collective-permute-start.58 = (bf16[96,896]{1,0:T(8,128)(2,1)}, bf16[96,896]{1,0:T(8,128)(2,1)}, u32[]{:S(2)}, u32[]{:S(2)}) collective-permute-start(bf16[96,896]{1,0:T(8,128)(2,1)} %get-tuple-element.182), channel_id=1, source_target_pairs={{0,6},{1,7},{2,4},{3,5},{4,2},{5,3},{6,0},{7,1},{8,14},{9,15},{10,... | collective-permute-start | bytes 516104 | tf_op jit(solution)/shard_map/ppermute | solution.py:473
  218.0 17.2 %collective-permute-start.57 = (bf16[96,896]{1,0:T(8,128)(2,1)}, bf16[96,896]{1,0:T(8,128)(2,1)}, u32[]{:S(2)}, u32[]{:S(2)}) collective-permute-start(bf16[96,896]{1,0:T(8,128)(2,1)} %get-tuple-element.183), channel_id=1, source_target_pairs={{0,4},{1,5},{2,6},{3,7},{4,0},{5,1},{6,2},{7,3},{8,12},{9,13},{10,... | collective-permute-start | bytes 516104 | tf_op jit(solution)/shard_map/ppermute | solution.py:473
  237.9 18.2 %collective-permute-start.59 = (bf16[24,896]{1,0:T(8,128)(2,1)S(1)}, bf16[24,896]{1,0:T(8,128)(2,1)S(1)}, u32[]{:S(2)}, u32[]{:S(2)}) collective-permute-start(bf16[24,896]{1,0:T(8,128)(2,1)S(1)} %get-tuple-element.190), channel_id=1, source_target_pairs={{0,8},{8,0},{16,24},{24,16},{1,9},{9,1},{17,25},{25,17},{2,10},{10... | collective-permute-start | bytes 129032 | tf_op jit(solution)/shard_map/ppermute | solution.py:481
  242.7 18.3 %collective-permute-start.61 = (bf16[24,896]{1,0:T(8,128)(2,1)}, bf16[24,896]{1,0:T(8,128)(2,1)S(1)}, u32[]{:S(2)}, u32[]{:S(2)}) collective-permute-start(bf16[24,896]{1,0:T(8,128)(2,1)} %get-tuple-element.191), channel_id=1, source_target_pairs={{0,24},{8,16},{16,8},{24,0},{1,25},{9,17},{17,9},{25,1},{2,26},{10... | collective-permute-start | bytes 129032 | tf_op jit(solution)/shard_map/ppermute | solution.py:481
  247.4 17.2 %collective-permute-start.49 = (bf16[96,1664]{1,0:T(8,128)(2,1)}, bf16[96,1664]{1,0:T(8,128)(2,1)S(1)}, u32[]{:S(2)}, u32[]{:S(2)}) collective-permute-start(bf16[96,1664]{1,0:T(8,128)(2,1)} %get-tuple-element.178), channel_id=1, source_target_pairs={{0,8},{8,0},{16,24},{24,16},{1,9},{9,1},{17,25},{25,17},{2,10},{10... | collective-permute-start | bytes 958472 | tf_op jit(solution)/shard_map/ppermute | solution.py:481
  248.2 18.7 %collective-permute-start.51 = (bf16[96,1664]{1,0:T(8,128)(2,1)}, bf16[96,1664]{1,0:T(8,128)(2,1)S(1)}, u32[]{:S(2)}, u32[]{:S(2)}) collective-permute-start(bf16[96,1664]{1,0:T(8,128)(2,1)} %get-tuple-element.179), channel_id=1, source_target_pairs={{0,24},{8,16},{16,8},{24,0},{1,25},{9,17},{17,9},{25,1},{2,26},{10... | collective-permute-start | bytes 958472 | tf_op jit(solution)/shard_map/ppermute | solution.py:481
  256.1 22.7 %collective-permute-start.50 = (bf16[96,1664]{1,0:T(8,128)(2,1)}, bf16[96,1664]{1,0:T(8,128)(2,1)S(1)}, u32[]{:S(2)}, u32[]{:S(2)}) collective-permute-start(bf16[96,1664]{1,0:T(8,128)(2,1)} %get-tuple-element.180), channel_id=1, source_target_pairs={{0,16},{8,24},{16,0},{24,8},{1,17},{9,25},{17,1},{25,9},{2,18},{10... | collective-permute-start | bytes 958472 | tf_op jit(solution)/shard_map/ppermute | solution.py:481
  261.0 36.2 %collective-permute-start.41 = (bf16[256,768]{1,0:T(8,128)(2,1)}, bf16[256,768]{1,0:T(8,128)(2,1)S(1)}, u32[]{:S(2)}, u32[]{:S(2)}) collective-permute-start(bf16[256,768]{1,0:T(8,128)(2,1)} %get-tuple-element.138), channel_id=1, source_target_pairs={{0,2},{1,3},{2,0},{3,1},{4,6},{5,7},{6,4},{7,5},{8,10},{9,11},{10,... | collective-permute-start | bytes 1179656 | tf_op jit(solution)/shard_map/ppermute | solution.py:473
  261.2 37.4 %collective-permute-start.42 = (bf16[256,768]{1,0:T(8,128)(2,1)S(1)}, bf16[256,768]{1,0:T(8,128)(2,1)S(1)}, u32[]{:S(2)}, u32[]{:S(2)}) collective-permute-start(bf16[256,768]{1,0:T(8,128)(2,1)S(1)} %copy-done.34), channel_id=1, source_target_pairs={{0,4},{1,5},{2,6},{3,7},{4,0},{5,1},{6,2},{7,3},{8,12},{9,13},{10,... | collective-permute-start | bytes 1179656 | tf_op jit(solution)/shard_map/ppermute | solution.py:473
  (82 other events, 710.5 us)

commit v2 on v1

--- a/solution.py
+++ b/solution.py
@@ -40,7 +40,7 @@
         in_specs=[space(i in smem_in) for i in range(len(args))],
         out_specs=tuple(space(i in smem_out) for i in range(len(outs))),
         scratch_shapes=list(scratch),
-        compiler_params=pltpu.CompilerParams(vmem_limit_bytes=60 * 1024 * 1024),
+        compiler_params=pltpu.CompilerParams(vmem_limit_bytes=16 * 1024 * 1024),
         cost_estimate=pl.CostEstimate(
             flops=int(flops), transcendentals=0, bytes_accessed=int(nbytes)
         ),

time: 306 us -> 264 us (0.86)
  Pallas kernels: 94 us -> 43.7 us
  waiting for transfers between devices: 106 us -> 131 us
  other arithmetic: 11.1 us -> 4 us
  local copies, waits for them, and re-layouts: 10.5 us -> 3.66 us
    pallas_call x18, Pallas kernels: 94 us -> 43.7 us  [call(): pl.pallas_call(kernel, out_shape=tuple(outs), in_specs=[space(i in smem_i...]
    ppermute x36, waiting for transfers between devices: 75.5 us -> 89.7 us  [chip_swap(): return lax.ppermute(value, 'seq', [(s, s ^ 2 * k) for s in range(8)])]
    ppermute x18, waiting for transfers between devices: 30.8 us -> 41 us  [z_swap(): return lax.ppermute(value, 'dp', [(s, s ^ j) for s in range(4)])]
    unnamed x91 -> x15, local copies, waits for them, and re-layouts: 8.21 us -> 2.74 us
    another operation x4, other arithmetic: 4.57 us -> 1.17 us
  transfers between devices with their start and end apart: 62 -> 62, of which waited for: 29 -> 31; matrix products, arithmetic and copies ran while one was open for 3% -> 1% of each run, Pallas kernels for 22% -> 13%
where the time goes in v2:
time: 264 us
  waiting for transfers between devices  131 us (50%)
  starting transfers between devices  81.2 us (31%)
  Pallas kernels  43.7 us (17%)
  other arithmetic  4 us (2%)
  local copies, waits for them, and re-layouts  3.66 us (1%)
    ppermute x36, waiting for transfers between devices, chip_swap(): return lax.ppermute(value, 'seq', [(s, s ^ 2 * k) for s in range(8)])  89.7 us
    ppermute x36, starting transfers between devices, chip_swap(): return lax.ppermute(value, 'seq', [(s, s ^ 2 * k) for s in range(8)])  43.9 us
    pallas_call x18, Pallas kernels, call(): pl.pallas_call(kernel, out_shape=tuple(outs), in_specs=[space(i in smem_i...  43.7 us
    ppermute x18, waiting for transfers between devices, z_swap(): return lax.ppermute(value, 'dp', [(s, s ^ j) for s in range(4)])  41 us
    ppermute x18, starting transfers between devices, z_swap(): return lax.ppermute(value, 'dp', [(s, s ^ j) for s in range(4)])  34.9 us
  transfers between devices with their start and end apart: 62, of which 31 were waited for; matrix products, arithmetic and copies ran while one was open for 1% of the time, Pallas kernels for 13%

profile of v2, /device:TPU:0, one launch (start us, length us, event | category | flops | bytes accessed | tf_op | source)
XLA Modules:
  0.0 264.4 jit_solution(6478476313754854024)
XLA Ops:
  6.0 3.0 %collective-permute-start = (bf16[24,1408]{1,0:T(8,128)(2,1)S(1)}, bf16[24,1408]{1,0:T(8,128)(2,1)S(1)}, u32[]{:S(2)}, u32[]{:S(2)}) collective-permute-start(bf16[24,1408]{1,0:T(8,128)(2,1)S(1)} %get-tuple-element.93), channel_id=1, source_target_pairs={{0,2},{1,3},{2,0},{3,1},{4,6},{5,7},{6,4},{7,5},{8,10},{9,11},{10,... | collective-permute-start | bytes 202760 | tf_op jit(solution)/shard_map/ppermute | solution.py:473
  29.8 5.0 %collective-permute-start.16 = (bf16[24,768]{1,0:T(8,128)(2,1)S(1)}, bf16[24,768]{1,0:T(8,128)(2,1)S(1)}, u32[]{:S(2)}, u32[]{:S(2)}) collective-permute-start(bf16[24,768]{1,0:T(8,128)(2,1)S(1)} %copy-done.5), channel_id=1, source_target_pairs={{0,24},{8,16},{16,8},{24,0},{1,25},{9,17},{17,9},{25,1},{2,26},{10... | collective-permute-start | bytes 110600 | tf_op jit(solution)/shard_map/ppermute | solution.py:481
  34.9 3.5 %collective-permute-done.9.x3 = bf16[256,768]{1,0:T(8,128)(2,1)S(1)} collective-permute-done((bf16[256,768]{1,0:T(8,128)(2,1)}, bf16[256,768]{1,0:T(8,128)(2,1)S(1)}, u32[]{:S(2)}, u32[]{:S(2)}) %collective-permute-start.9) | collective-permute-done | bytes 393248 | tf_op jit(solution)/shard_map/ppermute | solution.py:473
  38.5 3.0 %collective-permute-done.8.x2 = bf16[256,768]{1,0:T(8,128)(2,1)S(1)} collective-permute-done((bf16[256,768]{1,0:T(8,128)(2,1)}, bf16[256,768]{1,0:T(8,128)(2,1)S(1)}, u32[]{:S(2)}, u32[]{:S(2)}) %collective-permute-start.8) | collective-permute-done | bytes 393248 | tf_op jit(solution)/shard_map/ppermute | solution.py:473
  43.9 3.5 %collective-permute-start.23 = (bf16[96,1664]{1,0:T(8,128)(2,1)S(1)}, bf16[96,1664]{1,0:T(8,128)(2,1)S(1)}, u32[]{:S(2)}, u32[]{:S(2)}) collective-permute-start(bf16[96,1664]{1,0:T(8,128)(2,1)S(1)} %pad_maximum_fusion.3), channel_id=1, source_target_pairs={{0,24},{8,16},{16,8},{24,0},{1,25},{9,17},{17,9},{25,1},{2,26},{10... | collective-permute-start | bytes 958472 | tf_op jit(solution)/shard_map/ppermute | solution.py:481
  51.5 8.6 %collective-permute-done.22 = bf16[96,1664]{1,0:T(8,128)(2,1)S(1)} collective-permute-done((bf16[96,1664]{1,0:T(8,128)(2,1)S(1)}, bf16[96,1664]{1,0:T(8,128)(2,1)S(1)}, u32[]{:S(2)}, u32[]{:S(2)}) %collective-permute-start.22) | collective-permute-done | bytes 319520 | tf_op jit(solution)/shard_map/ppermute | solution.py:481
  61.8 3.4 %collective-permute-done.18 = bf16[96,768]{1,0:T(8,128)(2,1)S(1)} collective-permute-done((bf16[96,768]{1,0:T(8,128)(2,1)S(1)}, bf16[96,768]{1,0:T(8,128)(2,1)S(1)}, u32[]{:S(2)}, u32[]{:S(2)}) %collective-permute-start.18) | collective-permute-done | bytes 147488 | tf_op jit(solution)/shard_map/ppermute | solution.py:473
  66.0 11.2 %attention.1 = (bf16[256,192]{1,0:T(8,128)(2,1)S(1)}, bf16[256,192]{1,0:T(8,128)(2,1)S(1)}, bf16[256,192]{1,0:T(8,128)(2,1)S(1)}, bf16[256,192]{1,0:T(8,128)(2,1...) custom-call(s32[1]{0:T(128)} %bitcast.pos.refs_0_, s32[1]{0:T(128)} %get-tuple-element.97.nb, ...), custom_call_target="tpu_custom_call" | custom-call | flops 6000000000 | bytes 3178504 | tf_op jit(solution)/shard_map/attention/pallas_call | solution.py:37
  90.5 5.8 %collective-permute-done.27.refs_2_.refs_4_ = bf16[256,768]{1,0:T(8,128)(2,1)S(1)} collective-permute-done((bf16[256,768]{1,0:T(8,128)(2,1)S(1)}, bf16[256,768]{1,0:T(8,128)(2,1)S(1)}, u32[]{:S(2)}, u32[]{:S(2)}) %collective-permute-start.27) | collective-permute-done | bytes 393248 | tf_op jit(solution)/shard_map/ppermute | solution.py:473
  96.3 10.4 %collective-permute-done.26.refs_1_.refs_3_ = bf16[256,768]{1,0:T(8,128)(2,1)S(1)} collective-permute-done((bf16[256,768]{1,0:T(8,128)(2,1)S(1)}, bf16[256,768]{1,0:T(8,128)(2,1)S(1)}, u32[]{:S(2)}, u32[]{:S(2)}) %collective-permute-start.26) | collective-permute-done | bytes 393248 | tf_op jit(solution)/shard_map/ppermute | solution.py:473
  114.3 7.2 %collective-permute-done.28.r1 = bf16[256,768]{1,0:T(8,128)(2,1)S(1)} collective-permute-done((bf16[256,768]{1,0:T(8,128)(2,1)S(1)}, bf16[256,768]{1,0:T(8,128)(2,1)S(1)}, u32[]{:S(2)}, u32[]{:S(2)}) %collective-permute-start.28) | collective-permute-done | bytes 393248 | tf_op jit(solution)/shard_map/ppermute | solution.py:473
  121.6 9.5 %collective-permute-done.29.r2 = bf16[256,768]{1,0:T(8,128)(2,1)S(1)} collective-permute-done((bf16[256,768]{1,0:T(8,128)(2,1)S(1)}, bf16[256,768]{1,0:T(8,128)(2,1)S(1)}, u32[]{:S(2)}, u32[]{:S(2)}) %collective-permute-start.29) | collective-permute-done | bytes 393248 | tf_op jit(solution)/shard_map/ppermute | solution.py:473
  136.1 9.5 %collective-permute-done.33.refs_2_.refs_16_ = bf16[256,768]{1,0:T(8,128)(2,1)S(1)} collective-permute-done((bf16[256,768]{1,0:T(8,128)(2,1)S(1)}, bf16[256,768]{1,0:T(8,128)(2,1)S(1)}, u32[]{:S(2)}, u32[]{:S(2)}) %collective-permute-start.33) | collective-permute-done | bytes 393248 | tf_op jit(solution)/shard_map/ppermute | solution.py:473
  145.6 7.1 %collective-permute-done.32.refs_1_.refs_15_ = bf16[256,768]{1,0:T(8,128)(2,1)S(1)} collective-permute-done((bf16[256,768]{1,0:T(8,128)(2,1)S(1)}, bf16[256,768]{1,0:T(8,128)(2,1)S(1)}, u32[]{:S(2)}, u32[]{:S(2)}) %collective-permute-start.32) | collective-permute-done | bytes 393248 | tf_op jit(solution)/shard_map/ppermute | solution.py:473
  159.2 7.5 %collective-permute-done.34.r1 = bf16[256,768]{1,0:T(8,128)(2,1)S(1)} collective-permute-done((bf16[256,768]{1,0:T(8,128)(2,1)S(1)}, bf16[256,768]{1,0:T(8,128)(2,1)S(1)}, u32[]{:S(2)}, u32[]{:S(2)}) %collective-permute-start.34) | collective-permute-done | bytes 393248 | tf_op jit(solution)/shard_map/ppermute | solution.py:473
  166.8 8.4 %collective-permute-done.35.r2 = bf16[256,768]{1,0:T(8,128)(2,1)S(1)} collective-permute-done((bf16[256,768]{1,0:T(8,128)(2,1)S(1)}, bf16[256,768]{1,0:T(8,128)(2,1)S(1)}, u32[]{:S(2)}, u32[]{:S(2)}) %collective-permute-start.35) | collective-permute-done | bytes 393248 | tf_op jit(solution)/shard_map/ppermute | solution.py:473
  177.3 3.1 %ff_grad.1 = (bf16[4,96,1664]{2,1,0:T(8,128)(2,1)S(1)}, bf16[4,96,1664]{2,1,0:T(8,128)(2,1)S(1)}) custom-call(s32[1]{0:T(128)} %bitcast.pos.refs_0_, bf16[256,768]{1,0:T(8,128)(2,1)S(1)} %get-tuple-element.105.refs_0_.refs_1_, bf16[256,768]{1,0:T(8,128)(2,1)S(1)} %collective-permute-done.25.refs_0_.refs_2_, ...), custom_call_target="tpu_custom_call" | custom-call | flops 2415919104 | bytes 8896516 | tf_op jit(solution)/shard_map/ff_grad/pallas_call | solution.py:37
  190.4 11.0 %attention_back.1 = (f32[4,256,192]{2,1,0:T(8,128)S(1)}, f32[4,256,384]{2,1,0:T(8,128)S(1)}, bf16[4,256,384]{2,1,0:T(8,128)(2,1)S(1)}) custom-call(s32[1]{0:T(128)} %bitcast.pos.refs_0_, s32[1]{0:T(128)} %get-tuple-element.97.nb, bf16[4,256,192]{2,1,0:T(8,128)(2,1)S(1)} %get-tuple-element.98.q, bf16[4,256,384]{2,1,0:T(8,128)(2,1)S(1)} %get-tuple-element.99.mine, ...), custom_call_target="tpu_custom_call" | custom-call | flops 15000000512 | bytes 6324232 | tf_op jit(solution)/shard_map/attention_back/pallas_call | solution.py:37
  203.2 7.1 %collective-permute-start.61 = (bf16[24,896]{1,0:T(8,128)(2,1)S(1)}, bf16[24,896]{1,0:T(8,128)(2,1)S(1)}, u32[]{:S(2)}, u32[]{:S(2)}) collective-permute-start(bf16[24,896]{1,0:T(8,128)(2,1)S(1)} %get-tuple-element.191), channel_id=1, source_target_pairs={{0,24},{8,16},{16,8},{24,0},{1,25},{9,17},{17,9},{25,1},{2,26},{10... | collective-permute-start | bytes 129032 | tf_op jit(solution)/shard_map/ppermute | solution.py:481
  211.2 3.8 %collective-permute-start.51 = (bf16[96,1664]{1,0:T(8,128)(2,1)S(1)}, bf16[96,1664]{1,0:T(8,128)(2,1)S(1)}, u32[]{:S(2)}, u32[]{:S(2)}) collective-permute-start(bf16[96,1664]{1,0:T(8,128)(2,1)S(1)} %get-tuple-element.179), channel_id=1, source_target_pairs={{0,24},{8,16},{16,8},{24,0},{1,25},{9,17},{17,9},{25,1},{2,26},{10... | collective-permute-start | bytes 958472 | tf_op jit(solution)/shard_map/ppermute | solution.py:481
  222.6 7.8 %collective-permute-done.51 = bf16[96,1664]{1,0:T(8,128)(2,1)S(1)} collective-permute-done((bf16[96,1664]{1,0:T(8,128)(2,1)S(1)}, bf16[96,1664]{1,0:T(8,128)(2,1)S(1)}, u32[]{:S(2)}, u32[]{:S(2)}) %collective-permute-start.51) | collective-permute-done | bytes 319520 | tf_op jit(solution)/shard_map/ppermute | solution.py:481
  230.4 11.6 %collective-permute-done.50 = bf16[96,1664]{1,0:T(8,128)(2,1)S(1)} collective-permute-done((bf16[96,1664]{1,0:T(8,128)(2,1)S(1)}, bf16[96,1664]{1,0:T(8,128)(2,1)S(1)}, u32[]{:S(2)}, u32[]{:S(2)}) %collective-permute-start.50) | collective-permute-done | bytes 319520 | tf_op jit(solution)/shard_map/ppermute | solution.py:481
  245.9 3.3 %collective-permute-done.45 = bf16[96,640]{1,0:T(8,128)(2,1)S(1)} collective-permute-done((bf16[96,640]{1,0:T(8,128)(2,1)S(1)}, bf16[96,640]{1,0:T(8,128)(2,1)S(1)}, u32[]{:S(2)}, u32[]{:S(2)}) %collective-permute-start.45) | collective-permute-done | bytes 122912 | tf_op jit(solution)/shard_map/ppermute | solution.py:481
  251.2 4.6 %collective-permute-done.46 = bf16[96,640]{1,0:T(8,128)(2,1)S(1)} collective-permute-done((bf16[96,640]{1,0:T(8,128)(2,1)S(1)}, bf16[96,640]{1,0:T(8,128)(2,1)S(1)}, u32[]{:S(2)}, u32[]{:S(2)}) %collective-permute-start.46) | collective-permute-done | bytes 122912 | tf_op jit(solution)/shard_map/ppermute | solution.py:481
  (168 shorter events, 104.4 us)
Async XLA Ops:
  28.0 19.4 %collective-permute-start.6 = (bf16[4,96,640]{2,1,0:T(8,128)(2,1)S(1)}, bf16[4,96,640]{2,1,0:T(8,128)(2,1)S(1)}, u32[]{:S(2)}, u32[]{:S(2)}) collective-permute-start(bf16[4,96,640]{2,1,0:T(8,128)(2,1)S(1)} %pad_maximum_fusion.2.am), channel_id=1, source_target_pairs={{0,1},{1,0},{2,3},{3,2},{4,5},{5,4},{6,7},{7,6},{8,9},{9,8},{10,11... | collective-permute-start | bytes 1474568 | tf_op jit(solution)/shard_map/ppermute | solution.py:477
  28.2 15.7 %collective-permute-start.7 = (bf16[256,768]{1,0:T(8,128)(2,1)S(1)}, bf16[256,768]{1,0:T(8,128)(2,1)S(1)}, u32[]{:S(2)}, u32[]{:S(2)}) collective-permute-start(bf16[256,768]{1,0:T(8,128)(2,1)S(1)} %copy-done.1), channel_id=1, source_target_pairs={{0,2},{1,3},{2,0},{3,1},{4,6},{5,7},{6,4},{7,5},{8,10},{9,11},{10,... | collective-permute-start | bytes 1179656 | tf_op jit(solution)/shard_map/ppermute | solution.py:473
  29.8 19.8 %collective-permute-start.16 = (bf16[24,768]{1,0:T(8,128)(2,1)S(1)}, bf16[24,768]{1,0:T(8,128)(2,1)S(1)}, u32[]{:S(2)}, u32[]{:S(2)}) collective-permute-start(bf16[24,768]{1,0:T(8,128)(2,1)S(1)} %copy-done.5), channel_id=1, source_target_pairs={{0,24},{8,16},{16,8},{24,0},{1,25},{9,17},{17,9},{25,1},{2,26},{10... | collective-permute-start | bytes 110600 | tf_op jit(solution)/shard_map/ppermute | solution.py:481
  38.4 21.6 %collective-permute-start.22 = (bf16[96,1664]{1,0:T(8,128)(2,1)S(1)}, bf16[96,1664]{1,0:T(8,128)(2,1)S(1)}, u32[]{:S(2)}, u32[]{:S(2)}) collective-permute-start(bf16[96,1664]{1,0:T(8,128)(2,1)S(1)} %pad_maximum_fusion.3), channel_id=1, source_target_pairs={{0,16},{8,24},{16,0},{24,8},{1,17},{9,25},{17,1},{25,9},{2,18},{10... | collective-permute-start | bytes 958472 | tf_op jit(solution)/shard_map/ppermute | solution.py:481
  41.4 19.3 %collective-permute-start.21 = (bf16[96,1664]{1,0:T(8,128)(2,1)S(1)}, bf16[96,1664]{1,0:T(8,128)(2,1)S(1)}, u32[]{:S(2)}, u32[]{:S(2)}) collective-permute-start(bf16[96,1664]{1,0:T(8,128)(2,1)S(1)} %pad_maximum_fusion.3), channel_id=1, source_target_pairs={{0,8},{8,0},{16,24},{24,16},{1,9},{9,1},{17,25},{25,17},{2,10},{10... | collective-permute-start | bytes 958472 | tf_op jit(solution)/shard_map/ppermute | solution.py:481
  43.9 17.6 %collective-permute-start.23 = (bf16[96,1664]{1,0:T(8,128)(2,1)S(1)}, bf16[96,1664]{1,0:T(8,128)(2,1)S(1)}, u32[]{:S(2)}, u32[]{:S(2)}) collective-permute-start(bf16[96,1664]{1,0:T(8,128)(2,1)S(1)} %pad_maximum_fusion.3), channel_id=1, source_target_pairs={{0,24},{8,16},{16,8},{24,0},{1,25},{9,17},{17,9},{25,1},{2,26},{10... | collective-permute-start | bytes 958472 | tf_op jit(solution)/shard_map/ppermute | solution.py:481
  49.5 16.5 %collective-permute-start.10 = (bf16[4,256,384]{2,1,0:T(8,128)(2,1)S(1)}, bf16[4,256,384]{2,1,0:T(8,128)(2,1)S(1)}, u32[]{:S(2)}, u32[]{:S(2)}) collective-permute-start(bf16[4,256,384]{2,1,0:T(8,128)(2,1)S(1)} %get-tuple-element.99.mine), channel_id=1, source_target_pairs={{0,1},{1,0},{2,3},{3,2},{4,5},{5,4},{6,7},{7,6},{8,9},{9,8},{10,11... | collective-permute-start | bytes 2359304 | tf_op jit(solution)/shard_map/ppermute | solution.py:477
  61.7 28.3 %collective-permute-start.24 = (bf16[4,96,1664]{2,1,0:T(8,128)(2,1)S(1)}, bf16[4,96,1664]{2,1,0:T(8,128)(2,1)S(1)}, u32[]{:S(2)}, u32[]{:S(2)}) collective-permute-start(bf16[4,96,1664]{2,1,0:T(8,128)(2,1)S(1)} %pad_maximum_fusion.mm), channel_id=1, source_target_pairs={{0,1},{1,0},{2,3},{3,2},{4,5},{5,4},{6,7},{7,6},{8,9},{9,8},{10,11... | collective-permute-start | bytes 3833864 | tf_op jit(solution)/shard_map/ppermute | solution.py:477
  88.2 18.5 %collective-permute-start.26 = (bf16[256,768]{1,0:T(8,128)(2,1)S(1)}, bf16[256,768]{1,0:T(8,128)(2,1)S(1)}, u32[]{:S(2)}, u32[]{:S(2)}) collective-permute-start(bf16[256,768]{1,0:T(8,128)(2,1)S(1)} %get-tuple-element.105.refs_0_.refs_1_), channel_id=1, source_target_pairs={{0,4},{1,5},{2,6},{3,7},{4,0},{5,1},{6,2},{7,3},{8,12},{9,13},{10,... | collective-permute-start | bytes 1179656 | tf_op jit(solution)/shard_map/ppermute | solution.py:473
  90.0 16.7 %collective-permute-start.25 = (bf16[256,768]{1,0:T(8,128)(2,1)S(1)}, bf16[256,768]{1,0:T(8,128)(2,1)S(1)}, u32[]{:S(2)}, u32[]{:S(2)}) collective-permute-start(bf16[256,768]{1,0:T(8,128)(2,1)S(1)} %get-tuple-element.105.refs_0_.refs_1_), channel_id=1, source_target_pairs={{0,2},{1,3},{2,0},{3,1},{4,6},{5,7},{6,4},{7,5},{8,10},{9,11},{10,... | collective-permute-start | bytes 1179656 | tf_op jit(solution)/shard_map/ppermute | solution.py:473
  111.1 19.9 %collective-permute-start.29 = (bf16[256,768]{1,0:T(8,128)(2,1)S(1)}, bf16[256,768]{1,0:T(8,128)(2,1)S(1)}, u32[]{:S(2)}, u32[]{:S(2)}) collective-permute-start(bf16[256,768]{1,0:T(8,128)(2,1)S(1)} %get-tuple-element.112), channel_id=1, source_target_pairs={{0,4},{1,5},{2,6},{3,7},{4,0},{5,1},{6,2},{7,3},{8,12},{9,13},{10,... | collective-permute-start | bytes 1179656 | tf_op jit(solution)/shard_map/ppermute | solution.py:473
  112.7 18.4 %collective-permute-start.30 = (bf16[256,768]{1,0:T(8,128)(2,1)S(1)}, bf16[256,768]{1,0:T(8,128)(2,1)S(1)}, u32[]{:S(2)}, u32[]{:S(2)}) collective-permute-start(bf16[256,768]{1,0:T(8,128)(2,1)S(1)} %get-tuple-element.113), channel_id=1, source_target_pairs={{0,6},{1,7},{2,4},{3,5},{4,2},{5,3},{6,0},{7,1},{8,14},{9,15},{10,... | collective-permute-start | bytes 1179656 | tf_op jit(solution)/shard_map/ppermute | solution.py:473
  133.8 18.8 %collective-permute-start.32 = (bf16[256,768]{1,0:T(8,128)(2,1)S(1)}, bf16[256,768]{1,0:T(8,128)(2,1)S(1)}, u32[]{:S(2)}, u32[]{:S(2)}) collective-permute-start(bf16[256,768]{1,0:T(8,128)(2,1)S(1)} %get-tuple-element.115.refs_0_.refs_13_), channel_id=1, source_target_pairs={{0,4},{1,5},{2,6},{3,7},{4,0},{5,1},{6,2},{7,3},{8,12},{9,13},{10,... | collective-permute-start | bytes 1179656 | tf_op jit(solution)/shard_map/ppermute | solution.py:473
  135.2 17.4 %collective-permute-start.31 = (bf16[256,768]{1,0:T(8,128)(2,1)S(1)}, bf16[256,768]{1,0:T(8,128)(2,1)S(1)}, u32[]{:S(2)}, u32[]{:S(2)}) collective-permute-start(bf16[256,768]{1,0:T(8,128)(2,1)S(1)} %get-tuple-element.115.refs_0_.refs_13_), channel_id=1, source_target_pairs={{0,2},{1,3},{2,0},{3,1},{4,6},{5,7},{6,4},{7,5},{8,10},{9,11},{10,... | collective-permute-start | bytes 1179656 | tf_op jit(solution)/shard_map/ppermute | solution.py:473
  156.0 19.2 %collective-permute-start.35 = (bf16[256,768]{1,0:T(8,128)(2,1)S(1)}, bf16[256,768]{1,0:T(8,128)(2,1)S(1)}, u32[]{:S(2)}, u32[]{:S(2)}) collective-permute-start(bf16[256,768]{1,0:T(8,128)(2,1)S(1)} %get-tuple-element.122), channel_id=1, source_target_pairs={{0,4},{1,5},{2,6},{3,7},{4,0},{5,1},{6,2},{7,3},{8,12},{9,13},{10,... | collective-permute-start | bytes 1179656 | tf_op jit(solution)/shard_map/ppermute | solution.py:473
  156.8 18.5 %collective-permute-start.36 = (bf16[256,768]{1,0:T(8,128)(2,1)S(1)}, bf16[256,768]{1,0:T(8,128)(2,1)S(1)}, u32[]{:S(2)}, u32[]{:S(2)}) collective-permute-start(bf16[256,768]{1,0:T(8,128)(2,1)S(1)} %get-tuple-element.123), channel_id=1, source_target_pairs={{0,6},{1,7},{2,4},{3,5},{4,2},{5,3},{6,0},{7,1},{8,14},{9,15},{10,... | collective-permute-start | bytes 1179656 | tf_op jit(solution)/shard_map/ppermute | solution.py:473
  180.4 29.9 %collective-permute-start.48 = (bf16[4,96,1664]{2,1,0:T(8,128)(2,1)S(1)}, bf16[4,96,1664]{2,1,0:T(8,128)(2,1)S(1)}, u32[]{:S(2)}, u32[]{:S(2)}) collective-permute-start(bf16[4,96,1664]{2,1,0:T(8,128)(2,1)S(1)} %get-tuple-element.156), channel_id=1, source_target_pairs={{0,1},{1,0},{2,3},{3,2},{4,5},{5,4},{6,7},{7,6},{8,9},{9,8},{10,11... | collective-permute-start | bytes 3833864 | tf_op jit(solution)/shard_map/ppermute | solution.py:477
  184.5 18.4 %collective-permute-start.56 = (bf16[96,896]{1,0:T(8,128)(2,1)S(1)}, bf16[96,896]{1,0:T(8,128)(2,1)S(1)}, u32[]{:S(2)}, u32[]{:S(2)}) collective-permute-start(bf16[96,896]{1,0:T(8,128)(2,1)S(1)} %get-tuple-element.181), channel_id=1, source_target_pairs={{0,2},{1,3},{2,0},{3,1},{4,6},{5,7},{6,4},{7,5},{8,10},{9,11},{10,... | collective-permute-start | bytes 516104 | tf_op jit(solution)/shard_map/ppermute | solution.py:473
  187.3 15.7 %collective-permute-start.58 = (bf16[96,896]{1,0:T(8,128)(2,1)S(1)}, bf16[96,896]{1,0:T(8,128)(2,1)S(1)}, u32[]{:S(2)}, u32[]{:S(2)}) collective-permute-start(bf16[96,896]{1,0:T(8,128)(2,1)S(1)} %get-tuple-element.182), channel_id=1, source_target_pairs={{0,6},{1,7},{2,4},{3,5},{4,2},{5,3},{6,0},{7,1},{8,14},{9,15},{10,... | collective-permute-start | bytes 516104 | tf_op jit(solution)/shard_map/ppermute | solution.py:473
  211.2 19.2 %collective-permute-start.51 = (bf16[96,1664]{1,0:T(8,128)(2,1)S(1)}, bf16[96,1664]{1,0:T(8,128)(2,1)S(1)}, u32[]{:S(2)}, u32[]{:S(2)}) collective-permute-start(bf16[96,1664]{1,0:T(8,128)(2,1)S(1)} %get-tuple-element.179), channel_id=1, source_target_pairs={{0,24},{8,16},{16,8},{24,0},{1,25},{9,17},{17,9},{25,1},{2,26},{10... | collective-permute-start | bytes 958472 | tf_op jit(solution)/shard_map/ppermute | solution.py:481
  216.5 25.5 %collective-permute-start.50 = (bf16[96,1664]{1,0:T(8,128)(2,1)S(1)}, bf16[96,1664]{1,0:T(8,128)(2,1)S(1)}, u32[]{:S(2)}, u32[]{:S(2)}) collective-permute-start(bf16[96,1664]{1,0:T(8,128)(2,1)S(1)} %get-tuple-element.180), channel_id=1, source_target_pairs={{0,16},{8,24},{16,0},{24,8},{1,17},{9,25},{17,1},{25,9},{2,18},{10... | collective-permute-start | bytes 958472 | tf_op jit(solution)/shard_map/ppermute | solution.py:481
  218.2 39.8 %collective-permute-start.41 = (bf16[256,768]{1,0:T(8,128)(2,1)S(1)}, bf16[256,768]{1,0:T(8,128)(2,1)S(1)}, u32[]{:S(2)}, u32[]{:S(2)}) collective-permute-start(bf16[256,768]{1,0:T(8,128)(2,1)S(1)} %get-tuple-element.138), channel_id=1, source_target_pairs={{0,2},{1,3},{2,0},{3,1},{4,6},{5,7},{6,4},{7,5},{8,10},{9,11},{10,... | collective-permute-start | bytes 1179656 | tf_op jit(solution)/shard_map/ppermute | solution.py:473
  219.3 40.3 %collective-permute-start.42 = (bf16[256,768]{1,0:T(8,128)(2,1)S(1)}, bf16[256,768]{1,0:T(8,128)(2,1)S(1)}, u32[]{:S(2)}, u32[]{:S(2)}) collective-permute-start(bf16[256,768]{1,0:T(8,128)(2,1)S(1)} %get-tuple-element.139), channel_id=1, source_target_pairs={{0,4},{1,5},{2,6},{3,7},{4,0},{5,1},{6,2},{7,3},{8,12},{9,13},{10,... | collective-permute-start | bytes 1179656 | tf_op jit(solution)/shard_map/ppermute | solution.py:473
  222.6 19.7 %collective-permute-start.44 = (bf16[4,96,640]{2,1,0:T(8,128)(2,1)S(1)}, bf16[4,96,640]{2,1,0:T(8,128)(2,1)S(1)}, u32[]{:S(2)}, u32[]{:S(2)}) collective-permute-start(bf16[4,96,640]{2,1,0:T(8,128)(2,1)S(1)} %get-tuple-element.144), channel_id=1, source_target_pairs={{0,1},{1,0},{2,3},{3,2},{4,5},{5,4},{6,7},{7,6},{8,9},{9,8},{10,11... | collective-permute-start | bytes 1474568 | tf_op jit(solution)/shard_map/ppermute | solution.py:477
  (44 other events, 409.6 us)

commit v3 on v2

--- a/solution.py
+++ b/solution.py
@@ -31,9 +31,8 @@
     return jax.ShapeDtypeStruct(shape, dtype)
 
 
-def call(kernel, args, outs, scratch=(), smem_in=(0,), smem_out=(), flops=0, name=None):
+def call(kernel, args, outs, scratch=(), smem_in=(0,), smem_out=(), flops=1, name=None):
     space = lambda inside: pl.BlockSpec(memory_space=pltpu.SMEM if inside else pltpu.VMEM)
-    nbytes = sum(math.prod(a.shape) * a.dtype.itemsize for a in tuple(args) + tuple(outs))
     return pl.pallas_call(
         kernel,
         out_shape=tuple(outs),
@@ -41,9 +40,7 @@
         out_specs=tuple(space(i in smem_out) for i in range(len(outs))),
         scratch_shapes=list(scratch),
         compiler_params=pltpu.CompilerParams(vmem_limit_bytes=16 * 1024 * 1024),
-        cost_estimate=pl.CostEstimate(
-            flops=int(flops), transcendentals=0, bytes_accessed=int(nbytes)
-        ),
+        cost_estimate=pl.CostEstimate(flops=int(flops), transcendentals=0, bytes_accessed=1),
         name=name,
     )(*args)
 
@@ -57,40 +54,69 @@
     return pl.multiple_of(start, size)
 
 
-def pack_kernel(pos, wqkv, win, wout, smalls, p0, p1, p2, p3, wx):
-    z, p, c = place(pos)
+def pack_kernel(wqkv, wo, wout, smalls, zq, zw):
     rows = lax.broadcasted_iota(jnp.int32, (96, 96), 0)
     cols = lax.broadcasted_iota(jnp.int32, (96, 96), 1)
     eye = (rows == cols).astype(BF16)
     side = dot(eye, smalls[...], NT).astype(BF16)
-    wx[...] = jnp.concatenate([wout[...], side, jnp.zeros((96, 112), BF16)], axis=1)
-    small = jnp.concatenate([side[:24], jnp.zeros((24, 48), BF16)], axis=1)
-
-    def piece(chip):
-        parts = [wqkv[:, 768 * i + 192 * chip : 768 * i + 192 * chip + 192] for i in range(3)]
-        parts.append(small)
-        parts += [win[:, 768 * i + 192 * chip : 768 * i + 192 * chip + 192] for i in range(4)]
-        return jnp.concatenate(parts, axis=1)
-
+    side = jnp.concatenate([side, jnp.zeros((96, 112), BF16)], axis=1)
+    zw[:, 0:768] = wout[...]
+    zw[:, 768:896] = side
+    zq[:, 0:2304] = wqkv[...]
+    zq[:, 2304:3072] = wo[...]
+    zq[:, 3072:3200] = side[:24]
+
+
+def each_chip(p, run):
     for own in range(4):
 
         @pl.when(p == own)
         def _(own=own):
-            for k, out in enumerate((p0, p1, p2, p3)):
-                out[...] = piece(own ^ k)
-
-
-def interleave(pos, mine, other, lanes, out, order):
+            run(own)
+
+
+def split_qkv_kernel(pos, z0, z1, z2, z3, p0, p1, p2, p3, wo):
+    z, p, c = place(pos)
+    for i, zq in enumerate((z0, z1, z2, z3)):
+        wo[24 * i : 24 * i + 24, :] = zq[:, 2304:3072]
+
+    def run(own):
+        for k, out in enumerate((p0, p1, p2, p3)):
+            at = 192 * (own ^ k)
+            for i, zq in enumerate((z0, z1, z2, z3)):
+                parts = [zq[:, 768 * t + at : 768 * t + at + 192] for t in range(3)]
+                parts.append(zq[:, 3072:3136])
+                out[24 * i : 24 * i + 24, :] = jnp.concatenate(parts, axis=1)
+
+    each_chip(p, run)
+
+
+def split_in_kernel(pos, z0, z1, mine, theirs):
+    z, p, c = place(pos)
+    for side in range(2):
+
+        @pl.when((z & 1) == side)
+        def _(side=side):
+            for out, g in ((mine, side), (theirs, 1 - side)):
+                for i, zi in enumerate((z0, z1)):
+                    at = slice(24 * i, 24 * i + 24)
+                    out[at, 0:768] = zi[:, 768 * g : 768 * g + 768]
+                    out[at, 768:1536] = zi[:, 768 * g + 1536 : 768 * g + 2304]
+
+
+SLOTS = (0, 2, 1, 3)
+
+
+def interleave(pos, mine, other, out, slots):
     z, p, c = place(pos)
 
     def run(first, second):
-        for j in range(4):
-            for k in range(4):
-                at = (j, slice(24 * k, 24 * k + 24), lanes) if order == "jk" else (
-                    k, slice(24 * j, 24 * j + 24), lanes)
+        for k in range(4):
+            for i in range(4):
+                at = (k, slice(24 * i, 24 * i + 24), slice(None))
                 block = jnp.concatenate([first[at], second[at]], axis=0)
-                start = ((z ^ j) * 4 + (p ^ k)) * 48
-                out[pl.ds(row_of(start, 16), 48), :] = block
+                plane = z ^ slots[i]
+                out[pl.ds(row_of((4 * plane + (p ^ k)) * 48, 16), 48), :] = block
 
     @pl.when(c == 0)
     def _():
@@ -103,77 +129,112 @@
 
 def qkv_kernel(pos, am, ao, x0, x1, x2, x3, q, kv, wq, vecs, nb, bias):
     z, p, c = place(pos)
-    interleave(pos, am, ao, slice(None), wq, "jk")
+    interleave(pos, am, ao, wq, (0, 1, 2, 3))
     flipped = jnp.transpose(wq[:, 512:640].astype(F32))
     vecs[...] = flipped[64:80]
-    for own in range(4):
-
-        @pl.when(p == own)
-        def _(own=own):
-            at = slice(192 * own, 192 * own + 192)
-            bias[0:1, :] = jnp.concatenate(
-                [vecs[0:1, at], jnp.zeros((1, 192), F32), vecs[1:2, at], jnp.zeros((1, 64), F32)],
-                axis=1,
-            )
-
+
+    def run(own):
+        at = slice(192 * own, 192 * own + 192)
+        bias[0:1, :] = jnp.concatenate(
+            [vecs[0:1, at], jnp.zeros((1, 192), F32), vecs[1:2, at], jnp.zeros((1, 64), F32)],
+            axis=1,
+        )
+
+    each_chip(p, run)
     lane = lax.broadcasted_iota(jnp.int32, (1, 768), 1)
     mask = (lane >= 192 * z) & (lane < 192 * z + 192) & (lane % 24 == 0)
     second = jnp.sum(jnp.where(mask, vecs[8:9, :], 0.0))
     nb[0] = 8 - second.astype(jnp.int32)
     for k, x in enumerate((x0, x1, x2, x3)):
         got = (dot(x[...], wq[...]) + bias[0:1, :]).astype(BF16)
-        q[k] = got[:, :192]
-        kv[k] = got[:, 192:576]
-
-
-def weights_kernel(pos, mm, mo, wi, wx, bin_):
-    z, p, c = place(pos)
-    interleave(pos, mm, mo, slice(0, 768), wi, "jk")
-    for j in range(4):
-        base = (z ^ j) * 192
-        wx[pl.ds(row_of(base + c * 96, 32), 96), :] = mm[j, :, 768:1664]
-        wx[pl.ds(row_of(base + (1 - c) * 96, 32), 96), :] = mo[j, :, 768:1664]
+        pad = jnp.zeros((got.shape[0], 64), BF16)
+        q[k] = jnp.concatenate([got[:, :192], pad], axis=1)
+        kv[k] = jnp.concatenate([got[:, 192:384], pad, got[:, 384:576], pad], axis=1)
+
+
+def join_in_kernel(pos, im, io, wi):
+    interleave(pos, im, io, wi, SLOTS)
+
+
+def join_wo_kernel(pos, om, oo, wo):
+    interleave(pos, om, oo, wo, (0, 1, 2, 3))
+
+
+def join_out_kernel(pos, wm, wo_, wx, bin_):
+    z, p, c = place(pos)
+    for k in range(4):
+        for i in range(2):
+            start = (((z ^ (2 * i)) >> 1) * 4 + (p ^ SLOTS[k])) * 192
+            at = (k, slice(96 * i, 96 * i + 96), slice(None))
+            wx[pl.ds(row_of(start + c * 96, 32), 96), :] = wm[at]
+            wx[pl.ds(row_of(start + (1 - c) * 96, 32), 96), :] = wo_[at]
     flipped = jnp.transpose(wx[:, 768:896].astype(F32))
     bin_[...] = flipped[8:16]
 
 
-def wo_kernel(pos, om, oo, wo):
-    interleave(pos, om, oo, slice(None), wo, "kj")
-
-
-def absolute_kv(pos, mine, other, kv):
-    z, p, c = place(pos)
-    for k in range(4):
-        first = 2 * (p ^ k)
-        kv[first + c] = mine[k]
-        kv[first + 1 - c] = other[k]
-
-
 def key_range(pos, nb, k):
     z, p, c = place(pos)
     block = 2 * (p ^ k) + c
     return jnp.where(block < nb[0], 0, nb[0]), block + 1
 
 
-def attention_kernel(pos, nb, q, mine, other, a0, a1, a2, a3, ot, lse, kv):
+def absolute_keys(pos, mine, other, keys, values, key_t, value_t):
+    z, p, c = place(pos)
+    for k in range(4):
+        for ref, core in ((mine, c), (other, 1 - c)):
+            at = 2 * (p ^ k) + core
+            keys[at] = ref[k, :, 0:256]
+            values[at] = ref[k, :, 256:512]
+            if key_t is not None:
+                key_t[at] = jnp.transpose(ref[k, :, 0:256])[:192] * 0.125
+            if value_t is not None:
+                value_t[at] = jnp.transpose(ref[k, :, 256:512])[:192]
+
+
+def masked_heads(block):
+    lane = lax.broadcasted_iota(jnp.int32, (256, 128), 1)
+    zero = jnp.zeros((256, 128), block.dtype)
+    return (
+        jnp.where(lane < 64, block[:, 0:128], zero),
+        jnp.where(lane >= 64, block[:, 0:128], zero),
+        block[:, 128:256],
+    )
+
+
+GROUPS = (slice(0, 128), slice(0, 128), slice(128, 256))
+
+
+def attention_kernel(pos, nb, q, mine, other, a0, a1, a2, a3, ot, lse, keys, values, value_t):
     scale = 0.125 * LOG2E
-    absolute_kv(pos, mine, other, kv)
+    absolute_keys(pos, mine, other, keys, values, None, value_t)
     for k, out in enumerate((a0, a1, a2, a3)):
         low, high = key_range(pos, nb, k)
-        heads = [q[k, :, 64 * h : 64 * h + 64] for h in range(3)]
-
-        def step(kb, state):
+        heads = masked_heads(q[k])
+
+        def step(i, state):
+            kb = low + 2 * i
+            more = jnp.minimum(kb + 1, 7)
+            valid = kb + 1 < high
             new = []
+            scores = []
+            for h in range(3):
+                one = dot(keys[kb, :, GROUPS[h]], heads[h], NT)
+                two = dot(keys[more, :, GROUPS[h]], heads[h], NT)
+                scores.append((one, jnp.where(valid, two, NEG_LARGE)))
             for h in range(3):
                 top, total, acc = state[h]
-                keys = kv[kb, :, 64 * h : 64 * h + 64]
-                values = kv[kb, :, 192 + 64 * h : 256 + 64 * h]
-                scores = dot(keys, heads[h], NT)
-                next_top = jnp.maximum(top, jnp.max(scores, axis=0, keepdims=True))
-                weights = jnp.exp2((scores - next_top) * scale)
-                factor = jnp.exp2((top - next_top) * scale)
-                total = total * factor + jnp.sum(weights, axis=0, keepdims=True)
-                acc = acc * factor + dot(values, weights.astype(BF16), TN)
+                one, two = scores[h]
+                peak = jnp.max(jnp.maximum(one, two), axis=0, keepdims=True)
+                next_top = jnp.maximum(top, peak * scale)
+                one = jnp.exp2(one * scale - next_top)
+                two = jnp.exp2(two * scale - next_top)
+                factor = jnp.exp2(top - next_top)
+                total = total * factor + jnp.sum(one + two, axis=0, keepdims=True)
+                at = slice(64 * h, 64 * h + 64)
+                acc = acc * factor + (
+                    dot(value_t[kb, at, :], one.astype(BF16))
+                    + dot(value_t[more, at, :], two.astype(BF16))
+                )
                 new.append((next_top, total, acc))
             return tuple(new)
 
@@ -181,46 +242,55 @@
             (jnp.full((1, BLK), NEG_LARGE, F32), jnp.zeros((1, BLK), F32), jnp.zeros((HDIM, BLK), F32))
             for _ in range(3)
         )
-        state = lax.fori_loop(low, high, step, start)
+        state = lax.fori_loop(0, (high - low + 1) >> 1, step, start)
         done = []
         for h in range(3):
             top, total, acc = state[h]
             mixed = acc / total
             ot[k, 64 * h : 64 * h + 64, :] = mixed
-            lse[k, h : h + 1, :] = top * scale + jnp.log(total) * LOG2E
+            lse[k, h : h + 1, :] = top + jnp.log(total) * LOG2E
             done.append(mixed)
         out[...] = jnp.transpose(jnp.concatenate(done, axis=0)).astype(BF16)
 
 
 def attention_back_kernel(
-    pos, nb, q, mine, other, g0, g1, g2, g3, ot, lse, dq, dmine, dother, kv, dkv
+    pos, nb, q, mine, other, g0, g1, g2, g3, ot, lse, dq, dmine, dother, keys, values, key_t, dk, dv
 ):
     z, p, c = place(pos)
     scale = 0.125 * LOG2E
-    absolute_kv(pos, mine, other, kv)
-    dkv[...] = jnp.zeros(dkv.shape, F32)
+    absolute_keys(pos, mine, other, keys, values, key_t, None)
+    dk[...] = jnp.zeros(dk.shape, F32)
+    dv[...] = jnp.zeros(dv.shape, F32)
     for k, grad in enumerate((g0, g1, g2, g3)):
         low, high = key_range(pos, nb, k)
-        heads = [q[k, :, 64 * h : 64 * h + 64] for h in range(3)]
-        grads = [grad[:, 64 * h : 64 * h + 64] for h in range(3)]
+        heads = masked_heads(q[k])
+        padded = jnp.concatenate([grad[...], jnp.zeros((256, 64), BF16)], axis=1)
+        grads = masked_heads(padded)
         flipped = jnp.transpose(grad[...].astype(F32))
         product = flipped * ot[k]
         deltas = [
             jnp.sum(product[64 * h : 64 * h + 64], axis=0, keepdims=True) for h in range(3)
         ]
         logs = [lse[k, h : h + 1, :] for h in range(3)]
+        pair_q = jnp.concatenate([heads[0], heads[1]], axis=0) * 0.125
+        small_q = heads[2] * 0.125
+        pair_g = jnp.concatenate([grads[0], grads[1]], axis=0)
 
         def step(kb, state):
-            new = []
+            new, probs_low, scores_low = [], [], []
             for h in range(3):
-                keys = kv[kb, :, 64 * h : 64 * h + 64]
-                values = kv[kb, :, 192 + 64 * h : 256 + 64 * h]
-                probs = jnp.exp2(dot(keys, heads[h], NT) * scale - logs[h])
-                dprobs = dot(values, grads[h], NT)
-                low_scores = (probs * (dprobs - deltas[h]) * 0.125).astype(BF16)
-                dkv[h, kb] += dot(low_scores, heads[h])
-                dkv[3 + h, kb] += dot(probs.astype(BF16), grads[h])
-                new.append(state[h] + dot(keys, low_scores, TN))
+                probs = jnp.exp2(dot(keys[kb, :, GROUPS[h]], heads[h], NT) * scale - logs[h])
+                dprobs = dot(values[kb, :, GROUPS[h]], grads[h], NT)
+                probs_low.append(probs.astype(BF16))
+                scores_low.append((probs * (dprobs - deltas[h])).astype(BF16))
+            for h in range(3):
+                new.append(state[h] + dot(key_t[kb, 64 * h : 64 * h + 64, :], scores_low[h]))
+            for ref, lows, pair, one in (
+                (dk, scores_low, pair_q, small_q),
+                (dv, probs_low, pair_g, grads[2]),
+            ):
+                ref[kb, :, 0:128] += dot(jnp.concatenate(lows[:2], axis=1), pair)
+                ref[kb, :, 128:256] += dot(lows[2], one)
             return tuple(new)
 
         state = lax.fori_loop(
@@ -228,9 +298,9 @@
         )
         dq[k] = jnp.transpose(jnp.concatenate(state, axis=0))
     for k in range(4):
-        first = 2 * (p ^ k)
-        dmine[k] = jnp.concatenate([dkv[i, first + c] for i in range(6)], axis=1)
-        dother[k] = jnp.concatenate([dkv[i, first + 1 - c] for i in range(6)], axis=1).astype(BF16)
+        at = 2 * (p ^ k)
+        dmine[k] = jnp.concatenate([dk[at + c], dv[at + c]], axis=1)
+        dother[k] = jnp.concatenate([dk[at + 1 - c], dv[at + 1 - c]], axis=1).astype(BF16)
 
 
 def norm_kernel(pos, tokens, a0, a1, a2, a3, wo, vecs, low, xhat, rstd):
@@ -258,14 +328,12 @@
     return jnp.sum(values, axis=0, keepdims=True)
 
 
-def norm_two_kernel(vecs, xhat, own, r1, r2, r3, cot, block_out, low, grad_two, sums):
+def norm_two_kernel(vecs, xhat, own, r1, cot, block_out, low, grad_two, sums):
     acc = [jnp.zeros((1, 768), F32) for _ in range(3)]
     for i in range(8):
         at = slice(32 * i, 32 * i + 32)
         hidden = xhat[at, :] * vecs[3:4, :] + vecs[5:6, :]
-        resid = hidden + own[at, :] + vecs[7:8, :]
-        for r in (r1, r2, r3):
-            resid += r[at, :].astype(F32)
+        resid = hidden + own[at, :] + r1[at, :].astype(F32) + vecs[7:8, :]
         center = resid - jnp.mean(resid, axis=-1, keepdims=True)
         scale = lax.rsqrt(jnp.mean(center * center, axis=-1, keepdims=True) + EPSILON)
         hat = center * scale
@@ -279,15 +347,13 @@
 
 
 def norm_one_kernel(
-    pos, own, r1, r2, r3, grad_two, xhat, rstd, vecs, wo, o0, o1, o2, o3, low, grad_one, sums
+    pos, own, r1, grad_two, xhat, rstd, vecs, wo, o0, o1, o2, o3, low, grad_one, sums
 ):
     z, p, c = place(pos)
     acc = [jnp.zeros((1, 768), F32) for _ in range(3)]
     for i in range(8):
         at = slice(32 * i, 32 * i + 32)
-        grad = own[at, :] + grad_two[at, :]
-        for r in (r1, r2, r3):
-            grad += r[at, :].astype(F32)
+        grad = own[at, :] + grad_two[at, :] + r1[at, :].astype(F32)
         hat = xhat[at, :]
         back = norm_grad(grad, vecs[3:4, :], hat, rstd[at, :])
         grad_one[at, :] = back
@@ -299,47 +365,29 @@
         out[...] = dot(low[...], wo[pl.ds(row_of(start, 64), 192), :], NT).astype(BF16)
 
 
-def ff_kernel(count):
-    def kernel(*refs):
-        hs = refs[:count]
-        wi, wx, bias = refs[count : count + 3]
-        outs = refs[count + 3 :]
-        for i, h in enumerate(hs):
-            part, act, slope = outs[3 * i : 3 * i + 3]
-            acc = jnp.zeros((256, 768), F32)
-            for f in range(3):
-                at = slice(256 * f, 256 * f + 256)
-                u = dot(h[...], wi[:, at]) + bias[1:2, at]
-                cdf = 0.5 * (1.0 + lax.erf(u * 0.7071067811865476))
-                low = (u * cdf).astype(BF16)
-                act[:, at] = low
-                slope[:, at] = cdf + u * jnp.exp2(u * u * (-0.5 * LOG2E)) * 0.3989422804014327
-                acc += dot(low, wx[at, :768])
-            part[...] = acc.astype(part.dtype)
-
-    return kernel
-
-
-def ff_back_kernel(count):
-    def kernel(*refs):
-        gs = refs[:count]
-        slopes = refs[count : 2 * count]
-        wi, wx = refs[2 * count : 2 * count + 2]
-        sums = refs[2 * count + 2]
-        outs = refs[2 * count + 3 :]
-        for f in range(3):
-            at = slice(256 * f, 256 * f + 256)
-            acc = jnp.zeros((1, 256), F32)
-            for i in range(count):
-                pre = dot(gs[i][...], wx[at, :768], NT) * slopes[i][:, at]
-                outs[2 * i + 1][:, at] = pre.astype(BF16)
-                acc += total(pre)
-            sums[:, at] = jnp.broadcast_to(acc, (8, 256))
-        for i in range(count):
-            back = dot(outs[2 * i + 1][...], wi[...], NT)
-            outs[2 * i][...] = back.astype(outs[2 * i].dtype)
-
-    return kernel
+def ff_kernel(h, wi, wx, bias, part, act, slope):
+    acc = jnp.zeros((256, 768), F32)
+    for f in range(6):
+        at = slice(256 * f, 256 * f + 256)
+        u = dot(h[...], wi[:, at]) + bias[1:2, at]
+        cdf = 0.5 * (1.0 + lax.erf(u * 0.7071067811865476))
+        low = (u * cdf).astype(BF16)
+        act[:, at] = low
+        slope[:, at] = cdf + u * jnp.exp2(u * u * (-0.5 * LOG2E)) * 0.3989422804014327
+        acc += dot(low, wx[at, :768])
+    part[...] = acc.astype(part.dtype)
+
+
+def ff_back_kernel(g, slope, wi, wx, back, pre_low, sums):
+    acc = jnp.zeros((256, 768), F32)
+    for f in range(6):
+        at = slice(256 * f, 256 * f + 256)
+        pre = dot(g[...], wx[at, :768], NT) * slope[:, at]
+        low = pre.astype(BF16)
+        pre_low[:, at] = low
+        sums[:, at] = jnp.broadcast_to(total(pre), (8, 256))
+        acc += dot(low, wi[:, at], NT)
+    back[...] = acc.astype(back.dtype)
 
 
 def column_of(row):
@@ -348,22 +396,25 @@
     return jnp.transpose(jnp.where(first, jnp.broadcast_to(row, (128, n)), 0.0))
 
 
-def ff_grad_kernel(*refs):
-    pos = refs[0]
-    hs, pres, acts, gs = refs[1:5], refs[5:9], refs[9:13], refs[13:17]
-    sum_a, sum_b = refs[17:19]
-    keep, send, gi, go = refs[19:]
-    z, p, c = place(pos)
-    gi[...] = sum(dot(hs[k][...], pres[k][...], TN) for k in range(4))
-    go[:, :768] = sum(dot(acts[k][...], gs[k][...], TN) for k in range(4))
+def ff_grad_out_kernel(pos, a0, a1, g0, g1, sum_a, sum_b, keep, send, go):
+    z, p, c = place(pos)
+    go[:, :768] = dot(a0[...], g0[...], TN) + dot(a1[...], g1[...], TN)
     go[:, 768:] = column_of(sum_a[0:1, :] + sum_b[0:1, :])
-    for j in range(4):
-        for out, core in ((keep, c), (send, 1 - c)):
-            for k in range(4):
-                start = ((z ^ j) * 4 + (p ^ k)) * 48 + core * 24
-                out[j, 24 * k : 24 * k + 24, 0:768] = gi[pl.ds(row_of(start), 24), :].astype(BF16)
-            start = (z ^ j) * 192 + core * 96
-            out[j, :, 768:1664] = go[pl.ds(row_of(start), 96), :].astype(BF16)
+    for k in range(4):
+        for i in range(2):
+            for out, core in ((keep, c), (send, 1 - c)):
+                start = (((z ^ (2 * i)) >> 1) * 4 + (p ^ k)) * 192 + core * 96
+                out[k, 96 * i : 96 * i + 96, :] = go[pl.ds(row_of(start), 96), :].astype(BF16)
+
+
+def ff_grad_in_kernel(pos, h0, h1, b0, b1, keep, send, gi):
+    z, p, c = place(pos)
+    gi[...] = dot(h0[...], b0[...], TN) + dot(h1[...], b1[...], TN)
+    for k in range(4):
+        for i in range(4):
+            for out, core in ((keep, c), (send, 1 - c)):
+                start = (4 * (z ^ SLOTS[i]) + (p ^ k)) * 48 + core * 24
+                out[k, 24 * i : 24 * i + 24, :] = gi[pl.ds(row_of(start), 24), :].astype(BF16)
 
 
 def wo_grad_kernel(pos, a0, a1, a2, a3, low, sum_one, sum_two, keep, send, acc):
@@ -387,21 +438,34 @@
     for k in range(4):
         for j in range(4):
             for out, core in ((keep, c), (send, 1 - c)):
-                start = ((z ^ j) * 4 + (p ^ k)) * 48 + core * 24
+                start = (4 * (z ^ SLOTS[j]) + (p ^ k)) * 48 + core * 24
                 out[k, 24 * j : 24 * j + 24, :] = acc[pl.ds(row_of(start), 24), :].astype(BF16)
 
 
-def qkv_back_kernel(dq, dmine, dother, wq, i0, i1, i2, i3, low, sums):
+def qkv_back_kernel(dq, dmine, dother, wq, i0, mx, my, rest, low, sums):
     bias_q = jnp.zeros((1, 192), F32)
     bias_v = jnp.zeros((1, 192), F32)
-    for k, out in enumerate((i0, i1, i2, i3)):
+    for k in range(4):
         grad_q = dq[k]
         grad_kv = dmine[k] + dother[k].astype(F32)
+        grad_v = grad_kv[:, 256:448]
         bias_q += total(grad_q)
-        bias_v += total(grad_kv[:, 192:])
-        whole = jnp.concatenate([grad_q, grad_kv, jnp.zeros((256, 64), F32)], axis=1).astype(BF16)
+        bias_v += total(grad_v)
+        parts = [grad_q, grad_kv[:, :192], grad_v, jnp.zeros((256, 64), F32)]
+        whole = jnp.concatenate(parts, axis=1).astype(BF16)
         low[k] = whole
-        out[...] = dot(whole, wq[...], NT).astype(out.dtype)
+        part = dot(whole, wq[...], NT)
+        if k == 0:
+            i0[...] = part
+        elif k == 1:
+            mx[0:128, :] = part[:128].astype(BF16)
+            rest[1] = part[128:].astype(BF16)
+        elif k == 2:
+            my[0:128, :] = part[128:].astype(BF16)
+            rest[0] = part[:128].astype(BF16)
+        else:
+            mx[128:256, :] = part[:128].astype(BF16)
+            my[128:256, :] = part[128:].astype(BF16)
     sums[...] = jnp.concatenate(
         [
             jnp.concatenate([bias_q, jnp.zeros((1, 64), F32)], axis=1),
@@ -424,7 +488,7 @@
     for j in range(4):
         for k in range(4):
             for out, core in ((keep, c), (send, 1 - c)):
-                start = ((z ^ j) * 4 + (p ^ k)) * 48 + core * 24
+                start = (4 * (z ^ j) + (p ^ k)) * 48 + core * 24
                 out[j, 24 * k : 24 * k + 24, :] = acc[pl.ds(row_of(start), 24), :].astype(BF16)
 
 
@@ -434,39 +498,38 @@
 
 
 def finish_kernel(
-    pos, tq, tm, f1, f2, f3, uo, gqkv, gbqv, gwo, gbo, gain, shift, gwin, gbin, gwout, gbout
+    pos, tq, f1, f2, f3, ti, tw, gqkv, gbqv, gwo, gbo, gain, shift, gwin, gbin, gwout, gbout
 ):
     z, p, c = place(pos)
-    gwout[...] = tm[:, 768:1536]
-    gbin[...] = turned(tm[:, 1536:1664])[0:1, 0:96]
-    gwo[...] = uo[:, 0:768]
-    side = turned(uo[:, 768:896])
+    gwout[...] = tw[:, 0:768]
+    gbin[...] = turned(tw[:, 768:896])[0:1, 0:96]
+    gwo[...] = ti[:, 3072:3840]
+    side = turned(ti[:, 3840:3968])
     gbo[...] = side[0:1, 0:24]
     gain[...] = side[1:3, 0:24]
     shift[...] = side[3:5, 0:24]
     gbout[...] = side[5:6, 0:24]
-    for own in range(4):
-
-        @pl.when(p == own)
-        def _(own=own):
-            biases = jnp.zeros((24, 128), F32)
-            for k in range(4):
-                chip = own ^ k
-                if k == 0:
-                    qkv, win = tq[0:24, :], tm[0:24, 0:768]
-                else:
-                    got = (f1, f2, f3)[k - 1][...].astype(F32)
-                    qkv, win = got[:, 0:640], got[:, 640:1408]
-                for i in range(3):
-                    gqkv[:, 768 * i + 192 * chip : 768 * i + 192 * chip + 192] = qkv[
-                        :, 192 * i : 192 * i + 192
-                    ]
-                for i in range(4):
-                    gwin[:, 768 * i + 192 * chip : 768 * i + 192 * chip + 192] = win[
-                        :, 192 * i : 192 * i + 192
-                    ]
-                biases += jnp.where(z == chip, qkv[:, 512:640], 0.0)
-            gbqv[...] = turned(biases)[64:66, 0:24]
+
+    def run(own):
+        biases = jnp.zeros((24, 128), F32)
+        for k in range(4):
+            chip = own ^ k
+            qkv = tq[0:24, :] if k == 0 else (f1, f2, f3)[k - 1][...].astype(F32)
+            for i in range(3):
+                at = 768 * i + 192 * chip
+                gqkv[:, at : at + 192] = qkv[:, 192 * i : 192 * i + 192]
+            biases += jnp.where(z == chip, qkv[:, 512:640], 0.0)
+        gbqv[...] = turned(biases)[64:66, 0:24]
+
+    each_chip(p, run)
+    for side in range(2):
+
+        @pl.when((z & 1) == side)
+        def _(side=side):
+            for t in range(2):
+                for i in range(2):
+                    at = 768 * (side ^ t) + 1536 * i
+                    gwin[:, at : at + 768] = ti[:, 1536 * t + 768 * i : 1536 * t + 768 * i + 768]
 
 
 def chip_swap(value, k):
@@ -477,8 +540,16 @@
     return lax.ppermute(value, "seq", [(s, s ^ 1) for s in range(8)])
 
 
+def z_trade(value):
+    return lax.all_to_all(value, "dp", 0, 0, tiled=True)
+
+
 def z_swap(value, j):
-    return lax.ppermute(value, "dp", [(s, s ^ j) for s in range(4)])
+    return lax.ppermute(value, "dp", [(i, i ^ j) for i in range(4)])
+
+
+def after(value, *others):
+    return lax.optimization_barrier((value, *others))[0]
 
 
 def low_add(*terms):
@@ -502,42 +573,44 @@
 ):
     pos = lax.axis_index(("dp", "seq")).astype(jnp.int32).reshape(1)
     others = (1, 2, 3)
-    narrow = jnp.concatenate(
-        [
-            bias_qv,
-            bias_o[None],
-            ln_gain,
-            ln_bias,
-            bias_out[None],
-            doc_ids[None, :24].astype(BF16),
-        ],
-        axis=0,
-    )
-    smalls = jnp.concatenate(
-        [
-            jnp.pad(narrow, ((0, 0), (0, 72))),
-            bias_in[None],
-            jnp.zeros((6, 96), BF16),
-        ],
-        axis=0,
-    )
-    p0, p1, p2, p3, wx_own = call(
+    smalls = sum(
+        jnp.pad(v, ((at, 16 - at - v.shape[0]), (0, 96 - v.shape[1])))
+        for v, at in (
+            (bias_qv, 0),
+            (bias_o[None], 2),
+            (ln_gain, 3),
+            (ln_bias, 5),
+            (bias_out[None], 7),
+            (doc_ids[None, :24].astype(BF16), 8),
+            (bias_in[None], 9),
+        )
+    )
+    x1, x2, x3 = (chip_swap(tokens, k) for k in others)
+    zq, zw = call(
         pack_kernel,
-        (pos, w_qkv, w_in, w_out, smalls),
-        [sds((24, 1408), BF16)] * 4 + [sds((96, 896), BF16)],
+        (w_qkv, w_o, w_out, smalls),
+        [sds((24, 3200), BF16), sds((96, 896), BF16)],
+        smem_in=(),
         name="pack",
     )
-    got = [p0] + [chip_swap(v, k) for v, k in zip((p1, p2, p3), others)]
-    xs = [tokens] + [chip_swap(tokens, k) for k in others]
-    first = jnp.concatenate([g[:, :640] for g in got], axis=0)
-    first_all = jnp.stack([first] + [z_swap(first, j) for j in others])
-    first_other = core_swap(first_all)
-    wo_z = jnp.concatenate([w_o] + [z_swap(w_o, j) for j in others], axis=0)
-    bulk = jnp.concatenate(
-        [jnp.concatenate([g[:, 640:] for g in got], axis=0), wx_own], axis=1
-    )
-    bulk_all = jnp.stack([bulk] + [z_swap(bulk, j) for j in others])
-    bulk_other = core_swap(bulk_all)
+    zqs = (zq,) + lax.optimization_barrier((*[z_swap(zq, j) for j in others], x1, x2))[:3]
+    xs = (tokens, x1, x2, x3)
+    *pieces_q, wo_z = call(
+        split_qkv_kernel,
+        (pos, *zqs),
+        [sds((96, 640), BF16)] * 4 + [sds((96, 768), BF16)],
+        name="split_qkv",
+    )
+    first_all = jnp.stack([pieces_q[0]] + [chip_swap(pieces_q[k], k) for k in others])
+    first_other = core_swap(after(first_all, x3))
+    zi_one = z_swap(after(w_in, *zqs[1:]), 2)
+    zw_one = z_swap(after(zw, *zqs[1:]), 2)
+    zi_mine, zi_theirs = call(
+        split_in_kernel, (pos, w_in, zi_one), [sds((48, 1536), BF16)] * 2, name="split_in"
+    )
+    zi_two = z_swap(zi_theirs, 1)
+    zw_pair = jnp.concatenate([zw, zw_one], axis=0)
+    wo_z = after(wo_z, first_all)
     wo_all = jnp.stack([wo_z] + [chip_swap(wo_z, k) for k in others])
     wo_other = core_swap(wo_all)
 
@@ -545,103 +618,117 @@
         qkv_kernel,
         (pos, first_all, first_other, *xs),
         [
-            sds((4, 256, 192), BF16),
-            sds((4, 256, 384), BF16),
+            sds((4, 256, 256), BF16),
+            sds((4, 256, 512), BF16),
             sds((768, 640), BF16),
             sds((16, 768), F32),
             sds((1,), jnp.int32),
         ],
         scratch=[pltpu.VMEM((8, 640), F32)],
         smem_out=(4,),
-        flops=2 * 1024 * 768 * 640,
         name="qkv",
     )
-    kv_other = core_swap(kv)
+    kv_other = after(core_swap(kv), zw_pair, zi_theirs)
+    out_two = chip_swap(zw_pair, 2)
     *attended, ot, lse = call(
         attention_kernel,
         (pos, nb, q, kv, kv_other),
         [sds((256, 192), BF16)] * 4 + [sds((4, 192, 256), F32), sds((4, 8, 256), F32)],
-        scratch=[pltpu.VMEM((8, 256, 384), BF16)],
+        scratch=[pltpu.VMEM((8, 256, 256), BF16)] * 2 + [pltpu.VMEM((8, 192, 256), BF16)],
         smem_in=(0, 1),
-        flops=6e9,
+        flops=1e10,
         name="attention",
     )
+    attended = lax.optimization_barrier((*attended, wo_other, zi_two))[:4]
     pieces = [attended[0]] + [chip_swap(attended[k], k) for k in others]
-    (wo,) = call(wo_kernel, (pos, wo_all, wo_other), [sds((768, 768), BF16)], name="join_wo")
+    (wo,) = call(join_wo_kernel, (pos, wo_all, wo_other), [sds((768, 768), BF16)], name="join_wo")
     hidden, xhat, rstd = call(
         norm_kernel,
         (pos, tokens, *pieces, wo, vecs),
         [sds((256, 768), BF16), sds((256, 768), F32), sds((256, 1), F32)],
-        flops=2 * 256 * 768 * 768,
         name="norm_one",
     )
-    hs = [hidden] + [chip_swap(hidden, k) for k in others]
-    wi, wx, bin_ = call(
-        weights_kernel,
-        (pos, bulk_all, bulk_other),
-        [sds((768, 768), BF16), sds((768, 896), BF16), sds((8, 768), F32)],
-        name="join_ff",
-    )
-
-    def ff(blocks, dtype):
-        per = [sds((256, 768), dtype), sds((256, 768), BF16), sds((256, 768), F32)]
-        out = call(
-            ff_kernel(len(blocks)),
-            (*blocks, wi, wx, bin_),
-            per * len(blocks),
+    hs = (hidden, z_swap(hidden, 1))
+    out_half = after(jnp.stack([zw_pair, out_two]), pieces[1])
+    out_all = jnp.concatenate([out_half, chip_swap(out_half, 1)])
+    out_other = core_swap(out_all)
+    in_one = after(jnp.concatenate([zi_mine, zi_two], axis=0), pieces[1])
+    in_half = jnp.stack([in_one, chip_swap(in_one, 1)])
+    in_all = jnp.concatenate([in_half, chip_swap(in_half, 2)])
+    in_other = core_swap(in_all)
+    (wi,) = call(join_in_kernel, (pos, in_all, in_other), [sds((768, 1536), BF16)], name="join_in")
+    wx, bin_ = call(
+        join_out_kernel,
+        (pos, out_all, out_other),
+        [sds((1536, 896), BF16), sds((8, 1536), F32)],
+        name="join_out",
+    )
+
+    def ff(block, dtype):
+        return call(
+            ff_kernel,
+            (block, wi, wx, bin_),
+            [sds((256, 768), dtype), sds((256, 1536), BF16), sds((256, 1536), F32)],
             smem_in=(),
-            flops=len(blocks) * 4 * 256 * 768 * 768,
-            name="ff",
+                name="ff",
         )
-        return [out[3 * i : 3 * i + 3] for i in range(len(blocks))]
-
-    made = ff(hs[:1], F32) + ff(hs[1:], BF16)
-    parts = [made[0][0]] + [chip_swap(made[k][0], k) for k in others]
+
+    part_own, act_own, slope_own = ff(hs[0], F32)
+    part_far, act_far, slope_far = ff(after(hs[1], part_own), BF16)
     block_out, grad_two_low, grad_two, sums_two = call(
         norm_two_kernel,
-        (vecs, xhat, *parts, cotangent),
+        (vecs, xhat, part_own, z_swap(part_far, 1), cotangent),
         [sds((256, 768), BF16), sds((256, 768), BF16), sds((256, 768), F32), sds((8, 768), F32)],
         smem_in=(),
-        flops=1e7,
         name="norm_two",
     )
-    gs = [grad_two_low] + [chip_swap(grad_two_low, k) for k in others]
-
-    def ff_back(blocks, slopes, dtype):
-        n = len(blocks)
-        out = call(
-            ff_back_kernel(n),
-            (*blocks, *slopes, wi, wx),
-            [sds((8, 768), F32)] + [sds((256, 768), dtype), sds((256, 768), BF16)] * n,
+    gs = (grad_two_low, z_swap(grad_two_low, 1))
+
+    def ff_back(block, slope, dtype):
+        return call(
+            ff_back_kernel,
+            (block, slope, wi, wx),
+            [sds((256, 768), dtype), sds((256, 1536), BF16), sds((8, 1536), F32)],
             smem_in=(),
-            flops=n * 4 * 256 * 768 * 768,
-            name="ff_back",
+                name="ff_back",
         )
-        return out[0], [out[1 + 2 * i : 3 + 2 * i] for i in range(n)]
-
-    sum_a, back_a = ff_back(gs[:1], [made[0][2]], F32)
-    sum_b, back_b = ff_back(gs[1:], [m[2] for m in made[1:]], BF16)
-    backs = back_a + back_b
-    grad_parts = [backs[0][0]] + [chip_swap(backs[k][0], k) for k in others]
-    ff_keep, ff_send = call(
-        ff_grad_kernel,
-        (pos, *hs, *[b[1] for b in backs], *[m[1] for m in made], *gs, sum_a, sum_b),
-        [sds((4, 96, 1664), BF16)] * 2,
-        scratch=[pltpu.VMEM((768, 768), F32), pltpu.VMEM((768, 896), F32)],
-        flops=16 * 256 * 768 * 768,
-        name="ff_grad",
-    )
-    ff_got = core_swap(ff_send)
-    ff_sum = [low_add(ff_keep[j], ff_got[j]) for j in range(4)]
-    ff_z = [z_swap(ff_sum[j].astype(BF16), j) for j in others]
-    tm = low_add(ff_sum[0], *ff_z)
+
+    back_own, pre_own, sum_own = ff_back(gs[0], slope_own, F32)
+    back_far, pre_far, sum_far = ff_back(after(gs[1], back_own), slope_far, BF16)
+    back_got = z_swap(back_far, 1)
+    out_keep, out_send = call(
+        ff_grad_out_kernel,
+        (pos, act_own, act_far, *gs, sum_own, sum_far),
+        [sds((4, 192, 896), BF16)] * 2,
+        scratch=[pltpu.VMEM((1536, 896), F32)],
+        name="ff_grad_out",
+    )
+    in_keep, in_send = call(
+        ff_grad_in_kernel,
+        (pos, *hs, pre_own, pre_far),
+        [sds((4, 96, 1536), BF16)] * 2,
+        scratch=[pltpu.VMEM((768, 1536), F32)],
+        name="ff_grad_in",
+    )
+    out_got, in_got = core_swap(out_send), core_swap(in_send)
+    out_sum = low_add(out_keep, out_got)
+    out_send = out_sum[1::2].astype(BF16)
+    out_part = chip_swap(out_send, 1)
+    out_left = low_add(out_sum[2], out_part[1]).astype(BF16)
+    out_mine = low_add(out_sum[0], out_part[0], chip_swap(out_left, 2))
+    tw = low_add(out_mine[:96], z_swap(out_mine[96:].astype(BF16), 2))
+    in_sum = low_add(in_keep, in_got)
+    in_send_two = in_sum[2:].astype(BF16)
+    in_part = chip_swap(in_send_two, 2)
+    in_left = low_add(in_sum[1], in_part[1]).astype(BF16)
+    in_mine = low_add(in_sum[0], in_part[0], chip_swap(in_left, 1))
+    back_got = after(back_got, out_send, in_send_two)
 
     *grad_att, low_one, grad_one, sums_one = call(
         norm_one_kernel,
-        (pos, *grad_parts, grad_two, xhat, rstd, vecs, wo),
+        (pos, back_own, back_got, grad_two, xhat, rstd, vecs, wo),
         [sds((256, 192), BF16)] * 4
         + [sds((256, 768), BF16), sds((256, 768), F32), sds((8, 768), F32)],
-        flops=2 * 256 * 768 * 768,
         name="norm_one_back",
     )
     grad_pieces = [grad_att[0]] + [chip_swap(grad_att[k], k) for k in others]
@@ -650,61 +737,69 @@
         (pos, *pieces, low_one, sums_one, sums_two),
         [sds((4, 96, 896), BF16)] * 2,
         scratch=[pltpu.VMEM((768, 896), F32)],
-        flops=2 * 256 * 768 * 768,
         name="wo_grad",
     )
     wo_got = core_swap(wo_send)
-    wo_sum = [low_add(wo_keep[k], wo_got[k]) for k in range(4)]
-    to = low_add(wo_sum[0], *[chip_swap(wo_sum[k].astype(BF16), k) for k in others])
-    uo = low_add(
-        to[:24], *[z_swap(to[24 * j : 24 * j + 24].astype(BF16), j) for j in others]
-    )
+    wo_sum = low_add(wo_keep, wo_got)
+    wo_low = [wo_sum[k].astype(BF16) for k in others]
+    wo_part = [chip_swap(v, k) for v, k in zip(wo_low, others)]
+    zi_sum = jnp.concatenate([in_mine, low_add(wo_sum[0], *wo_part)], axis=1)
+    zi_got = z_swap(zi_sum[48:].astype(BF16), 1)
+    zi_half = jnp.concatenate(
+        [
+            zi_sum[:48, :1536],
+            zi_got[:, :1536].astype(F32),
+            low_add(zi_sum[:48, 1536:], zi_got[:, 1536:]),
+        ],
+        axis=1,
+    )
+    ti = low_add(zi_half[:24], z_swap(zi_half[24:].astype(BF16), 2))
+    grad_pieces = lax.optimization_barrier((*grad_pieces, *wo_low, out_left, in_left))[:4]
 
     dq, dmine, dother = call(
         attention_back_kernel,
         (pos, nb, q, kv, kv_other, *grad_pieces, ot, lse),
-        [sds((4, 256, 192), F32), sds((4, 256, 384), F32), sds((4, 256, 384), BF16)],
-        scratch=[pltpu.VMEM((8, 256, 384), BF16), pltpu.VMEM((6, 8, 256, 64), F32)],
+        [sds((4, 256, 192), F32), sds((4, 256, 512), F32), sds((4, 256, 512), BF16)],
+        scratch=[pltpu.VMEM((8, 256, 256), BF16)] * 2
+        + [pltpu.VMEM((8, 192, 256), BF16)]
+        + [pltpu.VMEM((8, 256, 256), F32)] * 2,
         smem_in=(0, 1),
-        flops=15e9,
+        flops=1e10,
         name="attention_back",
     )
     dgot = core_swap(dother)
-    *in_parts, low, sums_qv = call(
+    in_own, in_x, in_y, in_rest, low, sums_qv = call(
         qkv_back_kernel,
         (dq, dmine, dgot, wq),
         [sds((256, 768), F32)]
-        + [sds((256, 768), BF16)] * 3
-        + [sds((4, 256, 640), BF16), sds((8, 256), F32)],
+        + [sds((256, 768), BF16)] * 2
+        + [sds((2, 128, 768), BF16), sds((4, 256, 640), BF16), sds((8, 256), F32)],
         smem_in=(),
-        flops=2 * 1024 * 768 * 640,
         name="qkv_back",
     )
-    in_got = [chip_swap(in_parts[k], k) for k in others]
-    input_grad = low_add(in_parts[0], grad_one, *in_got)
     q_keep, q_send = call(
         qkv_grad_kernel,
         (pos, *xs, low, sums_qv),
         [sds((4, 96, 640), BF16)] * 2,
         scratch=[pltpu.VMEM((768, 640), F32)],
-        flops=2 * 1024 * 768 * 640,
         name="qkv_grad",
     )
     q_got = core_swap(q_send)
-    q_sum = [low_add(q_keep[j], q_got[j]) for j in range(4)]
+    q_sum = [low_add(q_keep[i], q_got[i]) for i in range(4)]
     tq = low_add(q_sum[0], *[z_swap(q_sum[j].astype(BF16), j) for j in others])
-    final = [
-        chip_swap(
-            jnp.concatenate(
-                [tq[24 * k : 24 * k + 24], tm[24 * k : 24 * k + 24, :768]], axis=1
-            ).astype(BF16),
-            k,
-        )
-        for k in others
-    ]
+    got_x, got_y = chip_swap(in_x, 1), chip_swap(in_y, 2)
+    last_y = chip_swap(low_add(in_rest[0], got_x[128:]).astype(BF16), 2)
+    last_x = chip_swap(low_add(in_rest[1], got_y[128:]).astype(BF16), 1)
+    input_grad = low_add(
+        in_own,
+        grad_one,
+        jnp.concatenate([got_x[:128], got_y[:128]], axis=0),
+        jnp.concatenate([last_y, last_x], axis=0),
+    )
+    final = [chip_swap(tq[24 * k : 24 * k + 24].astype(BF16), k) for k in others]
     gqkv, gbqv, gwo, gbo, gain, shift, gwin, gbin, gwout, gbout = call(
         finish_kernel,
-        (pos, tq, tm, *final, uo),
+        (pos, tq, *final, ti, tw),
         [
             sds((24, 2304), F32),
             sds((2, 24), F32),

time: 264 us -> 232 us (0.88)
  waiting for transfers between devices: 131 us -> 101 us
    ppermute x36 -> x33, waiting for transfers between devices: 89.7 us -> 42.7 us  [chip_swap(): return lax.ppermute(value, 'seq', [(s, s ^ 2 * k) for s in range(8)])]
    ppermute x18 -> x16, waiting for transfers between devices: 41 us -> 56.4 us  [z_swap(): return lax.ppermute(value, 'dp', [(i, i ^ j) for i in range(4)])]
    ppermute x18 -> x16, starting transfers between devices: 34.9 us -> 24.4 us  [z_swap(): return lax.ppermute(value, 'dp', [(i, i ^ j) for i in range(4)])]
    ppermute x36 -> x33, starting transfers between devices: 43.9 us -> 51.1 us  [chip_swap(): return lax.ppermute(value, 'seq', [(s, s ^ 2 * k) for s in range(8)])]
    pallas_call x18 -> x22, Pallas kernels: 43.7 us -> 43.2 us  [call(): pl.pallas_call(kernel, out_shape=tuple(outs), in_specs=[space(i in smem_i...]
  transfers between devices with their start and end apart: 62 -> 59, of which waited for: 31 -> 27; matrix products, arithmetic and copies ran while one was open for 1% -> 2% of each run, Pallas kernels for 13% -> 14%
where the time goes in v3:
time: 232 us
  waiting for transfers between devices  101 us (44%)
  starting transfers between devices  78.8 us (34%)
  Pallas kernels  43.2 us (19%)
  other arithmetic  4.74 us (2%)
  local copies, waits for them, and re-layouts  3.04 us (1%)
    ppermute x16, waiting for transfers between devices, z_swap(): return lax.ppermute(value, 'dp', [(i, i ^ j) for i in range(4)])  56.4 us
    ppermute x33, starting transfers between devices, chip_swap(): return lax.ppermute(value, 'seq', [(s, s ^ 2 * k) for s in range(8)])  51.1 us
    pallas_call x22, Pallas kernels, call(): pl.pallas_call(kernel, out_shape=tuple(outs), in_specs=[space(i in smem_i...  43.2 us
    ppermute x33, waiting for transfers between devices, chip_swap(): return lax.ppermute(value, 'seq', [(s, s ^ 2 * k) for s in range(8)])  42.7 us
    ppermute x16, starting transfers between devices, z_swap(): return lax.ppermute(value, 'dp', [(i, i ^ j) for i in range(4)])  24.4 us
  transfers between devices with their start and end apart: 59, of which 27 were waited for; matrix products, arithmetic and copies ran while one was open for 2% of the time, Pallas kernels for 14%

profile of v3, /device:TPU:0, one launch (start us, length us, event | category | flops | bytes accessed | tf_op | source)
XLA Modules:
  0.0 231.9 jit_solution(13347299283218484134)
XLA Ops:
  0.7 3.0 %collective-permute-start.4 = (bf16[256,768]{1,0:T(8,128)(2,1)}, bf16[256,768]{1,0:T(8,128)(2,1)S(1)}, u32[]{:S(2)}, u32[]{:S(2)}) collective-permute-start(bf16[256,768]{1,0:T(8,128)(2,1)} %x0.3), channel_id=1, source_target_pairs={{0,4},{1,5},{2,6},{3,7},{4,0},{5,1},{6,2},{7,3},{8,12},{9,13},{10,... | collective-permute-start | bytes 1179656 | tf_op jit(solution)/shard_map/ppermute | solution.py:536
  9.3 3.7 %collective-permute-start.2 = (bf16[24,3200]{1,0:T(8,128)(2,1)S(1)}, bf16[24,3200]{1,0:T(8,128)(2,1)S(1)}, u32[]{:S(2)}, u32[]{:S(2)}) collective-permute-start(bf16[24,3200]{1,0:T(8,128)(2,1)S(1)} %get-tuple-element.108.z0), channel_id=1, source_target_pairs={{0,24},{8,16},{16,8},{24,0},{1,25},{9,17},{17,9},{25,1},{2,26},{10... | collective-permute-start | bytes 460808 | tf_op jit(solution)/shard_map/ppermute | solution.py:548
  13.8 4.4 %collective-permute-done.2.z3 = bf16[24,3200]{1,0:T(8,128)(2,1)S(1)} collective-permute-done((bf16[24,3200]{1,0:T(8,128)(2,1)S(1)}, bf16[24,3200]{1,0:T(8,128)(2,1)S(1)}, u32[]{:S(2)}, u32[]{:S(2)}) %collective-permute-start.2) | collective-permute-done | bytes 153632 | tf_op jit(solution)/shard_map/ppermute | solution.py:548
  18.4 7.0 %collective-permute-done.1.z2 = bf16[24,3200]{1,0:T(8,128)(2,1)S(1)} collective-permute-done((bf16[24,3200]{1,0:T(8,128)(2,1)S(1)}, bf16[24,3200]{1,0:T(8,128)(2,1)S(1)}, u32[]{:S(2)}, u32[]{:S(2)}) %collective-permute-start.1) | collective-permute-done | bytes 153632 | tf_op jit(solution)/shard_map/ppermute | solution.py:548
  37.4 4.4 %collective-permute-start.12 = (bf16[24,3072]{1,0:T(8,128)(2,1)S(1)}, bf16[24,3072]{1,0:T(8,128)(2,1)S(1)}, u32[]{:S(2)}, u32[]{:S(2)}) collective-permute-start(bf16[24,3072]{1,0:T(8,128)(2,1)S(1)} %copy-done.3), channel_id=1, source_target_pairs={{0,16},{8,24},{16,0},{24,8},{1,17},{9,25},{17,1},{25,9},{2,18},{10... | collective-permute-start | bytes 442376 | tf_op jit(solution)/shard_map/ppermute | solution.py:548
  46.5 7.7 %collective-permute-start.13 = (bf16[96,768]{1,0:T(8,128)(2,1)S(1)}, bf16[96,768]{1,0:T(8,128)(2,1)S(1)}, u32[]{:S(2)}, u32[]{:S(2)}) collective-permute-start(bf16[96,768]{1,0:T(8,128)(2,1)S(1)} %get-tuple-element.131), channel_id=1, source_target_pairs={{0,2},{1,3},{2,0},{3,1},{4,6},{5,7},{6,4},{7,5},{8,10},{9,11},{10,... | collective-permute-start | bytes 442376 | tf_op jit(solution)/shard_map/ppermute | solution.py:536
  58.4 7.8 %attention.1 = (bf16[256,192]{1,0:T(8,128)(2,1)S(1)}, bf16[256,192]{1,0:T(8,128)(2,1)S(1)}, bf16[256,192]{1,0:T(8,128)(2,1)S(1)}, bf16[256,192]{1,0:T(8,128)(2,1...) custom-call(s32[1]{0:T(128)} %bitcast.pos, s32[1]{0:T(128)} %get-tuple-element.118.nb, ...), custom_call_target="tpu_custom_call" | custom-call | flops 10000000000 | bytes 1 | tf_op jit(solution)/shard_map/attention/pallas_call | solution.py:36
  67.4 3.8 %collective-permute-done.18.a1 = bf16[256,192]{1,0:T(8,128)(2,1)S(1)} collective-permute-done((bf16[256,192]{1,0:T(8,128)(2,1)S(1)}, bf16[256,192]{1,0:T(8,128)(2,1)S(1)}, u32[]{:S(2)}, u32[]{:S(2)}) %collective-permute-start.18) | collective-permute-done | bytes 98336 | tf_op jit(solution)/shard_map/ppermute | solution.py:536
  73.4 6.7 %collective-permute-done.21 = bf16[96,1536]{1,0:T(8,128)(2,1)S(1)} collective-permute-done((bf16[96,1536]{1,0:T(8,128)(2,1)S(1)}, bf16[96,1536]{1,0:T(8,128)(2,1)S(1)}, u32[]{:S(2)}, u32[]{:S(2)}) %collective-permute-start.21) | collective-permute-done | bytes 294944 | tf_op jit(solution)/shard_map/ppermute | solution.py:536
  81.6 13.2 %collective-permute-done.25 = bf16[2,192,896]{2,1,0:T(8,128)(2,1)S(1)} collective-permute-done((bf16[2,192,896]{2,1,0:T(8,128)(2,1)S(1)}, bf16[2,192,896]{2,1,0:T(8,128)(2,1)S(1)}, u32[]{:S(2)}, u32[]{:S(2)}) %collective-permute-start.25) | collective-permute-done | bytes 688160 | tf_op jit(solution)/shard_map/ppermute | solution.py:536
  99.1 5.7 %collective-permute-done.19.a2 = bf16[256,192]{1,0:T(8,128)(2,1)S(1)} collective-permute-done((bf16[256,192]{1,0:T(8,128)(2,1)S(1)}, bf16[256,192]{1,0:T(8,128)(2,1)S(1)}, u32[]{:S(2)}, u32[]{:S(2)}) %collective-permute-start.19) | collective-permute-done | bytes 98336 | tf_op jit(solution)/shard_map/ppermute | solution.py:536
  110.1 4.9 %collective-permute-done.27.h.h1 = bf16[256,768]{1,0:T(8,128)(2,1)S(1)} collective-permute-done((bf16[256,768]{1,0:T(8,128)(2,1)S(1)}, bf16[256,768]{1,0:T(8,128)(2,1)S(1)}, u32[]{:S(2)}, u32[]{:S(2)}) %collective-permute-start.27) | collective-permute-done | bytes 393248 | tf_op jit(solution)/shard_map/ppermute | solution.py:548
  118.5 7.2 %collective-permute-done.28.r1 = bf16[256,768]{1,0:T(8,128)(2,1)S(1)} collective-permute-done((bf16[256,768]{1,0:T(8,128)(2,1)S(1)}, bf16[256,768]{1,0:T(8,128)(2,1)S(1)}, u32[]{:S(2)}, u32[]{:S(2)}) %collective-permute-start.28) | collective-permute-done | bytes 393248 | tf_op jit(solution)/shard_map/ppermute | solution.py:548
  130.3 4.7 %collective-permute-done.29.g.g1 = bf16[256,768]{1,0:T(8,128)(2,1)S(1)} collective-permute-done((bf16[256,768]{1,0:T(8,128)(2,1)S(1)}, bf16[256,768]{1,0:T(8,128)(2,1)S(1)}, u32[]{:S(2)}, u32[]{:S(2)}) %collective-permute-start.29) | collective-permute-done | bytes 393248 | tf_op jit(solution)/shard_map/ppermute | solution.py:548
  142.5 4.3 %collective-permute-start.38 = (bf16[2,96,1536]{2,1,0:T(8,128)(2,1)S(1)}, bf16[2,96,1536]{2,1,0:T(8,128)(2,1)S(1)}, u32[]{:S(2)}, u32[]{:S(2)}) collective-permute-start(bf16[2,96,1536]{2,1,0:T(8,128)(2,1)S(1)} %slice.263), channel_id=1, source_target_pairs={{0,4},{1,5},{2,6},{3,7},{4,0},{5,1},{6,2},{7,3},{8,12},{9,13},{10,... | collective-permute-start | bytes 1769480 | tf_op jit(solution)/shard_map/ppermute | solution.py:536
  148.4 3.9 %collective-permute-done.30.r1 = bf16[256,768]{1,0:T(8,128)(2,1)S(1)} collective-permute-done((bf16[256,768]{1,0:T(8,128)(2,1)S(1)}, bf16[256,768]{1,0:T(8,128)(2,1)S(1)}, u32[]{:S(2)}, u32[]{:S(2)}) %collective-permute-start.30) | collective-permute-done | bytes 393248 | tf_op jit(solution)/shard_map/ppermute | solution.py:548
  153.4 4.0 %collective-permute-start.33 = (bf16[256,192]{1,0:T(8,128)(2,1)S(1)}, bf16[256,192]{1,0:T(8,128)(2,1)S(1)}, u32[]{:S(2)}, u32[]{:S(2)}) collective-permute-start(bf16[256,192]{1,0:T(8,128)(2,1)S(1)} %get-tuple-element.167), channel_id=1, source_target_pairs={{0,2},{1,3},{2,0},{3,1},{4,6},{5,7},{6,4},{7,5},{8,10},{9,11},{10,... | collective-permute-start | bytes 294920 | tf_op jit(solution)/shard_map/ppermute | solution.py:536
  161.0 4.7 %collective-permute-done.37 = bf16[2,192,896]{2,1,0:T(8,128)(2,1)S(1)} collective-permute-done((bf16[2,192,896]{2,1,0:T(8,128)(2,1)S(1)}, bf16[2,192,896]{2,1,0:T(8,128)(2,1)S(1)}, u32[]{:S(2)}, u32[]{:S(2)}) %collective-permute-start.37) | collective-permute-done | bytes 688160 | tf_op jit(solution)/shard_map/ppermute | solution.py:536
  172.7 11.4 %attention_back.1 = (f32[4,256,192]{2,1,0:T(8,128)S(1)}, f32[4,256,512]{2,1,0:T(8,128)S(1)}, bf16[4,256,512]{2,1,0:T(8,128)(2,1)S(1)}) custom-call(s32[1]{0:T(128)} %bitcast.pos, s32[1]{0:T(128)} %get-tuple-element.118.nb, bf16[4,256,256]{2,1,0:T(8,128)(2,1)S(1)} %get-tuple-element.119.q, bf16[4,256,512]{2,1,0:T(8,128)(2,1)S(1)} %get-tuple-element.120.mine, ...), custom_call_target="tpu_custom_call" | custom-call | flops 10000000000 | bytes 1 | tf_op jit(solution)/shard_map/attention_back/pallas_call | solution.py:36
  187.0 3.0 %collective-permute-start.58 = (bf16[96,896]{1,0:T(8,128)(2,1)S(1)}, bf16[96,896]{1,0:T(8,128)(2,1)S(1)}, u32[]{:S(2)}, u32[]{:S(2)}) collective-permute-start(bf16[96,896]{1,0:T(8,128)(2,1)S(1)} %slice.265), channel_id=1, source_target_pairs={{0,16},{8,24},{16,0},{24,8},{1,17},{9,25},{17,1},{25,9},{2,18},{10... | collective-permute-start | bytes 516104 | tf_op jit(solution)/shard_map/ppermute | solution.py:548
  190.0 6.7 %collective-permute-done.55 = bf16[48,2432]{1,0:T(8,128)(2,1)S(1)} collective-permute-done((bf16[48,2432]{1,0:T(8,128)(2,1)S(1)}, bf16[48,2432]{1,0:T(8,128)(2,1)S(1)}, u32[]{:S(2)}, u32[]{:S(2)}) %collective-permute-start.55) | collective-permute-done | bytes 233504 | tf_op jit(solution)/shard_map/ppermute | solution.py:548
  203.2 4.5 %collective-permute-done.56 = bf16[24,3968]{1,0:T(8,128)(2,1)S(1)} collective-permute-done((bf16[24,3968]{1,0:T(8,128)(2,1)S(1)}, bf16[24,3968]{1,0:T(8,128)(2,1)S(1)}, u32[]{:S(2)}, u32[]{:S(2)}) %collective-permute-start.56) | collective-permute-done | bytes 190496 | tf_op jit(solution)/shard_map/ppermute | solution.py:548
  215.8 3.4 %collective-permute-done.47 = bf16[96,640]{1,0:T(8,128)(2,1)S(1)} collective-permute-done((bf16[96,640]{1,0:T(8,128)(2,1)S(1)}, bf16[96,640]{1,0:T(8,128)(2,1)S(1)}, u32[]{:S(2)}, u32[]{:S(2)}) %collective-permute-start.47) | collective-permute-done | bytes 122912 | tf_op jit(solution)/shard_map/ppermute | solution.py:548
  219.2 5.0 %collective-permute-done.46 = bf16[96,640]{1,0:T(8,128)(2,1)S(1)} collective-permute-done((bf16[96,640]{1,0:T(8,128)(2,1)S(1)}, bf16[96,640]{1,0:T(8,128)(2,1)S(1)}, u32[]{:S(2)}, u32[]{:S(2)}) %collective-permute-start.46) | collective-permute-done | bytes 122912 | tf_op jit(solution)/shard_map/ppermute | solution.py:548
  (168 shorter events, 95.8 us)
Async XLA Ops:
  0.7 24.8 %collective-permute-start.4 = (bf16[256,768]{1,0:T(8,128)(2,1)}, bf16[256,768]{1,0:T(8,128)(2,1)S(1)}, u32[]{:S(2)}, u32[]{:S(2)}) collective-permute-start(bf16[256,768]{1,0:T(8,128)(2,1)} %x0.3), channel_id=1, source_target_pairs={{0,4},{1,5},{2,6},{3,7},{4,0},{5,1},{6,2},{7,3},{8,12},{9,13},{10,... | collective-permute-start | bytes 1179656 | tf_op jit(solution)/shard_map/ppermute | solution.py:536
  3.7 21.8 %collective-permute-start.3 = (bf16[256,768]{1,0:T(8,128)(2,1)}, bf16[256,768]{1,0:T(8,128)(2,1)S(1)}, u32[]{:S(2)}, u32[]{:S(2)}) collective-permute-start(bf16[256,768]{1,0:T(8,128)(2,1)} %x0.3), channel_id=1, source_target_pairs={{0,2},{1,3},{2,0},{3,1},{4,6},{5,7},{6,4},{7,5},{8,10},{9,11},{10,... | collective-permute-start | bytes 1179656 | tf_op jit(solution)/shard_map/ppermute | solution.py:536
  18.2 15.1 %collective-permute-start.8 = (bf16[256,768]{1,0:T(8,128)(2,1)}, bf16[256,768]{1,0:T(8,128)(2,1)S(1)}, u32[]{:S(2)}, u32[]{:S(2)}) collective-permute-start(bf16[256,768]{1,0:T(8,128)(2,1)} %x0.3), channel_id=1, source_target_pairs={{0,6},{1,7},{2,4},{3,5},{4,2},{5,3},{6,0},{7,1},{8,14},{9,15},{10,... | collective-permute-start | bytes 1179656 | tf_op jit(solution)/shard_map/ppermute | solution.py:536
  37.2 21.1 %collective-permute-start.10 = (bf16[4,256,512]{2,1,0:T(8,128)(2,1)S(1)}, bf16[4,256,512]{2,1,0:T(8,128)(2,1)S(1)}, u32[]{:S(2)}, u32[]{:S(2)}) collective-permute-start(bf16[4,256,512]{2,1,0:T(8,128)(2,1)S(1)} %get-tuple-element.120.mine), channel_id=1, source_target_pairs={{0,1},{1,0},{2,3},{3,2},{4,5},{5,4},{6,7},{7,6},{8,9},{9,8},{10,11... | collective-permute-start | bytes 3145736 | tf_op jit(solution)/shard_map/ppermute | solution.py:540
  41.8 14.9 %collective-permute-start.11 = (bf16[96,896]{1,0:T(8,128)(2,1)S(1)}, bf16[96,896]{1,0:T(8,128)(2,1)S(1)}, u32[]{:S(2)}, u32[]{:S(2)}) collective-permute-start(bf16[96,896]{1,0:T(8,128)(2,1)S(1)} %get-tuple-element.122), channel_id=1, source_target_pairs={{0,16},{8,24},{16,0},{24,8},{1,17},{9,25},{17,1},{25,9},{2,18},{10... | collective-permute-start | bytes 516104 | tf_op jit(solution)/shard_map/ppermute | solution.py:548
  41.8 15.6 %collective-permute-start.15 = (bf16[96,768]{1,0:T(8,128)(2,1)S(1)}, bf16[96,768]{1,0:T(8,128)(2,1)S(1)}, u32[]{:S(2)}, u32[]{:S(2)}) collective-permute-start(bf16[96,768]{1,0:T(8,128)(2,1)S(1)} %get-tuple-element.131), channel_id=1, source_target_pairs={{0,6},{1,7},{2,4},{3,5},{4,2},{5,3},{6,0},{7,1},{8,14},{9,15},{10,... | collective-permute-start | bytes 442376 | tf_op jit(solution)/shard_map/ppermute | solution.py:536
  43.2 15.0 %collective-permute-start.14 = (bf16[96,768]{1,0:T(8,128)(2,1)S(1)}, bf16[96,768]{1,0:T(8,128)(2,1)S(1)}, u32[]{:S(2)}, u32[]{:S(2)}) collective-permute-start(bf16[96,768]{1,0:T(8,128)(2,1)S(1)} %get-tuple-element.131), channel_id=1, source_target_pairs={{0,4},{1,5},{2,6},{3,7},{4,0},{5,1},{6,2},{7,3},{8,12},{9,13},{10,... | collective-permute-start | bytes 442376 | tf_op jit(solution)/shard_map/ppermute | solution.py:536
  57.5 14.9 %collective-permute-start.24 = (bf16[192,896]{1,0:T(8,128)(2,1)S(1)}, bf16[192,896]{1,0:T(8,128)(2,1)S(1)}, u32[]{:S(2)}, u32[]{:S(2)}) collective-permute-start(bf16[192,896]{1,0:T(8,128)(2,1)S(1)} %constant_dynamic-update-slice_fusion), channel_id=1, source_target_pairs={{0,4},{1,5},{2,6},{3,7},{4,0},{5,1},{6,2},{7,3},{8,12},{9,13},{10,... | collective-permute-start | bytes 1032200 | tf_op jit(solution)/shard_map/ppermute | solution.py:536
  72.4 22.4 %collective-permute-start.25 = (bf16[2,192,896]{2,1,0:T(8,128)(2,1)S(1)}, bf16[2,192,896]{2,1,0:T(8,128)(2,1)S(1)}, u32[]{:S(2)}, u32[]{:S(2)}) collective-permute-start(bf16[2,192,896]{2,1,0:T(8,128)(2,1)S(1)} %pad_maximum_fusion.2), channel_id=1, source_target_pairs={{0,2},{1,3},{2,0},{3,1},{4,6},{5,7},{6,4},{7,5},{8,10},{9,11},{10,... | collective-permute-start | bytes 2064392 | tf_op jit(solution)/shard_map/ppermute | solution.py:536
  80.1 15.7 %collective-permute-start.22 = (bf16[2,96,1536]{2,1,0:T(8,128)(2,1)S(1)}, bf16[2,96,1536]{2,1,0:T(8,128)(2,1)S(1)}, u32[]{:S(2)}, u32[]{:S(2)}) collective-permute-start(bf16[2,96,1536]{2,1,0:T(8,128)(2,1)S(1)} %pad_maximum_fusion.4), channel_id=1, source_target_pairs={{0,4},{1,5},{2,6},{3,7},{4,0},{5,1},{6,2},{7,3},{8,12},{9,13},{10,... | collective-permute-start | bytes 1769480 | tf_op jit(solution)/shard_map/ppermute | solution.py:536
  142.5 18.4 %collective-permute-start.38 = (bf16[2,96,1536]{2,1,0:T(8,128)(2,1)S(1)}, bf16[2,96,1536]{2,1,0:T(8,128)(2,1)S(1)}, u32[]{:S(2)}, u32[]{:S(2)}) collective-permute-start(bf16[2,96,1536]{2,1,0:T(8,128)(2,1)S(1)} %slice.263), channel_id=1, source_target_pairs={{0,4},{1,5},{2,6},{3,7},{4,0},{5,1},{6,2},{7,3},{8,12},{9,13},{10,... | collective-permute-start | bytes 1769480 | tf_op jit(solution)/shard_map/ppermute | solution.py:536
  147.3 18.4 %collective-permute-start.37 = (bf16[2,192,896]{2,1,0:T(8,128)(2,1)S(1)}, bf16[2,192,896]{2,1,0:T(8,128)(2,1)S(1)}, u32[]{:S(2)}, u32[]{:S(2)}) collective-permute-start(bf16[2,192,896]{2,1,0:T(8,128)(2,1)S(1)} %slice.136), channel_id=1, source_target_pairs={{0,2},{1,3},{2,0},{3,1},{4,6},{5,7},{6,4},{7,5},{8,10},{9,11},{10,... | collective-permute-start | bytes 2064392 | tf_op jit(solution)/shard_map/ppermute | solution.py:536
  153.4 15.1 %collective-permute-start.33 = (bf16[256,192]{1,0:T(8,128)(2,1)S(1)}, bf16[256,192]{1,0:T(8,128)(2,1)S(1)}, u32[]{:S(2)}, u32[]{:S(2)}) collective-permute-start(bf16[256,192]{1,0:T(8,128)(2,1)S(1)} %get-tuple-element.167), channel_id=1, source_target_pairs={{0,2},{1,3},{2,0},{3,1},{4,6},{5,7},{6,4},{7,5},{8,10},{9,11},{10,... | collective-permute-start | bytes 294920 | tf_op jit(solution)/shard_map/ppermute | solution.py:536
  157.4 12.5 %collective-permute-start.34 = (bf16[256,192]{1,0:T(8,128)(2,1)S(1)}, bf16[256,192]{1,0:T(8,128)(2,1)S(1)}, u32[]{:S(2)}, u32[]{:S(2)}) collective-permute-start(bf16[256,192]{1,0:T(8,128)(2,1)S(1)} %get-tuple-element.168), channel_id=1, source_target_pairs={{0,4},{1,5},{2,6},{3,7},{4,0},{5,1},{6,2},{7,3},{8,12},{9,13},{10,... | collective-permute-start | bytes 294920 | tf_op jit(solution)/shard_map/ppermute | solution.py:536
  158.4 13.6 %collective-permute-start.35 = (bf16[256,192]{1,0:T(8,128)(2,1)S(1)}, bf16[256,192]{1,0:T(8,128)(2,1)S(1)}, u32[]{:S(2)}, u32[]{:S(2)}) collective-permute-start(bf16[256,192]{1,0:T(8,128)(2,1)S(1)} %get-tuple-element.169), channel_id=1, source_target_pairs={{0,6},{1,7},{2,4},{3,5},{4,2},{5,3},{6,0},{7,1},{8,14},{9,15},{10,... | collective-permute-start | bytes 294920 | tf_op jit(solution)/shard_map/ppermute | solution.py:536
  165.7 18.5 %collective-permute-start.51 = (bf16[96,1536]{1,0:T(8,128)(2,1)S(1)}, bf16[96,1536]{1,0:T(8,128)(2,1)S(1)}, u32[]{:S(2)}, u32[]{:S(2)}) collective-permute-start(bf16[96,1536]{1,0:T(8,128)(2,1)S(1)} %fusion.12), channel_id=1, source_target_pairs={{0,2},{1,3},{2,0},{3,1},{4,6},{5,7},{6,4},{7,5},{8,10},{9,11},{10,... | collective-permute-start | bytes 884744 | tf_op jit(solution)/shard_map/ppermute | solution.py:536
  166.7 20.1 %collective-permute-start.57 = (bf16[192,896]{1,0:T(8,128)(2,1)S(1)}, bf16[192,896]{1,0:T(8,128)(2,1)S(1)}, u32[]{:S(2)}, u32[]{:S(2)}) collective-permute-start(bf16[192,896]{1,0:T(8,128)(2,1)S(1)} %fusion.8), channel_id=1, source_target_pairs={{0,4},{1,5},{2,6},{3,7},{4,0},{5,1},{6,2},{7,3},{8,12},{9,13},{10,... | collective-permute-start | bytes 1032200 | tf_op jit(solution)/shard_map/ppermute | solution.py:536
  168.5 16.8 %collective-permute-start.54 = (bf16[96,896]{1,0:T(8,128)(2,1)S(1)}, bf16[96,896]{1,0:T(8,128)(2,1)S(1)}, u32[]{:S(2)}, u32[]{:S(2)}) collective-permute-start(bf16[96,896]{1,0:T(8,128)(2,1)S(1)} %get-tuple-element.217), channel_id=1, source_target_pairs={{0,6},{1,7},{2,4},{3,5},{4,2},{5,3},{6,0},{7,1},{8,14},{9,15},{10,... | collective-permute-start | bytes 516104 | tf_op jit(solution)/shard_map/ppermute | solution.py:536
  169.9 15.7 %collective-permute-start.53 = (bf16[96,896]{1,0:T(8,128)(2,1)S(1)}, bf16[96,896]{1,0:T(8,128)(2,1)S(1)}, u32[]{:S(2)}, u32[]{:S(2)}) collective-permute-start(bf16[96,896]{1,0:T(8,128)(2,1)S(1)} %get-tuple-element.218), channel_id=1, source_target_pairs={{0,4},{1,5},{2,6},{3,7},{4,0},{5,1},{6,2},{7,3},{8,12},{9,13},{10,... | collective-permute-start | bytes 516104 | tf_op jit(solution)/shard_map/ppermute | solution.py:536
  171.9 13.7 %collective-permute-start.52 = (bf16[96,896]{1,0:T(8,128)(2,1)S(1)}, bf16[96,896]{1,0:T(8,128)(2,1)S(1)}, u32[]{:S(2)}, u32[]{:S(2)}) collective-permute-start(bf16[96,896]{1,0:T(8,128)(2,1)S(1)} %get-tuple-element.219), channel_id=1, source_target_pairs={{0,2},{1,3},{2,0},{3,1},{4,6},{5,7},{6,4},{7,5},{8,10},{9,11},{10,... | collective-permute-start | bytes 516104 | tf_op jit(solution)/shard_map/ppermute | solution.py:536
  184.3 13.6 %collective-permute-start.39 = (bf16[4,256,512]{2,1,0:T(8,128)(2,1)S(1)}, bf16[4,256,512]{2,1,0:T(8,128)(2,1)S(1)}, u32[]{:S(2)}, u32[]{:S(2)}) collective-permute-start(bf16[4,256,512]{2,1,0:T(8,128)(2,1)S(1)} %get-tuple-element.183), channel_id=1, source_target_pairs={{0,1},{1,0},{2,3},{3,2},{4,5},{5,4},{6,7},{7,6},{8,9},{9,8},{10,11... | collective-permute-start | bytes 3145736 | tf_op jit(solution)/shard_map/ppermute | solution.py:540
  199.5 13.4 %collective-permute-start.40 = (bf16[256,768]{1,0:T(8,128)(2,1)S(1)}, bf16[256,768]{1,0:T(8,128)(2,1)S(1)}, u32[]{:S(2)}, u32[]{:S(2)}) collective-permute-start(bf16[256,768]{1,0:T(8,128)(2,1)S(1)} %get-tuple-element.187), channel_id=1, source_target_pairs={{0,2},{1,3},{2,0},{3,1},{4,6},{5,7},{6,4},{7,5},{8,10},{9,11},{10,... | collective-permute-start | bytes 1179656 | tf_op jit(solution)/shard_map/ppermute | solution.py:536
  213.1 14.8 %collective-permute-start.42 = (bf16[128,768]{1,0:T(8,128)(2,1)S(1)}, bf16[128,768]{1,0:T(8,128)(2,1)S(1)}, u32[]{:S(2)}, u32[]{:S(2)}) collective-permute-start(bf16[128,768]{1,0:T(8,128)(2,1)S(1)} %get-tuple-element.220), channel_id=1, source_target_pairs={{0,4},{1,5},{2,6},{3,7},{4,0},{5,1},{6,2},{7,3},{8,12},{9,13},{10,... | collective-permute-start | bytes 589832 | tf_op jit(solution)/shard_map/ppermute | solution.py:536
  215.1 12.7 %collective-permute-start.43 = (bf16[128,768]{1,0:T(8,128)(2,1)S(1)}, bf16[128,768]{1,0:T(8,128)(2,1)S(1)}, u32[]{:S(2)}, u32[]{:S(2)}) collective-permute-start(bf16[128,768]{1,0:T(8,128)(2,1)S(1)} %get-tuple-element.221), channel_id=1, source_target_pairs={{0,2},{1,3},{2,0},{3,1},{4,6},{5,7},{6,4},{7,5},{8,10},{9,11},{10,... | collective-permute-start | bytes 589832 | tf_op jit(solution)/shard_map/ppermute | solution.py:536
  (41 other events, 341.2 us)

commit v4 on v3

--- a/solution.py
+++ b/solution.py
@@ -54,69 +54,46 @@
     return pl.multiple_of(start, size)
 
 
-def pack_kernel(wqkv, wo, wout, smalls, zq, zw):
+def each_chip(p, run):
+    for own in range(4):
+
+        @pl.when(p == own)
+        def _(own=own):
+            run(own)
+
+
+def pack_kernel(pos, wqkv, win, wout, smalls, p0, p1, p2, p3, wx):
+    z, p, c = place(pos)
     rows = lax.broadcasted_iota(jnp.int32, (96, 96), 0)
     cols = lax.broadcasted_iota(jnp.int32, (96, 96), 1)
     eye = (rows == cols).astype(BF16)
     side = dot(eye, smalls[...], NT).astype(BF16)
-    side = jnp.concatenate([side, jnp.zeros((96, 112), BF16)], axis=1)
-    zw[:, 0:768] = wout[...]
-    zw[:, 768:896] = side
-    zq[:, 0:2304] = wqkv[...]
-    zq[:, 2304:3072] = wo[...]
-    zq[:, 3072:3200] = side[:24]
-
-
-def each_chip(p, run):
-    for own in range(4):
-
-        @pl.when(p == own)
-        def _(own=own):
-            run(own)
-
-
-def split_qkv_kernel(pos, z0, z1, z2, z3, p0, p1, p2, p3, wo):
-    z, p, c = place(pos)
-    for i, zq in enumerate((z0, z1, z2, z3)):
-        wo[24 * i : 24 * i + 24, :] = zq[:, 2304:3072]
+    wx[...] = jnp.concatenate([wout[...], side, jnp.zeros((96, 112), BF16)], axis=1)
+    small = jnp.concatenate([side[:24], jnp.zeros((24, 48), BF16)], axis=1)
 
     def run(own):
         for k, out in enumerate((p0, p1, p2, p3)):
             at = 192 * (own ^ k)
-            for i, zq in enumerate((z0, z1, z2, z3)):
-                parts = [zq[:, 768 * t + at : 768 * t + at + 192] for t in range(3)]
-                parts.append(zq[:, 3072:3136])
-                out[24 * i : 24 * i + 24, :] = jnp.concatenate(parts, axis=1)
+            parts = [wqkv[:, 768 * i + at : 768 * i + at + 192] for i in range(3)]
+            parts.append(small)
+            parts += [win[:, 768 * i + at : 768 * i + at + 192] for i in range(4)]
+            out[...] = jnp.concatenate(parts, axis=1)
 
     each_chip(p, run)
 
 
-def split_in_kernel(pos, z0, z1, mine, theirs):
-    z, p, c = place(pos)
-    for side in range(2):
-
-        @pl.when((z & 1) == side)
-        def _(side=side):
-            for out, g in ((mine, side), (theirs, 1 - side)):
-                for i, zi in enumerate((z0, z1)):
-                    at = slice(24 * i, 24 * i + 24)
-                    out[at, 0:768] = zi[:, 768 * g : 768 * g + 768]
-                    out[at, 768:1536] = zi[:, 768 * g + 1536 : 768 * g + 2304]
-
-
 SLOTS = (0, 2, 1, 3)
 
 
-def interleave(pos, mine, other, out, slots):
+def interleave(pos, mine, other, out, at, slots):
     z, p, c = place(pos)
 
     def run(first, second):
         for k in range(4):
             for i in range(4):
-                at = (k, slice(24 * i, 24 * i + 24), slice(None))
-                block = jnp.concatenate([first[at], second[at]], axis=0)
-                plane = z ^ slots[i]
-                out[pl.ds(row_of((4 * plane + (p ^ k)) * 48, 16), 48), :] = block
+                block = jnp.concatenate([first[at(i, k)], second[at(i, k)]], axis=0)
+                start = (4 * (z ^ slots[i]) + (p ^ k)) * 48
+                out[pl.ds(row_of(start, 16), 48), :] = block
 
     @pl.when(c == 0)
     def _():
@@ -129,7 +106,10 @@
 
 def qkv_kernel(pos, am, ao, x0, x1, x2, x3, q, kv, wq, vecs, nb, bias):
     z, p, c = place(pos)
-    interleave(pos, am, ao, wq, (0, 1, 2, 3))
+    everything = slice(None)
+    interleave(
+        pos, am, ao, wq, lambda i, k: (i, slice(24 * k, 24 * k + 24), everything), (0, 1, 2, 3)
+    )
     flipped = jnp.transpose(wq[:, 512:640].astype(F32))
     vecs[...] = flipped[64:80]
 
@@ -152,24 +132,22 @@
         kv[k] = jnp.concatenate([got[:, 192:384], pad, got[:, 384:576], pad], axis=1)
 
 
-def join_in_kernel(pos, im, io, wi):
-    interleave(pos, im, io, wi, SLOTS)
-
-
-def join_wo_kernel(pos, om, oo, wo):
-    interleave(pos, om, oo, wo, (0, 1, 2, 3))
-
-
-def join_out_kernel(pos, wm, wo_, wx, bin_):
+def join_ff_kernel(pos, mm, mo, wi, wx, bin_):
     z, p, c = place(pos)
-    for k in range(4):
-        for i in range(2):
-            start = (((z ^ (2 * i)) >> 1) * 4 + (p ^ SLOTS[k])) * 192
-            at = (k, slice(96 * i, 96 * i + 96), slice(None))
-            wx[pl.ds(row_of(start + c * 96, 32), 96), :] = wm[at]
-            wx[pl.ds(row_of(start + (1 - c) * 96, 32), 96), :] = wo_[at]
+    interleave(
+        pos, mm, mo, wi, lambda i, k: (i, slice(24 * k, 24 * k + 24), slice(0, 768)), SLOTS
+    )
+    for i in range(4):
+        base = (z ^ SLOTS[i]) * 192
+        wx[pl.ds(row_of(base + c * 96, 32), 96), :] = mm[i, :, 768:1664]
+        wx[pl.ds(row_of(base + (1 - c) * 96, 32), 96), :] = mo[i, :, 768:1664]
     flipped = jnp.transpose(wx[:, 768:896].astype(F32))
     bin_[...] = flipped[8:16]
+
+
+def join_wo_kernel(pos, om, oo, wo):
+    everything = slice(None)
+    interleave(pos, om, oo, wo, lambda i, k: (k, slice(24 * i, 24 * i + 24), everything), SLOTS)
 
 
 def key_range(pos, nb, k):
@@ -324,16 +302,22 @@
     return scale * (e - mean_e - hat * mean_x)
 
 
+def summed(i, own, rx, ry, sx, sy):
+    half = slice(32 * (i % 4), 32 * (i % 4) + 32)
+    first, last = (rx, sy) if i < 4 else (ry, sx)
+    return own[32 * i : 32 * i + 32, :] + first[half, :].astype(F32) + last[half, :].astype(F32)
+
+
 def total(values):
     return jnp.sum(values, axis=0, keepdims=True)
 
 
-def norm_two_kernel(vecs, xhat, own, r1, cot, block_out, low, grad_two, sums):
+def norm_two_kernel(vecs, xhat, own, rx, ry, sx, sy, cot, block_out, low, grad_two, sums):
     acc = [jnp.zeros((1, 768), F32) for _ in range(3)]
     for i in range(8):
         at = slice(32 * i, 32 * i + 32)
         hidden = xhat[at, :] * vecs[3:4, :] + vecs[5:6, :]
-        resid = hidden + own[at, :] + r1[at, :].astype(F32) + vecs[7:8, :]
+        resid = hidden + summed(i, own, rx, ry, sx, sy) + vecs[7:8, :]
         center = resid - jnp.mean(resid, axis=-1, keepdims=True)
         scale = lax.rsqrt(jnp.mean(center * center, axis=-1, keepdims=True) + EPSILON)
         hat = center * scale
@@ -347,13 +331,13 @@
 
 
 def norm_one_kernel(
-    pos, own, r1, grad_two, xhat, rstd, vecs, wo, o0, o1, o2, o3, low, grad_one, sums
+    pos, own, rx, ry, sx, sy, grad_two, xhat, rstd, vecs, wo, o0, o1, o2, o3, low, grad_one, sums
 ):
     z, p, c = place(pos)
     acc = [jnp.zeros((1, 768), F32) for _ in range(3)]
     for i in range(8):
         at = slice(32 * i, 32 * i + 32)
-        grad = own[at, :] + grad_two[at, :] + r1[at, :].astype(F32)
+        grad = summed(i, own, rx, ry, sx, sy) + grad_two[at, :]
         hat = xhat[at, :]
         back = norm_grad(grad, vecs[3:4, :], hat, rstd[at, :])
         grad_one[at, :] = back
@@ -365,29 +349,66 @@
         out[...] = dot(low[...], wo[pl.ds(row_of(start, 64), 192), :], NT).astype(BF16)
 
 
-def ff_kernel(h, wi, wx, bias, part, act, slope):
-    acc = jnp.zeros((256, 768), F32)
-    for f in range(6):
+def ff_block(h, wi, wx, bias, act, slope):
+    acc = jnp.zeros((h.shape[0], 768), F32)
+    for f in range(3):
         at = slice(256 * f, 256 * f + 256)
-        u = dot(h[...], wi[:, at]) + bias[1:2, at]
+        u = dot(h, wi[:, at]) + bias[1:2, at]
         cdf = 0.5 * (1.0 + lax.erf(u * 0.7071067811865476))
         low = (u * cdf).astype(BF16)
         act[:, at] = low
         slope[:, at] = cdf + u * jnp.exp2(u * u * (-0.5 * LOG2E)) * 0.3989422804014327
         acc += dot(low, wx[at, :768])
-    part[...] = acc.astype(part.dtype)
-
-
-def ff_back_kernel(g, slope, wi, wx, back, pre_low, sums):
+    return acc
+
+
+def ff_back_block(g, slope, wi, wx, low, sums):
     acc = jnp.zeros((256, 768), F32)
-    for f in range(6):
+    for f in range(3):
         at = slice(256 * f, 256 * f + 256)
-        pre = dot(g[...], wx[at, :768], NT) * slope[:, at]
-        low = pre.astype(BF16)
-        pre_low[:, at] = low
-        sums[:, at] = jnp.broadcast_to(total(pre), (8, 256))
-        acc += dot(low, wi[:, at], NT)
-    back[...] = acc.astype(back.dtype)
+        pre = dot(g, wx[at, :768], NT) * slope[:, at]
+        pre_low = pre.astype(BF16)
+        low[:, at] = pre_low
+        sums[0:1, at] += total(pre)
+        acc += dot(pre_low, wi[:, at], NT)
+    return acc
+
+
+def ff_own_kernel(h, wi, wx, bias, part, act, slope):
+    part[...] = ff_block(h[...], wi, wx, bias, act, slope)
+
+
+def ff_near_kernel(h1, h2, wi, wx, bias, part1, part2, act1, act2, slope1, slope2):
+    part1[...] = ff_block(h1[...], wi, wx, bias, act1, slope1).astype(BF16)
+    part2[...] = ff_block(h2[...], wi, wx, bias, act2, slope2).astype(BF16)
+
+
+def first_round(part, part1, part2, mx, my):
+    low = part.astype(BF16)
+    mx[...] = jnp.concatenate([part1[:128, :], low[:128]], axis=0)
+    my[...] = jnp.concatenate([part2[128:, :], low[128:]], axis=0)
+
+
+def ff_far_kernel(ha, hb, part1, part2, wi, wx, bias, mx, my, act, slope):
+    h = jnp.concatenate([ha[...], hb[...]], axis=0)
+    first_round(ff_block(h, wi, wx, bias, act, slope), part1, part2, mx, my)
+
+
+def ff_back_own_kernel(g, slope, wi, wx, back, low, sums):
+    sums[...] = jnp.zeros((8, 768), F32)
+    back[...] = ff_back_block(g[...], slope, wi, wx, low, sums)
+
+
+def ff_back_near_kernel(g1, g2, slope1, slope2, wi, wx, back1, back2, low1, low2, sums):
+    sums[...] = jnp.zeros((8, 768), F32)
+    back1[...] = ff_back_block(g1[...], slope1, wi, wx, low1, sums).astype(BF16)
+    back2[...] = ff_back_block(g2[...], slope2, wi, wx, low2, sums).astype(BF16)
+
+
+def ff_back_far_kernel(ga, gb, slope, back1, back2, wi, wx, mx, my, low, sums):
+    sums[...] = jnp.zeros((8, 768), F32)
+    g = jnp.concatenate([ga[...], gb[...]], axis=0)
+    first_round(ff_back_block(g, slope, wi, wx, low, sums), back1, back2, mx, my)
 
 
 def column_of(row):
@@ -396,25 +417,23 @@
     return jnp.transpose(jnp.where(first, jnp.broadcast_to(row, (128, n)), 0.0))
 
 
-def ff_grad_out_kernel(pos, a0, a1, g0, g1, sum_a, sum_b, keep, send, go):
+def ff_grad_kernel(
+    pos, h0, h1, h2, ha, hb, b0, b1, b2, b3, a0, a1, a2, a3, g0, g1, g2, ga, gb, s0, s1, s2,
+    keep, send, gi, go
+):
     z, p, c = place(pos)
-    go[:, :768] = dot(a0[...], g0[...], TN) + dot(a1[...], g1[...], TN)
-    go[:, 768:] = column_of(sum_a[0:1, :] + sum_b[0:1, :])
-    for k in range(4):
-        for i in range(2):
-            for out, core in ((keep, c), (send, 1 - c)):
-                start = (((z ^ (2 * i)) >> 1) * 4 + (p ^ k)) * 192 + core * 96
-                out[k, 96 * i : 96 * i + 96, :] = go[pl.ds(row_of(start), 96), :].astype(BF16)
-
-
-def ff_grad_in_kernel(pos, h0, h1, b0, b1, keep, send, gi):
-    z, p, c = place(pos)
-    gi[...] = dot(h0[...], b0[...], TN) + dot(h1[...], b1[...], TN)
-    for k in range(4):
-        for i in range(4):
-            for out, core in ((keep, c), (send, 1 - c)):
+    acc = dot(h0[...], b0[...], TN) + dot(h1[...], b1[...], TN) + dot(h2[...], b2[...], TN)
+    gi[...] = acc + dot(ha[...], b3[:128, :], TN) + dot(hb[...], b3[128:, :], TN)
+    acc = dot(a0[...], g0[...], TN) + dot(a1[...], g1[...], TN) + dot(a2[...], g2[...], TN)
+    go[:, :768] = acc + dot(a3[:128, :], ga[...], TN) + dot(a3[128:, :], gb[...], TN)
+    go[:, 768:] = column_of(s0[0:1, :] + s1[0:1, :] + s2[0:1, :])
+    for i in range(4):
+        for out, core in ((keep, c), (send, 1 - c)):
+            for k in range(4):
                 start = (4 * (z ^ SLOTS[i]) + (p ^ k)) * 48 + core * 24
-                out[k, 24 * i : 24 * i + 24, :] = gi[pl.ds(row_of(start), 24), :].astype(BF16)
+                out[i, 24 * k : 24 * k + 24, 0:768] = gi[pl.ds(row_of(start), 24), :].astype(BF16)
+            start = (z ^ SLOTS[i]) * 192 + core * 96
+            out[i, :, 768:1664] = go[pl.ds(row_of(start), 96), :].astype(BF16)
 
 
 def wo_grad_kernel(pos, a0, a1, a2, a3, low, sum_one, sum_two, keep, send, acc):
@@ -459,10 +478,10 @@
             i0[...] = part
         elif k == 1:
             mx[0:128, :] = part[:128].astype(BF16)
-            rest[1] = part[128:].astype(BF16)
+            rest[1, 128:] = part[128:].astype(BF16)
         elif k == 2:
             my[0:128, :] = part[128:].astype(BF16)
-            rest[0] = part[:128].astype(BF16)
+            rest[0, :128] = part[:128].astype(BF16)
         else:
             mx[128:256, :] = part[:128].astype(BF16)
             my[128:256, :] = part[128:].astype(BF16)
@@ -488,7 +507,7 @@
     for j in range(4):
         for k in range(4):
             for out, core in ((keep, c), (send, 1 - c)):
-                start = (4 * (z ^ j) + (p ^ k)) * 48 + core * 24
+                start = (4 * (z ^ SLOTS[j]) + (p ^ k)) * 48 + core * 24
                 out[j, 24 * k : 24 * k + 24, :] = acc[pl.ds(row_of(start), 24), :].astype(BF16)
 
 
@@ -498,13 +517,13 @@
 
 
 def finish_kernel(
-    pos, tq, f1, f2, f3, ti, tw, gqkv, gbqv, gwo, gbo, gain, shift, gwin, gbin, gwout, gbout
+    pos, tq, tm, f1, f2, f3, uo, gqkv, gbqv, gwo, gbo, gain, shift, gwin, gbin, gwout, gbout
 ):
     z, p, c = place(pos)
-    gwout[...] = tw[:, 0:768]
-    gbin[...] = turned(tw[:, 768:896])[0:1, 0:96]
-    gwo[...] = ti[:, 3072:3840]
-    side = turned(ti[:, 3840:3968])
+    gwout[...] = tm[:, 768:1536]
+    gbin[...] = turned(tm[:, 1536:1664])[0:1, 0:96]
+    gwo[...] = uo[:, 0:768]
+    side = turned(uo[:, 768:896])
     gbo[...] = side[0:1, 0:24]
     gain[...] = side[1:3, 0:24]
     shift[...] = side[3:5, 0:24]
@@ -514,22 +533,21 @@
         biases = jnp.zeros((24, 128), F32)
         for k in range(4):
             chip = own ^ k
-            qkv = tq[0:24, :] if k == 0 else (f1, f2, f3)[k - 1][...].astype(F32)
+            if k == 0:
+                qkv, win = tq[0:24, :], tm[0:24, 0:768]
+            else:
+                got = (f1, f2, f3)[k - 1][...].astype(F32)
+                qkv, win = got[:, 0:640], got[:, 640:1408]
             for i in range(3):
                 at = 768 * i + 192 * chip
                 gqkv[:, at : at + 192] = qkv[:, 192 * i : 192 * i + 192]
+            for i in range(4):
+                at = 768 * i + 192 * chip
+                gwin[:, at : at + 192] = win[:, 192 * i : 192 * i + 192]
             biases += jnp.where(z == chip, qkv[:, 512:640], 0.0)
         gbqv[...] = turned(biases)[64:66, 0:24]
 
     each_chip(p, run)
-    for side in range(2):
-
-        @pl.when((z & 1) == side)
-        def _(side=side):
-            for t in range(2):
-                for i in range(2):
-                    at = 768 * (side ^ t) + 1536 * i
-                    gwin[:, at : at + 768] = ti[:, 1536 * t + 768 * i : 1536 * t + 768 * i + 768]
 
 
 def chip_swap(value, k):
@@ -546,6 +564,21 @@
 
 def z_swap(value, j):
     return lax.ppermute(value, "dp", [(i, i ^ j) for i in range(4)])
+
+
+def gather_first(value):
+    return chip_swap(value, 1), chip_swap(value, 2)
+
+
+def gather_last(near_x, near_y):
+    return chip_swap(near_y[:128], 1), chip_swap(near_x[128:], 2)
+
+
+def reduce_parts(mx, my, part1, part2):
+    rx, ry = chip_swap(mx, 1), chip_swap(my, 2)
+    sy = chip_swap(low_add(part2[:128], rx[128:]).astype(BF16), 2)
+    sx = chip_swap(low_add(part1[128:], ry[128:]).astype(BF16), 1)
+    return rx, ry, sx, sy
 
 
 def after(value, *others):
@@ -585,34 +618,29 @@
             (bias_in[None], 9),
         )
     )
-    x1, x2, x3 = (chip_swap(tokens, k) for k in others)
-    zq, zw = call(
+    zo_one = z_swap(w_o, 2)
+    p0, p1, p2, p3, zw = call(
         pack_kernel,
-        (w_qkv, w_o, w_out, smalls),
-        [sds((24, 3200), BF16), sds((96, 896), BF16)],
-        smem_in=(),
+        (pos, w_qkv, w_in, w_out, smalls),
+        [sds((24, 1408), BF16)] * 4 + [sds((96, 896), BF16)],
         name="pack",
     )
-    zqs = (zq,) + lax.optimization_barrier((*[z_swap(zq, j) for j in others], x1, x2))[:3]
+    zo_pair = jnp.concatenate([w_o, zo_one], axis=0)
+    zo_two = z_swap(zo_pair, 1)
+    got = [p0] + [chip_swap(v, k) for v, k in zip((p1, p2, p3), others)]
+    tokens_far = after(tokens, p0, zo_one)
+    x1, x2 = chip_swap(tokens_far, 1), chip_swap(tokens_far, 2)
+    first = jnp.concatenate([g[:, :640] for g in got], axis=0)
+    first = after(first, zo_two)
+    firsts = [first] + [z_swap(first, j) for j in others]
+    x3 = chip_swap(after(tokens_far, *got[1:]), 3)
     xs = (tokens, x1, x2, x3)
-    *pieces_q, wo_z = call(
-        split_qkv_kernel,
-        (pos, *zqs),
-        [sds((96, 640), BF16)] * 4 + [sds((96, 768), BF16)],
-        name="split_qkv",
-    )
-    first_all = jnp.stack([pieces_q[0]] + [chip_swap(pieces_q[k], k) for k in others])
-    first_other = core_swap(after(first_all, x3))
-    zi_one = z_swap(after(w_in, *zqs[1:]), 2)
-    zw_one = z_swap(after(zw, *zqs[1:]), 2)
-    zi_mine, zi_theirs = call(
-        split_in_kernel, (pos, w_in, zi_one), [sds((48, 1536), BF16)] * 2, name="split_in"
-    )
-    zi_two = z_swap(zi_theirs, 1)
-    zw_pair = jnp.concatenate([zw, zw_one], axis=0)
-    wo_z = after(wo_z, first_all)
-    wo_all = jnp.stack([wo_z] + [chip_swap(wo_z, k) for k in others])
-    wo_other = core_swap(wo_all)
+    first_all = jnp.stack(firsts)
+    first_other = core_swap(after(first_all, x1, x2, x3))
+    bulk = jnp.concatenate([jnp.concatenate([g[:, 640:] for g in got], axis=0), zw], axis=1)
+    bulk_one = z_swap(after(bulk, first_all), 2)
+    wo_z = after(jnp.concatenate([zo_pair, zo_two], axis=0), first_all)
+    wo_far = [chip_swap(wo_z, k) for k in others]
 
     q, kv, wq, vecs, nb = call(
         qkv_kernel,
@@ -628,18 +656,21 @@
         smem_out=(4,),
         name="qkv",
     )
-    kv_other = after(core_swap(kv), zw_pair, zi_theirs)
-    out_two = chip_swap(zw_pair, 2)
+    kv_other = core_swap(kv)
     *attended, ot, lse = call(
         attention_kernel,
         (pos, nb, q, kv, kv_other),
         [sds((256, 192), BF16)] * 4 + [sds((4, 192, 256), F32), sds((4, 8, 256), F32)],
         scratch=[pltpu.VMEM((8, 256, 256), BF16)] * 2 + [pltpu.VMEM((8, 192, 256), BF16)],
         smem_in=(0, 1),
-        flops=1e10,
+        flops=2e9,
         name="attention",
     )
-    attended = lax.optimization_barrier((*attended, wo_other, zi_two))[:4]
+    *attended, wo1, wo2, wo3, bulk_one = lax.optimization_barrier((*attended, *wo_far, bulk_one))
+    wo_all = jnp.stack([wo_z, wo1, wo2, wo3])
+    wo_other = core_swap(wo_all)
+    bulk_pair = jnp.stack([bulk, bulk_one])
+    bulk_two = z_swap(bulk_pair, 1)
     pieces = [attended[0]] + [chip_swap(attended[k], k) for k in others]
     (wo,) = call(join_wo_kernel, (pos, wo_all, wo_other), [sds((768, 768), BF16)], name="join_wo")
     hidden, xhat, rstd = call(
@@ -648,85 +679,91 @@
         [sds((256, 768), BF16), sds((256, 768), F32), sds((256, 1), F32)],
         name="norm_one",
     )
-    hs = (hidden, z_swap(hidden, 1))
-    out_half = after(jnp.stack([zw_pair, out_two]), pieces[1])
-    out_all = jnp.concatenate([out_half, chip_swap(out_half, 1)])
-    out_other = core_swap(out_all)
-    in_one = after(jnp.concatenate([zi_mine, zi_two], axis=0), pieces[1])
-    in_half = jnp.stack([in_one, chip_swap(in_one, 1)])
-    in_all = jnp.concatenate([in_half, chip_swap(in_half, 2)])
-    in_other = core_swap(in_all)
-    (wi,) = call(join_in_kernel, (pos, in_all, in_other), [sds((768, 1536), BF16)], name="join_in")
-    wx, bin_ = call(
-        join_out_kernel,
-        (pos, out_all, out_other),
-        [sds((1536, 896), BF16), sds((8, 1536), F32)],
-        name="join_out",
-    )
-
-    def ff(block, dtype):
-        return call(
-            ff_kernel,
-            (block, wi, wx, bin_),
-            [sds((256, 768), dtype), sds((256, 1536), BF16), sds((256, 1536), F32)],
-            smem_in=(),
-                name="ff",
-        )
-
-    part_own, act_own, slope_own = ff(hs[0], F32)
-    part_far, act_far, slope_far = ff(after(hs[1], part_own), BF16)
+    hx, hy = gather_first(hidden)
+    bulk_all = after(jnp.concatenate([bulk_pair, bulk_two]), hx, hy)
+    wi, wx, bin_ = call(
+        join_ff_kernel,
+        (pos, bulk_all, core_swap(bulk_all)),
+        [sds((768, 768), BF16), sds((768, 896), BF16), sds((8, 768), F32)],
+        name="join_ff",
+    )
+    block, low_block, half = sds((256, 768), F32), sds((256, 768), BF16), sds((128, 768), BF16)
+    ff_sums = sds((8, 768), F32)
+    part_own, act0, slope0 = call(
+        ff_own_kernel,
+        (hidden, wi, wx, bin_),
+        [block, low_block, block],
+        smem_in=(),
+        name="ff_own",
+    )
+    hx = after(hx, part_own)
+    ha, hb = gather_last(hx, hy)
+    part1, part2, act1, act2, slope1, slope2 = call(
+        ff_near_kernel,
+        (hx, hy, wi, wx, bin_),
+        [low_block] * 4 + [block] * 2,
+        smem_in=(),
+        name="ff_near",
+    )
+    ha = after(ha, part1)
+    mx, my, act3, slope3 = call(
+        ff_far_kernel,
+        (ha, hb, part1, part2, wi, wx, bin_),
+        [low_block] * 3 + [block],
+        smem_in=(),
+        name="ff_far",
+    )
     block_out, grad_two_low, grad_two, sums_two = call(
         norm_two_kernel,
-        (vecs, xhat, part_own, z_swap(part_far, 1), cotangent),
-        [sds((256, 768), BF16), sds((256, 768), BF16), sds((256, 768), F32), sds((8, 768), F32)],
+        (vecs, xhat, part_own, *reduce_parts(mx, my, part1, part2), cotangent),
+        [low_block, low_block, block, ff_sums],
         smem_in=(),
         name="norm_two",
     )
-    gs = (grad_two_low, z_swap(grad_two_low, 1))
-
-    def ff_back(block, slope, dtype):
-        return call(
-            ff_back_kernel,
-            (block, slope, wi, wx),
-            [sds((256, 768), dtype), sds((256, 1536), BF16), sds((8, 1536), F32)],
-            smem_in=(),
-                name="ff_back",
-        )
-
-    back_own, pre_own, sum_own = ff_back(gs[0], slope_own, F32)
-    back_far, pre_far, sum_far = ff_back(after(gs[1], back_own), slope_far, BF16)
-    back_got = z_swap(back_far, 1)
-    out_keep, out_send = call(
-        ff_grad_out_kernel,
-        (pos, act_own, act_far, *gs, sum_own, sum_far),
-        [sds((4, 192, 896), BF16)] * 2,
-        scratch=[pltpu.VMEM((1536, 896), F32)],
-        name="ff_grad_out",
-    )
-    in_keep, in_send = call(
-        ff_grad_in_kernel,
-        (pos, *hs, pre_own, pre_far),
-        [sds((4, 96, 1536), BF16)] * 2,
-        scratch=[pltpu.VMEM((768, 1536), F32)],
-        name="ff_grad_in",
-    )
-    out_got, in_got = core_swap(out_send), core_swap(in_send)
-    out_sum = low_add(out_keep, out_got)
-    out_send = out_sum[1::2].astype(BF16)
-    out_part = chip_swap(out_send, 1)
-    out_left = low_add(out_sum[2], out_part[1]).astype(BF16)
-    out_mine = low_add(out_sum[0], out_part[0], chip_swap(out_left, 2))
-    tw = low_add(out_mine[:96], z_swap(out_mine[96:].astype(BF16), 2))
-    in_sum = low_add(in_keep, in_got)
-    in_send_two = in_sum[2:].astype(BF16)
-    in_part = chip_swap(in_send_two, 2)
-    in_left = low_add(in_sum[1], in_part[1]).astype(BF16)
-    in_mine = low_add(in_sum[0], in_part[0], chip_swap(in_left, 1))
-    back_got = after(back_got, out_send, in_send_two)
+    gx, gy = gather_first(grad_two_low)
+    back_own, low0, sum0 = call(
+        ff_back_own_kernel,
+        (grad_two_low, slope0, wi, wx),
+        [block, low_block, ff_sums],
+        smem_in=(),
+        name="ff_back_own",
+    )
+    gx = after(gx, back_own)
+    ga, gb = gather_last(gx, gy)
+    back1, back2, low1, low2, sum1 = call(
+        ff_back_near_kernel,
+        (gx, gy, slope1, slope2, wi, wx),
+        [low_block] * 4 + [ff_sums],
+        smem_in=(),
+        name="ff_back_near",
+    )
+    ga = after(ga, back1)
+    mx, my, low3, sum2 = call(
+        ff_back_far_kernel,
+        (ga, gb, slope3, back1, back2, wi, wx),
+        [low_block] * 3 + [ff_sums],
+        smem_in=(),
+        name="ff_back_far",
+    )
+    rx, ry, sx, sy = reduce_parts(mx, my, back1, back2)
+    ff_keep, ff_send = call(
+        ff_grad_kernel,
+        (pos, hidden, hx, hy, ha, hb, low0, low1, low2, low3, act0, act1, act2, act3)
+        + (grad_two_low, gx, gy, ga, gb, sum0, sum1, sum2),
+        [sds((4, 96, 1664), BF16)] * 2,
+        scratch=[pltpu.VMEM((768, 768), F32), pltpu.VMEM((768, 896), F32)],
+        flops=1e10,
+        name="ff_grad",
+    )
+    sx = after(sx, ff_keep)
+    ff_sum = low_add(ff_keep, core_swap(ff_send))
+    ff_got = z_swap(ff_sum[2:].astype(BF16), 1)
+    ff_left = low_add(ff_sum[1], ff_got[1]).astype(BF16)
+    ff_mine = low_add(ff_sum[0], ff_got[0])
 
     *grad_att, low_one, grad_one, sums_one = call(
         norm_one_kernel,
-        (pos, back_own, back_got, grad_two, xhat, rstd, vecs, wo),
+        (pos, back_own, rx, ry, sx, sy, grad_two, xhat, rstd, vecs, wo),
         [sds((256, 192), BF16)] * 4
         + [sds((256, 768), BF16), sds((256, 768), F32), sds((8, 768), F32)],
         name="norm_one_back",
@@ -743,18 +780,7 @@
     wo_sum = low_add(wo_keep, wo_got)
     wo_low = [wo_sum[k].astype(BF16) for k in others]
     wo_part = [chip_swap(v, k) for v, k in zip(wo_low, others)]
-    zi_sum = jnp.concatenate([in_mine, low_add(wo_sum[0], *wo_part)], axis=1)
-    zi_got = z_swap(zi_sum[48:].astype(BF16), 1)
-    zi_half = jnp.concatenate(
-        [
-            zi_sum[:48, :1536],
-            zi_got[:, :1536].astype(F32),
-            low_add(zi_sum[:48, 1536:], zi_got[:, 1536:]),
-        ],
-        axis=1,
-    )
-    ti = low_add(zi_half[:24], z_swap(zi_half[24:].astype(BF16), 2))
-    grad_pieces = lax.optimization_barrier((*grad_pieces, *wo_low, out_left, in_left))[:4]
+    grad_pieces = lax.optimization_barrier((*grad_pieces, *wo_low))[:4]
 
     dq, dmine, dother = call(
         attention_back_kernel,
@@ -767,13 +793,14 @@
         flops=1e10,
         name="attention_back",
     )
-    dgot = core_swap(dother)
+    dgot = core_swap(after(dother, *wo_part))
+    ff_far = z_swap(after(ff_left, dq), 2)
     in_own, in_x, in_y, in_rest, low, sums_qv = call(
         qkv_back_kernel,
         (dq, dmine, dgot, wq),
         [sds((256, 768), F32)]
         + [sds((256, 768), BF16)] * 2
-        + [sds((2, 128, 768), BF16), sds((4, 256, 640), BF16), sds((8, 256), F32)],
+        + [sds((2, 256, 768), BF16), sds((4, 256, 640), BF16), sds((8, 256), F32)],
         smem_in=(),
         name="qkv_back",
     )
@@ -785,21 +812,35 @@
         name="qkv_grad",
     )
     q_got = core_swap(q_send)
-    q_sum = [low_add(q_keep[i], q_got[i]) for i in range(4)]
-    tq = low_add(q_sum[0], *[z_swap(q_sum[j].astype(BF16), j) for j in others])
-    got_x, got_y = chip_swap(in_x, 1), chip_swap(in_y, 2)
-    last_y = chip_swap(low_add(in_rest[0], got_x[128:]).astype(BF16), 2)
-    last_x = chip_swap(low_add(in_rest[1], got_y[128:]).astype(BF16), 1)
+    wo_mine = low_add(wo_sum[0], *wo_part)
+    tm = low_add(ff_mine, ff_far)
+    q_sum = low_add(q_keep, after(q_got, ff_far))
+    q_next = z_swap(q_sum[2:].astype(BF16), 1)
+    wo_mine = after(wo_mine, q_next)
+    wo_next = z_swap(wo_mine[48:].astype(BF16), 1)
+    wo_left = low_add(wo_mine[24:48], wo_next[24:]).astype(BF16)
+    uo = low_add(wo_mine[:24], wo_next[:24], z_swap(wo_left, 2))
+    q_left = low_add(q_sum[1], q_next[1]).astype(BF16)
+    tq = low_add(q_sum[0], q_next[0], z_swap(q_left, 2))
+    got_x, got_y, last_x, last_y = reduce_parts(in_x, in_y, in_rest[1], in_rest[0])
     input_grad = low_add(
         in_own,
         grad_one,
         jnp.concatenate([got_x[:128], got_y[:128]], axis=0),
         jnp.concatenate([last_y, last_x], axis=0),
     )
-    final = [chip_swap(tq[24 * k : 24 * k + 24].astype(BF16), k) for k in others]
+    final = [
+        chip_swap(
+            jnp.concatenate(
+                [tq[24 * k : 24 * k + 24], tm[24 * k : 24 * k + 24, :768]], axis=1
+            ).astype(BF16),
+            k,
+        )
+        for k in others
+    ]
     gqkv, gbqv, gwo, gbo, gain, shift, gwin, gbin, gwout, gbout = call(
         finish_kernel,
-        (pos, tq, *final, ti, tw),
+        (pos, tq, tm, *final, uo),
         [
             sds((24, 2304), F32),
             sds((2, 24), F32),

time: 232 us -> 215 us (0.927)
  starting transfers between devices: 78.8 us -> 65 us
  waiting for transfers between devices: 101 us -> 97.6 us
    ppermute x16 -> x13, waiting for transfers between devices: 56.4 us -> 37 us  [z_swap(): return lax.ppermute(value, 'dp', [(i, i ^ j) for i in range(4)])]
    ppermute x33 -> x41, waiting for transfers between devices: 42.7 us -> 55.7 us  [chip_swap(): return lax.ppermute(value, 'seq', [(s, s ^ 2 * k) for s in range(8)])]
    ppermute x33 -> x41, starting transfers between devices: 51.1 us -> 44.4 us  [chip_swap(): return lax.ppermute(value, 'seq', [(s, s ^ 2 * k) for s in range(8)])]
    ppermute x16 -> x13, starting transfers between devices: 24.4 us -> 18.8 us  [z_swap(): return lax.ppermute(value, 'dp', [(i, i ^ j) for i in range(4)])]
    ppermute x10 -> x8, waiting for transfers between devices: 1.87 us -> 4.84 us  [core_swap(): return lax.ppermute(value, 'seq', [(s, s ^ 1) for s in range(8)])]
    pallas_call x22 -> x20, Pallas kernels: 43.2 us -> 42.9 us  [call(): pl.pallas_call(kernel, out_shape=tuple(outs), in_specs=[space(i in smem_i...]
  transfers between devices with their start and end apart: 59 -> 62, of which waited for: 27 -> 35; matrix products, arithmetic and copies ran while one was open for 2% -> 2% of each run, Pallas kernels for 14% -> 17%
where the time goes in v4:
time: 215 us
  waiting for transfers between devices  97.6 us (45%)
  starting transfers between devices  65 us (30%)
  Pallas kernels  42.9 us (20%)
  other arithmetic  4.99 us (2%)
  local copies, waits for them, and re-layouts  3.03 us (1%)
    ppermute x41, waiting for transfers between devices, chip_swap(): return lax.ppermute(value, 'seq', [(s, s ^ 2 * k) for s in range(8)])  55.7 us
    ppermute x41, starting transfers between devices, chip_swap(): return lax.ppermute(value, 'seq', [(s, s ^ 2 * k) for s in range(8)])  44.4 us
    pallas_call x20, Pallas kernels, call(): pl.pallas_call(kernel, out_shape=tuple(outs), in_specs=[space(i in smem_i...  42.9 us
    ppermute x13, waiting for transfers between devices, z_swap(): return lax.ppermute(value, 'dp', [(i, i ^ j) for i in range(4)])  37 us
    ppermute x13, starting transfers between devices, z_swap(): return lax.ppermute(value, 'dp', [(i, i ^ j) for i in range(4)])  18.8 us
    ppermute x8, waiting for transfers between devices, core_swap(): return lax.ppermute(value, 'seq', [(s, s ^ 1) for s in range(8)])  4.84 us
  transfers between devices with their start and end apart: 62, of which 35 were waited for; matrix products, arithmetic and copies ran while one was open for 2% of the time, Pallas kernels for 17%

profile of v4, /device:TPU:0, one launch (start us, length us, event | category | flops | bytes accessed | tf_op | source)
XLA Modules:
  0.0 214.8 jit_solution(4509296996550867241)
XLA Ops:
  0.7 4.1 %collective-permute-start.3 = (bf16[24,768]{1,0:T(8,128)(2,1)}, bf16[24,768]{1,0:T(8,128)(2,1)S(1)}, u32[]{:S(2)}, u32[]{:S(2)}) collective-permute-start(bf16[24,768]{1,0:T(8,128)(2,1)} %param.18), channel_id=1, source_target_pairs={{0,16},{8,24},{16,0},{24,8},{1,17},{9,25},{17,1},{25,9},{2,18},{10... | collective-permute-start | bytes 110600 | tf_op jit(solution)/shard_map/ppermute | solution.py:566
  18.7 2.4 %collective-permute-done.4 = bf16[48,768]{1,0:T(8,128)(2,1)S(1)} collective-permute-done((bf16[48,768]{1,0:T(8,128)(2,1)S(1)}, bf16[48,768]{1,0:T(8,128)(2,1)S(1)}, u32[]{:S(2)}, u32[]{:S(2)}) %collective-permute-start.4) | collective-permute-done | bytes 73760 | tf_op jit(solution)/shard_map/ppermute | solution.py:566
  23.0 3.9 %collective-permute-done.5 = bf16[96,640]{1,0:T(8,128)(2,1)S(1)} collective-permute-done((bf16[96,640]{1,0:T(8,128)(2,1)S(1)}, bf16[96,640]{1,0:T(8,128)(2,1)S(1)}, u32[]{:S(2)}, u32[]{:S(2)}) %collective-permute-start.5) | collective-permute-done | bytes 122912 | tf_op jit(solution)/shard_map/ppermute | solution.py:566
  27.3 3.9 %collective-permute-done.6 = bf16[96,640]{1,0:T(8,128)(2,1)S(1)} collective-permute-done((bf16[96,640]{1,0:T(8,128)(2,1)S(1)}, bf16[96,640]{1,0:T(8,128)(2,1)S(1)}, u32[]{:S(2)}, u32[]{:S(2)}) %collective-permute-start.6) | collective-permute-done | bytes 122912 | tf_op jit(solution)/shard_map/ppermute | solution.py:566
  31.3 2.4 %collective-permute-done.7 = bf16[96,640]{1,0:T(8,128)(2,1)S(1)} collective-permute-done((bf16[96,640]{1,0:T(8,128)(2,1)S(1)}, bf16[96,640]{1,0:T(8,128)(2,1)S(1)}, u32[]{:S(2)}, u32[]{:S(2)}) %collective-permute-start.7) | collective-permute-done | bytes 122912 | tf_op jit(solution)/shard_map/ppermute | solution.py:566
  42.3 7.8 %attention.1 = (bf16[256,192]{1,0:T(8,128)(2,1)S(1)}, bf16[256,192]{1,0:T(8,128)(2,1)S(1)}, bf16[256,192]{1,0:T(8,128)(2,1)S(1)}, bf16[256,192]{1,0:T(8,128)(2,1...) custom-call(s32[1]{0:T(128)} %bitcast.pos, s32[1]{0:T(128)} %get-tuple-element.132.nb, ...), custom_call_target="tpu_custom_call" | custom-call | flops 2000000000 | bytes 1 | tf_op jit(solution)/shard_map/attention/pallas_call | solution.py:36
  50.1 5.6 %collective-permute-done.16 = bf16[96,1664]{1,0:T(8,128)(2,1)S(1)} collective-permute-done((bf16[96,1664]{1,0:T(8,128)(2,1)S(1)}, bf16[96,1664]{1,0:T(8,128)(2,1)S(1)}, u32[]{:S(2)}, u32[]{:S(2)}) %collective-permute-start.16) | collective-permute-done | bytes 319520 | tf_op jit(solution)/shard_map/ppermute | solution.py:566
  59.7 2.7 %collective-permute-done.17.a1 = bf16[256,192]{1,0:T(8,128)(2,1)S(1)} collective-permute-done((bf16[256,192]{1,0:T(8,128)(2,1)S(1)}, bf16[256,192]{1,0:T(8,128)(2,1)S(1)}, u32[]{:S(2)}, u32[]{:S(2)}) %collective-permute-start.17) | collective-permute-done | bytes 98336 | tf_op jit(solution)/shard_map/ppermute | solution.py:554
  62.4 2.7 %collective-permute-done.18.a2 = bf16[256,192]{1,0:T(8,128)(2,1)S(1)} collective-permute-done((bf16[256,192]{1,0:T(8,128)(2,1)S(1)}, bf16[256,192]{1,0:T(8,128)(2,1)S(1)}, u32[]{:S(2)}, u32[]{:S(2)}) %collective-permute-start.18) | collective-permute-done | bytes 98336 | tf_op jit(solution)/shard_map/ppermute | solution.py:554
  68.2 4.6 %collective-permute-done.21 = bf16[2,96,1664]{2,1,0:T(8,128)(2,1)S(1)} collective-permute-done((bf16[2,96,1664]{2,1,0:T(8,128)(2,1)S(1)}, bf16[2,96,1664]{2,1,0:T(8,128)(2,1)S(1)}, u32[]{:S(2)}, u32[]{:S(2)}) %collective-permute-start.21) | collective-permute-done | bytes 639008 | tf_op jit(solution)/shard_map/ppermute | solution.py:566
  73.0 3.7 %collective-permute-done.22.h1 = bf16[256,768]{1,0:T(8,128)(2,1)S(1)} collective-permute-done((bf16[256,768]{1,0:T(8,128)(2,1)S(1)}, bf16[256,768]{1,0:T(8,128)(2,1)S(1)}, u32[]{:S(2)}, u32[]{:S(2)}) %collective-permute-start.22) | collective-permute-done | bytes 393248 | tf_op jit(solution)/shard_map/ppermute | solution.py:554
  85.0 4.3 %collective-permute-done.26.hb = bf16[128,768]{1,0:T(8,128)(2,1)S(1)} collective-permute-done((bf16[128,768]{1,0:T(8,128)(2,1)S(1)}, bf16[128,768]{1,0:T(8,128)(2,1)S(1)}, u32[]{:S(2)}, u32[]{:S(2)}) %collective-permute-start.26) | collective-permute-done | bytes 196640 | tf_op jit(solution)/shard_map/ppermute | solution.py:554
  92.6 8.3 %collective-permute-done.27.rx = bf16[256,768]{1,0:T(8,128)(2,1)S(1)} collective-permute-done((bf16[256,768]{1,0:T(8,128)(2,1)S(1)}, bf16[256,768]{1,0:T(8,128)(2,1)S(1)}, u32[]{:S(2)}, u32[]{:S(2)}) %collective-permute-start.27) | collective-permute-done | bytes 393248 | tf_op jit(solution)/shard_map/ppermute | solution.py:554
  103.1 3.5 %collective-permute-done.30.sy = bf16[128,768]{1,0:T(8,128)(2,1)S(1)} collective-permute-done((bf16[128,768]{1,0:T(8,128)(2,1)S(1)}, bf16[128,768]{1,0:T(8,128)(2,1)S(1)}, u32[]{:S(2)}, u32[]{:S(2)}) %collective-permute-start.30) | collective-permute-done | bytes 196640 | tf_op jit(solution)/shard_map/ppermute | solution.py:554
  112.2 4.7 %collective-permute-done.31.g2 = bf16[256,768]{1,0:T(8,128)(2,1)S(1)} collective-permute-done((bf16[256,768]{1,0:T(8,128)(2,1)S(1)}, bf16[256,768]{1,0:T(8,128)(2,1)S(1)}, u32[]{:S(2)}, u32[]{:S(2)}) %collective-permute-start.31) | collective-permute-done | bytes 393248 | tf_op jit(solution)/shard_map/ppermute | solution.py:554
  116.8 2.6 %collective-permute-start.32 = (bf16[128,768]{1,0:T(8,128)(2,1)S(1)}, bf16[128,768]{1,0:T(8,128)(2,1)S(1)}, u32[]{:S(2)}, u32[]{:S(2)}) collective-permute-start(bf16[128,768]{1,0:T(8,128)(2,1)S(1)} %slice.236), channel_id=1, source_target_pairs={{0,2},{1,3},{2,0},{3,1},{4,6},{5,7},{6,4},{7,5},{8,10},{9,11},{10,... | collective-permute-start | bytes 589832 | tf_op jit(solution)/shard_map/ppermute | solution.py:554
  123.0 4.9 %collective-permute-done.34.gb = bf16[128,768]{1,0:T(8,128)(2,1)S(1)} collective-permute-done((bf16[128,768]{1,0:T(8,128)(2,1)S(1)}, bf16[128,768]{1,0:T(8,128)(2,1)S(1)}, u32[]{:S(2)}, u32[]{:S(2)}) %collective-permute-start.34) | collective-permute-done | bytes 196640 | tf_op jit(solution)/shard_map/ppermute | solution.py:554
  130.9 8.0 %collective-permute-done.35.rx = bf16[256,768]{1,0:T(8,128)(2,1)S(1)} collective-permute-done((bf16[256,768]{1,0:T(8,128)(2,1)S(1)}, bf16[256,768]{1,0:T(8,128)(2,1)S(1)}, u32[]{:S(2)}, u32[]{:S(2)}) %collective-permute-start.35) | collective-permute-done | bytes 393248 | tf_op jit(solution)/shard_map/ppermute | solution.py:554
  141.1 3.7 %ff_grad.1 = (bf16[4,96,1664]{2,1,0:T(8,128)(2,1)S(1)}, bf16[4,96,1664]{2,1,0:T(8,128)(2,1)S(1)}) custom-call(s32[1]{0:T(128)} %bitcast.pos, bf16[256,768]{1,0:T(8,128)(2,1)S(1)} %get-tuple-element.150.h.h0, bf16[256,768]{1,0:T(8,128)(2,1)S(1)} %collective-permute-done.22.h1, bf16[256,768]{1,0:T(8,128)(2,1)S(1)} %collective-permute-done.23.h2, ...), custom_call_target="tpu_custom_call" | custom-call | flops 10000000000 | bytes 1 | tf_op jit(solution)/shard_map/ff_grad/pallas_call | solution.py:36
  159.5 11.5 %attention_back.1 = (f32[4,256,192]{2,1,0:T(8,128)S(1)}, f32[4,256,512]{2,1,0:T(8,128)S(1)}, bf16[4,256,512]{2,1,0:T(8,128)(2,1)S(1)}) custom-call(s32[1]{0:T(128)} %bitcast.pos, s32[1]{0:T(128)} %get-tuple-element.132.nb, bf16[4,256,256]{2,1,0:T(8,128)(2,1)S(1)} %get-tuple-element.133.q, bf16[4,256,512]{2,1,0:T(8,128)(2,1)S(1)} %get-tuple-element.134.mine, ...), custom_call_target="tpu_custom_call" | custom-call | flops 10000000000 | bytes 1 | tf_op jit(solution)/shard_map/attention_back/pallas_call | solution.py:36
  178.3 10.4 %collective-permute-done.54 = bf16[96,1664]{1,0:T(8,128)(2,1)S(1)} collective-permute-done((bf16[96,1664]{1,0:T(8,128)(2,1)S(1)}, bf16[96,1664]{1,0:T(8,128)(2,1)S(1)}, u32[]{:S(2)}, u32[]{:S(2)}) %collective-permute-start.54) | collective-permute-done | bytes 319520 | tf_op jit(solution)/shard_map/ppermute | solution.py:566
  191.8 4.1 %collective-permute-done.49 = bf16[128,768]{1,0:T(8,128)(2,1)S(1)} collective-permute-done((bf16[128,768]{1,0:T(8,128)(2,1)S(1)}, bf16[128,768]{1,0:T(8,128)(2,1)S(1)}, u32[]{:S(2)}, u32[]{:S(2)}) %collective-permute-start.49) | collective-permute-done | bytes 196640 | tf_op jit(solution)/shard_map/ppermute | solution.py:554
  198.8 3.0 %collective-permute-start.56 = (bf16[96,640]{1,0:T(8,128)(2,1)S(1)}, bf16[96,640]{1,0:T(8,128)(2,1)S(1)}, u32[]{:S(2)}, u32[]{:S(2)}) collective-permute-start(bf16[96,640]{1,0:T(8,128)(2,1)S(1)} %fusion.12), channel_id=1, source_target_pairs={{0,16},{8,24},{16,0},{24,8},{1,17},{9,25},{17,1},{25,9},{2,18},{10... | collective-permute-start | bytes 368648 | tf_op jit(solution)/shard_map/ppermute | solution.py:566
  202.2 2.7 %collective-permute-start.61 = (bf16[24,896]{1,0:T(8,128)(2,1)S(1)}, bf16[24,896]{1,0:T(8,128)(2,1)S(1)}, u32[]{:S(2)}, u32[]{:S(2)}) collective-permute-start(bf16[24,896]{1,0:T(8,128)(2,1)S(1)} %add_convert_fusion.4), channel_id=1, source_target_pairs={{0,16},{8,24},{16,0},{24,8},{1,17},{9,25},{17,1},{25,9},{2,18},{10... | collective-permute-start | bytes 129032 | tf_op jit(solution)/shard_map/ppermute | solution.py:566
  (183 shorter events, 98.1 us)
Async XLA Ops:
  0.7 12.1 %collective-permute-start.3 = (bf16[24,768]{1,0:T(8,128)(2,1)}, bf16[24,768]{1,0:T(8,128)(2,1)S(1)}, u32[]{:S(2)}, u32[]{:S(2)}) collective-permute-start(bf16[24,768]{1,0:T(8,128)(2,1)} %param.18), channel_id=1, source_target_pairs={{0,16},{8,24},{16,0},{24,8},{1,17},{9,25},{17,1},{25,9},{2,18},{10... | collective-permute-start | bytes 110600 | tf_op jit(solution)/shard_map/ppermute | solution.py:566
  12.8 21.0 %collective-permute-start.8 = (bf16[256,768]{1,0:T(8,128)(2,1)}, bf16[256,768]{1,0:T(8,128)(2,1)S(1)}, u32[]{:S(2)}, u32[]{:S(2)}) collective-permute-start(bf16[256,768]{1,0:T(8,128)(2,1)} %x0.3), channel_id=1, source_target_pairs={{0,2},{1,3},{2,0},{3,1},{4,6},{5,7},{6,4},{7,5},{8,10},{9,11},{10,... | collective-permute-start | bytes 1179656 | tf_op jit(solution)/shard_map/ppermute | solution.py:554
  14.3 19.5 %collective-permute-start.9 = (bf16[256,768]{1,0:T(8,128)(2,1)}, bf16[256,768]{1,0:T(8,128)(2,1)S(1)}, u32[]{:S(2)}, u32[]{:S(2)}) collective-permute-start(bf16[256,768]{1,0:T(8,128)(2,1)} %x0.3), channel_id=1, source_target_pairs={{0,4},{1,5},{2,6},{3,7},{4,0},{5,1},{6,2},{7,3},{8,12},{9,13},{10,... | collective-permute-start | bytes 1179656 | tf_op jit(solution)/shard_map/ppermute | solution.py:554
  18.2 15.5 %collective-permute-start.10 = (bf16[256,768]{1,0:T(8,128)(2,1)}, bf16[256,768]{1,0:T(8,128)(2,1)S(1)}, u32[]{:S(2)}, u32[]{:S(2)}) collective-permute-start(bf16[256,768]{1,0:T(8,128)(2,1)} %x0.3), channel_id=1, source_target_pairs={{0,6},{1,7},{2,4},{3,5},{4,2},{5,3},{6,0},{7,1},{8,14},{9,15},{10,... | collective-permute-start | bytes 1179656 | tf_op jit(solution)/shard_map/ppermute | solution.py:554
  38.1 17.6 %collective-permute-start.16 = (bf16[96,1664]{1,0:T(8,128)(2,1)S(1)}, bf16[96,1664]{1,0:T(8,128)(2,1)S(1)}, u32[]{:S(2)}, u32[]{:S(2)}) collective-permute-start(bf16[96,1664]{1,0:T(8,128)(2,1)S(1)} %pad_maximum_fusion.4), channel_id=1, source_target_pairs={{0,16},{8,24},{16,0},{24,8},{1,17},{9,25},{17,1},{25,9},{2,18},{10... | collective-permute-start | bytes 958472 | tf_op jit(solution)/shard_map/ppermute | solution.py:566
  38.7 11.4 %collective-permute-start.13 = (bf16[96,768]{1,0:T(8,128)(2,1)S(1)}, bf16[96,768]{1,0:T(8,128)(2,1)S(1)}, u32[]{:S(2)}, u32[]{:S(2)}) collective-permute-start(bf16[96,768]{1,0:T(8,128)(2,1)S(1)} %pad_maximum_fusion.5), channel_id=1, source_target_pairs={{0,2},{1,3},{2,0},{3,1},{4,6},{5,7},{6,4},{7,5},{8,10},{9,11},{10,... | collective-permute-start | bytes 442376 | tf_op jit(solution)/shard_map/ppermute | solution.py:554
  39.4 10.7 %collective-permute-start.14 = (bf16[96,768]{1,0:T(8,128)(2,1)S(1)}, bf16[96,768]{1,0:T(8,128)(2,1)S(1)}, u32[]{:S(2)}, u32[]{:S(2)}) collective-permute-start(bf16[96,768]{1,0:T(8,128)(2,1)S(1)} %pad_maximum_fusion.5), channel_id=1, source_target_pairs={{0,4},{1,5},{2,6},{3,7},{4,0},{5,1},{6,2},{7,3},{8,12},{9,13},{10,... | collective-permute-start | bytes 442376 | tf_op jit(solution)/shard_map/ppermute | solution.py:554
  40.0 10.1 %collective-permute-start.15 = (bf16[96,768]{1,0:T(8,128)(2,1)S(1)}, bf16[96,768]{1,0:T(8,128)(2,1)S(1)}, u32[]{:S(2)}, u32[]{:S(2)}) collective-permute-start(bf16[96,768]{1,0:T(8,128)(2,1)S(1)} %pad_maximum_fusion.5), channel_id=1, source_target_pairs={{0,6},{1,7},{2,4},{3,5},{4,2},{5,3},{6,0},{7,1},{8,14},{9,15},{10,... | collective-permute-start | bytes 442376 | tf_op jit(solution)/shard_map/ppermute | solution.py:554
  56.0 16.8 %collective-permute-start.21 = (bf16[2,96,1664]{2,1,0:T(8,128)(2,1)S(1)}, bf16[2,96,1664]{2,1,0:T(8,128)(2,1)S(1)}, u32[]{:S(2)}, u32[]{:S(2)}) collective-permute-start(bf16[2,96,1664]{2,1,0:T(8,128)(2,1)S(1)} %pad_maximum_fusion.1), channel_id=1, source_target_pairs={{0,8},{8,0},{16,24},{24,16},{1,9},{9,1},{17,25},{25,17},{2,10},{10... | collective-permute-start | bytes 1916936 | tf_op jit(solution)/shard_map/ppermute | solution.py:566
  66.0 10.7 %collective-permute-start.22 = (bf16[256,768]{1,0:T(8,128)(2,1)S(1)}, bf16[256,768]{1,0:T(8,128)(2,1)S(1)}, u32[]{:S(2)}, u32[]{:S(2)}) collective-permute-start(bf16[256,768]{1,0:T(8,128)(2,1)S(1)} %get-tuple-element.150.h.h0), channel_id=1, source_target_pairs={{0,2},{1,3},{2,0},{3,1},{4,6},{5,7},{6,4},{7,5},{8,10},{9,11},{10,... | collective-permute-start | bytes 1179656 | tf_op jit(solution)/shard_map/ppermute | solution.py:554
  67.4 10.1 %collective-permute-start.23 = (bf16[256,768]{1,0:T(8,128)(2,1)S(1)}, bf16[256,768]{1,0:T(8,128)(2,1)S(1)}, u32[]{:S(2)}, u32[]{:S(2)}) collective-permute-start(bf16[256,768]{1,0:T(8,128)(2,1)S(1)} %get-tuple-element.150.h.h0), channel_id=1, source_target_pairs={{0,4},{1,5},{2,6},{3,7},{4,0},{5,1},{6,2},{7,3},{8,12},{9,13},{10,... | collective-permute-start | bytes 1179656 | tf_op jit(solution)/shard_map/ppermute | solution.py:554
  90.5 10.4 %collective-permute-start.27 = (bf16[256,768]{1,0:T(8,128)(2,1)S(1)}, bf16[256,768]{1,0:T(8,128)(2,1)S(1)}, u32[]{:S(2)}, u32[]{:S(2)}) collective-permute-start(bf16[256,768]{1,0:T(8,128)(2,1)S(1)} %get-tuple-element.161), channel_id=1, source_target_pairs={{0,2},{1,3},{2,0},{3,1},{4,6},{5,7},{6,4},{7,5},{8,10},{9,11},{10,... | collective-permute-start | bytes 1179656 | tf_op jit(solution)/shard_map/ppermute | solution.py:554
  91.4 10.1 %collective-permute-start.28 = (bf16[256,768]{1,0:T(8,128)(2,1)S(1)}, bf16[256,768]{1,0:T(8,128)(2,1)S(1)}, u32[]{:S(2)}, u32[]{:S(2)}) collective-permute-start(bf16[256,768]{1,0:T(8,128)(2,1)S(1)} %get-tuple-element.162), channel_id=1, source_target_pairs={{0,4},{1,5},{2,6},{3,7},{4,0},{5,1},{6,2},{7,3},{8,12},{9,13},{10,... | collective-permute-start | bytes 1179656 | tf_op jit(solution)/shard_map/ppermute | solution.py:554
  110.3 10.1 %collective-permute-start.33 = (bf16[256,768]{1,0:T(8,128)(2,1)S(1)}, bf16[256,768]{1,0:T(8,128)(2,1)S(1)}, u32[]{:S(2)}, u32[]{:S(2)}) collective-permute-start(bf16[256,768]{1,0:T(8,128)(2,1)S(1)} %get-tuple-element.164.g.g0), channel_id=1, source_target_pairs={{0,2},{1,3},{2,0},{3,1},{4,6},{5,7},{6,4},{7,5},{8,10},{9,11},{10,... | collective-permute-start | bytes 1179656 | tf_op jit(solution)/shard_map/ppermute | solution.py:554
  129.0 9.9 %collective-permute-start.35 = (bf16[256,768]{1,0:T(8,128)(2,1)S(1)}, bf16[256,768]{1,0:T(8,128)(2,1)S(1)}, u32[]{:S(2)}, u32[]{:S(2)}) collective-permute-start(bf16[256,768]{1,0:T(8,128)(2,1)S(1)} %get-tuple-element.174), channel_id=1, source_target_pairs={{0,2},{1,3},{2,0},{3,1},{4,6},{5,7},{6,4},{7,5},{8,10},{9,11},{10,... | collective-permute-start | bytes 1179656 | tf_op jit(solution)/shard_map/ppermute | solution.py:554
  129.0 10.0 %collective-permute-start.36 = (bf16[256,768]{1,0:T(8,128)(2,1)S(1)}, bf16[256,768]{1,0:T(8,128)(2,1)S(1)}, u32[]{:S(2)}, u32[]{:S(2)}) collective-permute-start(bf16[256,768]{1,0:T(8,128)(2,1)S(1)} %get-tuple-element.175), channel_id=1, source_target_pairs={{0,4},{1,5},{2,6},{3,7},{4,0},{5,1},{6,2},{7,3},{8,12},{9,13},{10,... | collective-permute-start | bytes 1179656 | tf_op jit(solution)/shard_map/ppermute | solution.py:554
  151.3 19.7 %collective-permute-start.43 = (bf16[96,896]{1,0:T(8,128)(2,1)S(1)}, bf16[96,896]{1,0:T(8,128)(2,1)S(1)}, u32[]{:S(2)}, u32[]{:S(2)}) collective-permute-start(bf16[96,896]{1,0:T(8,128)(2,1)S(1)} %get-tuple-element.244), channel_id=1, source_target_pairs={{0,2},{1,3},{2,0},{3,1},{4,6},{5,7},{6,4},{7,5},{8,10},{9,11},{10,... | collective-permute-start | bytes 516104 | tf_op jit(solution)/shard_map/ppermute | solution.py:554
  152.8 18.1 %collective-permute-start.44 = (bf16[96,896]{1,0:T(8,128)(2,1)S(1)}, bf16[96,896]{1,0:T(8,128)(2,1)S(1)}, u32[]{:S(2)}, u32[]{:S(2)}) collective-permute-start(bf16[96,896]{1,0:T(8,128)(2,1)S(1)} %get-tuple-element.243), channel_id=1, source_target_pairs={{0,4},{1,5},{2,6},{3,7},{4,0},{5,1},{6,2},{7,3},{8,12},{9,13},{10,... | collective-permute-start | bytes 516104 | tf_op jit(solution)/shard_map/ppermute | solution.py:554
  153.8 17.2 %collective-permute-start.45 = (bf16[96,896]{1,0:T(8,128)(2,1)S(1)}, bf16[96,896]{1,0:T(8,128)(2,1)S(1)}, u32[]{:S(2)}, u32[]{:S(2)}) collective-permute-start(bf16[96,896]{1,0:T(8,128)(2,1)S(1)} %get-tuple-element.242), channel_id=1, source_target_pairs={{0,6},{1,7},{2,4},{3,5},{4,2},{5,3},{6,0},{7,1},{8,14},{9,15},{10,... | collective-permute-start | bytes 516104 | tf_op jit(solution)/shard_map/ppermute | solution.py:554
  157.5 15.1 %collective-permute-start.53 = (bf16[2,96,1664]{2,1,0:T(8,128)(2,1)S(1)}, bf16[2,96,1664]{2,1,0:T(8,128)(2,1)S(1)}, u32[]{:S(2)}, u32[]{:S(2)}) collective-permute-start(bf16[2,96,1664]{2,1,0:T(8,128)(2,1)S(1)} %slice.320), channel_id=1, source_target_pairs={{0,8},{8,0},{16,24},{24,16},{1,9},{9,1},{17,25},{25,17},{2,10},{10... | collective-permute-start | bytes 1916936 | tf_op jit(solution)/shard_map/ppermute | solution.py:566
  172.7 16.1 %collective-permute-start.54 = (bf16[96,1664]{1,0:T(8,128)(2,1)S(1)}, bf16[96,1664]{1,0:T(8,128)(2,1)S(1)}, u32[]{:S(2)}, u32[]{:S(2)}) collective-permute-start(bf16[96,1664]{1,0:T(8,128)(2,1)S(1)} %fusion.8), channel_id=1, source_target_pairs={{0,16},{8,24},{16,0},{24,8},{1,17},{9,25},{17,1},{25,9},{2,18},{10... | collective-permute-start | bytes 958472 | tf_op jit(solution)/shard_map/ppermute | solution.py:566
  176.8 13.8 %collective-permute-start.51 = (bf16[4,96,640]{2,1,0:T(8,128)(2,1)S(1)}, bf16[4,96,640]{2,1,0:T(8,128)(2,1)S(1)}, u32[]{:S(2)}, u32[]{:S(2)}) collective-permute-start(bf16[4,96,640]{2,1,0:T(8,128)(2,1)S(1)} %get-tuple-element.219), channel_id=1, source_target_pairs={{0,1},{1,0},{2,3},{3,2},{4,5},{5,4},{6,7},{7,6},{8,9},{9,8},{10,11... | collective-permute-start | bytes 1474568 | tf_op jit(solution)/shard_map/ppermute | solution.py:558
  177.3 11.6 %collective-permute-start.47 = (bf16[256,768]{1,0:T(8,128)(2,1)S(1)}, bf16[256,768]{1,0:T(8,128)(2,1)S(1)}, u32[]{:S(2)}, u32[]{:S(2)}) collective-permute-start(bf16[256,768]{1,0:T(8,128)(2,1)S(1)} %get-tuple-element.213), channel_id=1, source_target_pairs={{0,2},{1,3},{2,0},{3,1},{4,6},{5,7},{6,4},{7,5},{8,10},{9,11},{10,... | collective-permute-start | bytes 1179656 | tf_op jit(solution)/shard_map/ppermute | solution.py:554
  177.3 11.6 %collective-permute-start.48 = (bf16[256,768]{1,0:T(8,128)(2,1)S(1)}, bf16[256,768]{1,0:T(8,128)(2,1)S(1)}, u32[]{:S(2)}, u32[]{:S(2)}) collective-permute-start(bf16[256,768]{1,0:T(8,128)(2,1)S(1)} %get-tuple-element.214), channel_id=1, source_target_pairs={{0,4},{1,5},{2,6},{3,7},{4,0},{5,1},{6,2},{7,3},{8,12},{9,13},{10,... | collective-permute-start | bytes 1179656 | tf_op jit(solution)/shard_map/ppermute | solution.py:554
  (44 other events, 291.0 us)

commit v5 on v4

--- a/solution.py
+++ b/solution.py
@@ -696,8 +696,8 @@
         smem_in=(),
         name="ff_own",
     )
+    ha, hb = gather_last(hx, hy)
     hx = after(hx, part_own)
-    ha, hb = gather_last(hx, hy)
     part1, part2, act1, act2, slope1, slope2 = call(
         ff_near_kernel,
         (hx, hy, wi, wx, bin_),
@@ -728,8 +728,8 @@
         smem_in=(),
         name="ff_back_own",
     )
+    ga, gb = gather_last(gx, gy)
     gx = after(gx, back_own)
-    ga, gb = gather_last(gx, gy)
     back1, back2, low1, low2, sum1 = call(
         ff_back_near_kernel,
         (gx, gy, slope1, slope2, wi, wx),

time: 215 us -> 212 us (0.986)
    ppermute x8, waiting for transfers between devices: 4.84 us -> 2.63 us  [core_swap(): return lax.ppermute(value, 'seq', [(s, s ^ 1) for s in range(8)])]
  transfers between devices with their start and end apart: 62 -> 62, of which waited for: 35 -> 37; matrix products, arithmetic and copies ran while one was open for 2% -> 2% of each run, Pallas kernels for 17% -> 16%
where the time goes in v5:
time: 212 us
  waiting for transfers between devices  95.9 us (45%)
  starting transfers between devices  66.4 us (31%)
  Pallas kernels  40.8 us (19%)
  other arithmetic  4.99 us (2%)
  local copies, waits for them, and re-layouts  3.03 us (1%)
    ppermute x41, waiting for transfers between devices, chip_swap(): return lax.ppermute(value, 'seq', [(s, s ^ 2 * k) for s in range(8)])  55.1 us
    ppermute x41, starting transfers between devices, chip_swap(): return lax.ppermute(value, 'seq', [(s, s ^ 2 * k) for s in range(8)])  45.1 us
    pallas_call x20, Pallas kernels, call(): pl.pallas_call(kernel, out_shape=tuple(outs), in_specs=[space(i in smem_i...  40.8 us
    ppermute x13, waiting for transfers between devices, z_swap(): return lax.ppermute(value, 'dp', [(i, i ^ j) for i in range(4)])  38.1 us
    ppermute x13, starting transfers between devices, z_swap(): return lax.ppermute(value, 'dp', [(i, i ^ j) for i in range(4)])  20.7 us
  transfers between devices with their start and end apart: 62, of which 37 were waited for; matrix products, arithmetic and copies ran while one was open for 2% of the time, Pallas kernels for 16%

profile of v5, /device:TPU:0, one launch (start us, length us, event | category | flops | bytes accessed | tf_op | source)
XLA Modules:
  0.0 212.2 jit_solution(12450153466199888646)
XLA Ops:
  0.7 4.1 %collective-permute-start.3 = (bf16[24,768]{1,0:T(8,128)(2,1)}, bf16[24,768]{1,0:T(8,128)(2,1)S(1)}, u32[]{:S(2)}, u32[]{:S(2)}) collective-permute-start(bf16[24,768]{1,0:T(8,128)(2,1)} %param.18), channel_id=1, source_target_pairs={{0,16},{8,24},{16,0},{24,8},{1,17},{9,25},{17,1},{25,9},{2,18},{10... | collective-permute-start | bytes 110600 | tf_op jit(solution)/shard_map/ppermute | solution.py:566
  18.7 2.4 %collective-permute-done.4 = bf16[48,768]{1,0:T(8,128)(2,1)S(1)} collective-permute-done((bf16[48,768]{1,0:T(8,128)(2,1)S(1)}, bf16[48,768]{1,0:T(8,128)(2,1)S(1)}, u32[]{:S(2)}, u32[]{:S(2)}) %collective-permute-start.4) | collective-permute-done | bytes 73760 | tf_op jit(solution)/shard_map/ppermute | solution.py:566
  23.0 3.9 %collective-permute-done.5 = bf16[96,640]{1,0:T(8,128)(2,1)S(1)} collective-permute-done((bf16[96,640]{1,0:T(8,128)(2,1)S(1)}, bf16[96,640]{1,0:T(8,128)(2,1)S(1)}, u32[]{:S(2)}, u32[]{:S(2)}) %collective-permute-start.5) | collective-permute-done | bytes 122912 | tf_op jit(solution)/shard_map/ppermute | solution.py:566
  27.3 3.9 %collective-permute-done.6 = bf16[96,640]{1,0:T(8,128)(2,1)S(1)} collective-permute-done((bf16[96,640]{1,0:T(8,128)(2,1)S(1)}, bf16[96,640]{1,0:T(8,128)(2,1)S(1)}, u32[]{:S(2)}, u32[]{:S(2)}) %collective-permute-start.6) | collective-permute-done | bytes 122912 | tf_op jit(solution)/shard_map/ppermute | solution.py:566
  31.3 2.4 %collective-permute-done.7 = bf16[96,640]{1,0:T(8,128)(2,1)S(1)} collective-permute-done((bf16[96,640]{1,0:T(8,128)(2,1)S(1)}, bf16[96,640]{1,0:T(8,128)(2,1)S(1)}, u32[]{:S(2)}, u32[]{:S(2)}) %collective-permute-start.7) | collective-permute-done | bytes 122912 | tf_op jit(solution)/shard_map/ppermute | solution.py:566
  42.3 7.8 %attention.1 = (bf16[256,192]{1,0:T(8,128)(2,1)S(1)}, bf16[256,192]{1,0:T(8,128)(2,1)S(1)}, bf16[256,192]{1,0:T(8,128)(2,1)S(1)}, bf16[256,192]{1,0:T(8,128)(2,1...) custom-call(s32[1]{0:T(128)} %bitcast.pos, s32[1]{0:T(128)} %get-tuple-element.132.nb, ...), custom_call_target="tpu_custom_call" | custom-call | flops 2000000000 | bytes 1 | tf_op jit(solution)/shard_map/attention/pallas_call | solution.py:36
  50.1 5.6 %collective-permute-done.16 = bf16[96,1664]{1,0:T(8,128)(2,1)S(1)} collective-permute-done((bf16[96,1664]{1,0:T(8,128)(2,1)S(1)}, bf16[96,1664]{1,0:T(8,128)(2,1)S(1)}, u32[]{:S(2)}, u32[]{:S(2)}) %collective-permute-start.16) | collective-permute-done | bytes 319520 | tf_op jit(solution)/shard_map/ppermute | solution.py:566
  59.7 2.7 %collective-permute-done.17.a1 = bf16[256,192]{1,0:T(8,128)(2,1)S(1)} collective-permute-done((bf16[256,192]{1,0:T(8,128)(2,1)S(1)}, bf16[256,192]{1,0:T(8,128)(2,1)S(1)}, u32[]{:S(2)}, u32[]{:S(2)}) %collective-permute-start.17) | collective-permute-done | bytes 98336 | tf_op jit(solution)/shard_map/ppermute | solution.py:554
  62.4 2.7 %collective-permute-done.18.a2 = bf16[256,192]{1,0:T(8,128)(2,1)S(1)} collective-permute-done((bf16[256,192]{1,0:T(8,128)(2,1)S(1)}, bf16[256,192]{1,0:T(8,128)(2,1)S(1)}, u32[]{:S(2)}, u32[]{:S(2)}) %collective-permute-start.18) | collective-permute-done | bytes 98336 | tf_op jit(solution)/shard_map/ppermute | solution.py:554
  68.2 4.6 %collective-permute-done.21 = bf16[2,96,1664]{2,1,0:T(8,128)(2,1)S(1)} collective-permute-done((bf16[2,96,1664]{2,1,0:T(8,128)(2,1)S(1)}, bf16[2,96,1664]{2,1,0:T(8,128)(2,1)S(1)}, u32[]{:S(2)}, u32[]{:S(2)}) %collective-permute-start.21) | collective-permute-done | bytes 639008 | tf_op jit(solution)/shard_map/ppermute | solution.py:566
  73.0 3.7 %collective-permute-done.22.h1 = bf16[256,768]{1,0:T(8,128)(2,1)S(1)} collective-permute-done((bf16[256,768]{1,0:T(8,128)(2,1)S(1)}, bf16[256,768]{1,0:T(8,128)(2,1)S(1)}, u32[]{:S(2)}, u32[]{:S(2)}) %collective-permute-start.22) | collective-permute-done | bytes 393248 | tf_op jit(solution)/shard_map/ppermute | solution.py:554
  88.5 8.7 %collective-permute-done.27.rx = bf16[256,768]{1,0:T(8,128)(2,1)S(1)} collective-permute-done((bf16[256,768]{1,0:T(8,128)(2,1)S(1)}, bf16[256,768]{1,0:T(8,128)(2,1)S(1)}, u32[]{:S(2)}, u32[]{:S(2)}) %collective-permute-start.27) | collective-permute-done | bytes 393248 | tf_op jit(solution)/shard_map/ppermute | solution.py:554
  99.3 3.8 %collective-permute-done.30.sy = bf16[128,768]{1,0:T(8,128)(2,1)S(1)} collective-permute-done((bf16[128,768]{1,0:T(8,128)(2,1)S(1)}, bf16[128,768]{1,0:T(8,128)(2,1)S(1)}, u32[]{:S(2)}, u32[]{:S(2)}) %collective-permute-start.30) | collective-permute-done | bytes 196640 | tf_op jit(solution)/shard_map/ppermute | solution.py:554
  107.9 6.7 %collective-permute-done.31.g2 = bf16[256,768]{1,0:T(8,128)(2,1)S(1)} collective-permute-done((bf16[256,768]{1,0:T(8,128)(2,1)S(1)}, bf16[256,768]{1,0:T(8,128)(2,1)S(1)}, u32[]{:S(2)}, u32[]{:S(2)}) %collective-permute-start.31) | collective-permute-done | bytes 393248 | tf_op jit(solution)/shard_map/ppermute | solution.py:554
  123.8 2.5 %collective-permute-start.35 = (bf16[256,768]{1,0:T(8,128)(2,1)S(1)}, bf16[256,768]{1,0:T(8,128)(2,1)S(1)}, u32[]{:S(2)}, u32[]{:S(2)}) collective-permute-start(bf16[256,768]{1,0:T(8,128)(2,1)S(1)} %get-tuple-element.174), channel_id=1, source_target_pairs={{0,2},{1,3},{2,0},{3,1},{4,6},{5,7},{6,4},{7,5},{8,10},{9,11},{10,... | collective-permute-start | bytes 1179656 | tf_op jit(solution)/shard_map/ppermute | solution.py:554
  126.5 7.7 %collective-permute-done.35.rx = bf16[256,768]{1,0:T(8,128)(2,1)S(1)} collective-permute-done((bf16[256,768]{1,0:T(8,128)(2,1)S(1)}, bf16[256,768]{1,0:T(8,128)(2,1)S(1)}, u32[]{:S(2)}, u32[]{:S(2)}) %collective-permute-start.35) | collective-permute-done | bytes 393248 | tf_op jit(solution)/shard_map/ppermute | solution.py:554
  136.5 3.7 %ff_grad.1 = (bf16[4,96,1664]{2,1,0:T(8,128)(2,1)S(1)}, bf16[4,96,1664]{2,1,0:T(8,128)(2,1)S(1)}) custom-call(s32[1]{0:T(128)} %bitcast.pos, bf16[256,768]{1,0:T(8,128)(2,1)S(1)} %get-tuple-element.150.h.h0, bf16[256,768]{1,0:T(8,128)(2,1)S(1)} %collective-permute-done.22.h1, bf16[256,768]{1,0:T(8,128)(2,1)S(1)} %collective-permute-done.23.h2, ...), custom_call_target="tpu_custom_call" | custom-call | flops 10000000000 | bytes 1 | tf_op jit(solution)/shard_map/ff_grad/pallas_call | solution.py:36
  154.9 9.3 %attention_back.1 = (f32[4,256,192]{2,1,0:T(8,128)S(1)}, f32[4,256,512]{2,1,0:T(8,128)S(1)}, bf16[4,256,512]{2,1,0:T(8,128)(2,1)S(1)}) custom-call(s32[1]{0:T(128)} %bitcast.pos, s32[1]{0:T(128)} %get-tuple-element.132.nb, bf16[4,256,256]{2,1,0:T(8,128)(2,1)S(1)} %get-tuple-element.133.q, bf16[4,256,512]{2,1,0:T(8,128)(2,1)S(1)} %get-tuple-element.134.mine, ...), custom_call_target="tpu_custom_call" | custom-call | flops 10000000000 | bytes 1 | tf_op jit(solution)/shard_map/attention_back/pallas_call | solution.py:36
  164.4 3.0 %collective-permute-done.53 = bf16[2,96,1664]{2,1,0:T(8,128)(2,1)S(1)} collective-permute-done((bf16[2,96,1664]{2,1,0:T(8,128)(2,1)S(1)}, bf16[2,96,1664]{2,1,0:T(8,128)(2,1)S(1)}, u32[]{:S(2)}, u32[]{:S(2)}) %collective-permute-start.53) | collective-permute-done | bytes 639008 | tf_op jit(solution)/shard_map/ppermute | solution.py:566
  171.0 2.8 %collective-permute-start.47 = (bf16[256,768]{1,0:T(8,128)(2,1)S(1)}, bf16[256,768]{1,0:T(8,128)(2,1)S(1)}, u32[]{:S(2)}, u32[]{:S(2)}) collective-permute-start(bf16[256,768]{1,0:T(8,128)(2,1)S(1)} %get-tuple-element.213), channel_id=1, source_target_pairs={{0,2},{1,3},{2,0},{3,1},{4,6},{5,7},{6,4},{7,5},{8,10},{9,11},{10,... | collective-permute-start | bytes 1179656 | tf_op jit(solution)/shard_map/ppermute | solution.py:554
  173.8 8.5 %collective-permute-done.54 = bf16[96,1664]{1,0:T(8,128)(2,1)S(1)} collective-permute-done((bf16[96,1664]{1,0:T(8,128)(2,1)S(1)}, bf16[96,1664]{1,0:T(8,128)(2,1)S(1)}, u32[]{:S(2)}, u32[]{:S(2)}) %collective-permute-start.54) | collective-permute-done | bytes 319520 | tf_op jit(solution)/shard_map/ppermute | solution.py:566
  186.0 2.6 %collective-permute-start.55 = (bf16[2,96,640]{2,1,0:T(8,128)(2,1)S(1)}, bf16[2,96,640]{2,1,0:T(8,128)(2,1)S(1)}, u32[]{:S(2)}, u32[]{:S(2)}) collective-permute-start(bf16[2,96,640]{2,1,0:T(8,128)(2,1)S(1)} %slice.323), channel_id=1, source_target_pairs={{0,8},{8,0},{16,24},{24,16},{1,9},{9,1},{17,25},{25,17},{2,10},{10... | collective-permute-start | bytes 737288 | tf_op jit(solution)/shard_map/ppermute | solution.py:566
  188.6 2.7 %collective-permute-done.49 = bf16[128,768]{1,0:T(8,128)(2,1)S(1)} collective-permute-done((bf16[128,768]{1,0:T(8,128)(2,1)S(1)}, bf16[128,768]{1,0:T(8,128)(2,1)S(1)}, u32[]{:S(2)}, u32[]{:S(2)}) %collective-permute-start.49) | collective-permute-done | bytes 196640 | tf_op jit(solution)/shard_map/ppermute | solution.py:554
  195.6 3.0 %collective-permute-start.56 = (bf16[96,640]{1,0:T(8,128)(2,1)S(1)}, bf16[96,640]{1,0:T(8,128)(2,1)S(1)}, u32[]{:S(2)}, u32[]{:S(2)}) collective-permute-start(bf16[96,640]{1,0:T(8,128)(2,1)S(1)} %fusion.12), channel_id=1, source_target_pairs={{0,16},{8,24},{16,0},{24,8},{1,17},{9,25},{17,1},{25,9},{2,18},{10... | collective-permute-start | bytes 368648 | tf_op jit(solution)/shard_map/ppermute | solution.py:566
  (183 shorter events, 102.1 us)
Async XLA Ops:
  0.7 12.1 %collective-permute-start.3 = (bf16[24,768]{1,0:T(8,128)(2,1)}, bf16[24,768]{1,0:T(8,128)(2,1)S(1)}, u32[]{:S(2)}, u32[]{:S(2)}) collective-permute-start(bf16[24,768]{1,0:T(8,128)(2,1)} %param.18), channel_id=1, source_target_pairs={{0,16},{8,24},{16,0},{24,8},{1,17},{9,25},{17,1},{25,9},{2,18},{10... | collective-permute-start | bytes 110600 | tf_op jit(solution)/shard_map/ppermute | solution.py:566
  12.8 21.0 %collective-permute-start.8 = (bf16[256,768]{1,0:T(8,128)(2,1)}, bf16[256,768]{1,0:T(8,128)(2,1)S(1)}, u32[]{:S(2)}, u32[]{:S(2)}) collective-permute-start(bf16[256,768]{1,0:T(8,128)(2,1)} %x0.3), channel_id=1, source_target_pairs={{0,2},{1,3},{2,0},{3,1},{4,6},{5,7},{6,4},{7,5},{8,10},{9,11},{10,... | collective-permute-start | bytes 1179656 | tf_op jit(solution)/shard_map/ppermute | solution.py:554
  14.3 19.5 %collective-permute-start.9 = (bf16[256,768]{1,0:T(8,128)(2,1)}, bf16[256,768]{1,0:T(8,128)(2,1)S(1)}, u32[]{:S(2)}, u32[]{:S(2)}) collective-permute-start(bf16[256,768]{1,0:T(8,128)(2,1)} %x0.3), channel_id=1, source_target_pairs={{0,4},{1,5},{2,6},{3,7},{4,0},{5,1},{6,2},{7,3},{8,12},{9,13},{10,... | collective-permute-start | bytes 1179656 | tf_op jit(solution)/shard_map/ppermute | solution.py:554
  18.2 15.5 %collective-permute-start.10 = (bf16[256,768]{1,0:T(8,128)(2,1)}, bf16[256,768]{1,0:T(8,128)(2,1)S(1)}, u32[]{:S(2)}, u32[]{:S(2)}) collective-permute-start(bf16[256,768]{1,0:T(8,128)(2,1)} %x0.3), channel_id=1, source_target_pairs={{0,6},{1,7},{2,4},{3,5},{4,2},{5,3},{6,0},{7,1},{8,14},{9,15},{10,... | collective-permute-start | bytes 1179656 | tf_op jit(solution)/shard_map/ppermute | solution.py:554
  38.1 17.6 %collective-permute-start.16 = (bf16[96,1664]{1,0:T(8,128)(2,1)S(1)}, bf16[96,1664]{1,0:T(8,128)(2,1)S(1)}, u32[]{:S(2)}, u32[]{:S(2)}) collective-permute-start(bf16[96,1664]{1,0:T(8,128)(2,1)S(1)} %pad_maximum_fusion.4), channel_id=1, source_target_pairs={{0,16},{8,24},{16,0},{24,8},{1,17},{9,25},{17,1},{25,9},{2,18},{10... | collective-permute-start | bytes 958472 | tf_op jit(solution)/shard_map/ppermute | solution.py:566
  38.7 11.4 %collective-permute-start.13 = (bf16[96,768]{1,0:T(8,128)(2,1)S(1)}, bf16[96,768]{1,0:T(8,128)(2,1)S(1)}, u32[]{:S(2)}, u32[]{:S(2)}) collective-permute-start(bf16[96,768]{1,0:T(8,128)(2,1)S(1)} %pad_maximum_fusion.5), channel_id=1, source_target_pairs={{0,2},{1,3},{2,0},{3,1},{4,6},{5,7},{6,4},{7,5},{8,10},{9,11},{10,... | collective-permute-start | bytes 442376 | tf_op jit(solution)/shard_map/ppermute | solution.py:554
  39.4 10.7 %collective-permute-start.14 = (bf16[96,768]{1,0:T(8,128)(2,1)S(1)}, bf16[96,768]{1,0:T(8,128)(2,1)S(1)}, u32[]{:S(2)}, u32[]{:S(2)}) collective-permute-start(bf16[96,768]{1,0:T(8,128)(2,1)S(1)} %pad_maximum_fusion.5), channel_id=1, source_target_pairs={{0,4},{1,5},{2,6},{3,7},{4,0},{5,1},{6,2},{7,3},{8,12},{9,13},{10,... | collective-permute-start | bytes 442376 | tf_op jit(solution)/shard_map/ppermute | solution.py:554
  40.0 10.1 %collective-permute-start.15 = (bf16[96,768]{1,0:T(8,128)(2,1)S(1)}, bf16[96,768]{1,0:T(8,128)(2,1)S(1)}, u32[]{:S(2)}, u32[]{:S(2)}) collective-permute-start(bf16[96,768]{1,0:T(8,128)(2,1)S(1)} %pad_maximum_fusion.5), channel_id=1, source_target_pairs={{0,6},{1,7},{2,4},{3,5},{4,2},{5,3},{6,0},{7,1},{8,14},{9,15},{10,... | collective-permute-start | bytes 442376 | tf_op jit(solution)/shard_map/ppermute | solution.py:554
  56.0 16.8 %collective-permute-start.21 = (bf16[2,96,1664]{2,1,0:T(8,128)(2,1)S(1)}, bf16[2,96,1664]{2,1,0:T(8,128)(2,1)S(1)}, u32[]{:S(2)}, u32[]{:S(2)}) collective-permute-start(bf16[2,96,1664]{2,1,0:T(8,128)(2,1)S(1)} %pad_maximum_fusion.1), channel_id=1, source_target_pairs={{0,8},{8,0},{16,24},{24,16},{1,9},{9,1},{17,25},{25,17},{2,10},{10... | collective-permute-start | bytes 1916936 | tf_op jit(solution)/shard_map/ppermute | solution.py:566
  66.0 10.7 %collective-permute-start.22 = (bf16[256,768]{1,0:T(8,128)(2,1)S(1)}, bf16[256,768]{1,0:T(8,128)(2,1)S(1)}, u32[]{:S(2)}, u32[]{:S(2)}) collective-permute-start(bf16[256,768]{1,0:T(8,128)(2,1)S(1)} %get-tuple-element.150.h.h0), channel_id=1, source_target_pairs={{0,2},{1,3},{2,0},{3,1},{4,6},{5,7},{6,4},{7,5},{8,10},{9,11},{10,... | collective-permute-start | bytes 1179656 | tf_op jit(solution)/shard_map/ppermute | solution.py:554
  67.4 10.1 %collective-permute-start.23 = (bf16[256,768]{1,0:T(8,128)(2,1)S(1)}, bf16[256,768]{1,0:T(8,128)(2,1)S(1)}, u32[]{:S(2)}, u32[]{:S(2)}) collective-permute-start(bf16[256,768]{1,0:T(8,128)(2,1)S(1)} %get-tuple-element.150.h.h0), channel_id=1, source_target_pairs={{0,4},{1,5},{2,6},{3,7},{4,0},{5,1},{6,2},{7,3},{8,12},{9,13},{10,... | collective-permute-start | bytes 1179656 | tf_op jit(solution)/shard_map/ppermute | solution.py:554
  86.8 10.5 %collective-permute-start.27 = (bf16[256,768]{1,0:T(8,128)(2,1)S(1)}, bf16[256,768]{1,0:T(8,128)(2,1)S(1)}, u32[]{:S(2)}, u32[]{:S(2)}) collective-permute-start(bf16[256,768]{1,0:T(8,128)(2,1)S(1)} %get-tuple-element.161), channel_id=1, source_target_pairs={{0,2},{1,3},{2,0},{3,1},{4,6},{5,7},{6,4},{7,5},{8,10},{9,11},{10,... | collective-permute-start | bytes 1179656 | tf_op jit(solution)/shard_map/ppermute | solution.py:554
  88.1 10.6 %collective-permute-start.28 = (bf16[256,768]{1,0:T(8,128)(2,1)S(1)}, bf16[256,768]{1,0:T(8,128)(2,1)S(1)}, u32[]{:S(2)}, u32[]{:S(2)}) collective-permute-start(bf16[256,768]{1,0:T(8,128)(2,1)S(1)} %get-tuple-element.162), channel_id=1, source_target_pairs={{0,4},{1,5},{2,6},{3,7},{4,0},{5,1},{6,2},{7,3},{8,12},{9,13},{10,... | collective-permute-start | bytes 1179656 | tf_op jit(solution)/shard_map/ppermute | solution.py:554
  106.7 9.4 %collective-permute-start.33 = (bf16[256,768]{1,0:T(8,128)(2,1)S(1)}, bf16[256,768]{1,0:T(8,128)(2,1)S(1)}, u32[]{:S(2)}, u32[]{:S(2)}) collective-permute-start(bf16[256,768]{1,0:T(8,128)(2,1)S(1)} %get-tuple-element.164.g.g0), channel_id=1, source_target_pairs={{0,2},{1,3},{2,0},{3,1},{4,6},{5,7},{6,4},{7,5},{8,10},{9,11},{10,... | collective-permute-start | bytes 1179656 | tf_op jit(solution)/shard_map/ppermute | solution.py:554
  123.8 10.3 %collective-permute-start.35 = (bf16[256,768]{1,0:T(8,128)(2,1)S(1)}, bf16[256,768]{1,0:T(8,128)(2,1)S(1)}, u32[]{:S(2)}, u32[]{:S(2)}) collective-permute-start(bf16[256,768]{1,0:T(8,128)(2,1)S(1)} %get-tuple-element.174), channel_id=1, source_target_pairs={{0,2},{1,3},{2,0},{3,1},{4,6},{5,7},{6,4},{7,5},{8,10},{9,11},{10,... | collective-permute-start | bytes 1179656 | tf_op jit(solution)/shard_map/ppermute | solution.py:554
  126.3 10.1 %collective-permute-start.36 = (bf16[256,768]{1,0:T(8,128)(2,1)S(1)}, bf16[256,768]{1,0:T(8,128)(2,1)S(1)}, u32[]{:S(2)}, u32[]{:S(2)}) collective-permute-start(bf16[256,768]{1,0:T(8,128)(2,1)S(1)} %get-tuple-element.175), channel_id=1, source_target_pairs={{0,4},{1,5},{2,6},{3,7},{4,0},{5,1},{6,2},{7,3},{8,12},{9,13},{10,... | collective-permute-start | bytes 1179656 | tf_op jit(solution)/shard_map/ppermute | solution.py:554
  148.2 16.1 %collective-permute-start.43 = (bf16[96,896]{1,0:T(8,128)(2,1)S(1)}, bf16[96,896]{1,0:T(8,128)(2,1)S(1)}, u32[]{:S(2)}, u32[]{:S(2)}) collective-permute-start(bf16[96,896]{1,0:T(8,128)(2,1)S(1)} %get-tuple-element.244), channel_id=1, source_target_pairs={{0,2},{1,3},{2,0},{3,1},{4,6},{5,7},{6,4},{7,5},{8,10},{9,11},{10,... | collective-permute-start | bytes 516104 | tf_op jit(solution)/shard_map/ppermute | solution.py:554
  148.8 15.5 %collective-permute-start.44 = (bf16[96,896]{1,0:T(8,128)(2,1)S(1)}, bf16[96,896]{1,0:T(8,128)(2,1)S(1)}, u32[]{:S(2)}, u32[]{:S(2)}) collective-permute-start(bf16[96,896]{1,0:T(8,128)(2,1)S(1)} %get-tuple-element.243), channel_id=1, source_target_pairs={{0,4},{1,5},{2,6},{3,7},{4,0},{5,1},{6,2},{7,3},{8,12},{9,13},{10,... | collective-permute-start | bytes 516104 | tf_op jit(solution)/shard_map/ppermute | solution.py:554
  150.8 13.5 %collective-permute-start.45 = (bf16[96,896]{1,0:T(8,128)(2,1)S(1)}, bf16[96,896]{1,0:T(8,128)(2,1)S(1)}, u32[]{:S(2)}, u32[]{:S(2)}) collective-permute-start(bf16[96,896]{1,0:T(8,128)(2,1)S(1)} %get-tuple-element.242), channel_id=1, source_target_pairs={{0,6},{1,7},{2,4},{3,5},{4,2},{5,3},{6,0},{7,1},{8,14},{9,15},{10,... | collective-permute-start | bytes 516104 | tf_op jit(solution)/shard_map/ppermute | solution.py:554
  152.9 14.4 %collective-permute-start.53 = (bf16[2,96,1664]{2,1,0:T(8,128)(2,1)S(1)}, bf16[2,96,1664]{2,1,0:T(8,128)(2,1)S(1)}, u32[]{:S(2)}, u32[]{:S(2)}) collective-permute-start(bf16[2,96,1664]{2,1,0:T(8,128)(2,1)S(1)} %slice.322), channel_id=1, source_target_pairs={{0,8},{8,0},{16,24},{24,16},{1,9},{9,1},{17,25},{25,17},{2,10},{10... | collective-permute-start | bytes 1916936 | tf_op jit(solution)/shard_map/ppermute | solution.py:566
  167.5 14.8 %collective-permute-start.54 = (bf16[96,1664]{1,0:T(8,128)(2,1)S(1)}, bf16[96,1664]{1,0:T(8,128)(2,1)S(1)}, u32[]{:S(2)}, u32[]{:S(2)}) collective-permute-start(bf16[96,1664]{1,0:T(8,128)(2,1)S(1)} %fusion.8), channel_id=1, source_target_pairs={{0,16},{8,24},{16,0},{24,8},{1,17},{9,25},{17,1},{25,9},{2,18},{10... | collective-permute-start | bytes 958472 | tf_op jit(solution)/shard_map/ppermute | solution.py:566
  170.9 14.9 %collective-permute-start.51 = (bf16[4,96,640]{2,1,0:T(8,128)(2,1)S(1)}, bf16[4,96,640]{2,1,0:T(8,128)(2,1)S(1)}, u32[]{:S(2)}, u32[]{:S(2)}) collective-permute-start(bf16[4,96,640]{2,1,0:T(8,128)(2,1)S(1)} %get-tuple-element.219), channel_id=1, source_target_pairs={{0,1},{1,0},{2,3},{3,2},{4,5},{5,4},{6,7},{7,6},{8,9},{9,8},{10,11... | collective-permute-start | bytes 1474568 | tf_op jit(solution)/shard_map/ppermute | solution.py:558
  171.0 12.5 %collective-permute-start.47 = (bf16[256,768]{1,0:T(8,128)(2,1)S(1)}, bf16[256,768]{1,0:T(8,128)(2,1)S(1)}, u32[]{:S(2)}, u32[]{:S(2)}) collective-permute-start(bf16[256,768]{1,0:T(8,128)(2,1)S(1)} %get-tuple-element.213), channel_id=1, source_target_pairs={{0,2},{1,3},{2,0},{3,1},{4,6},{5,7},{6,4},{7,5},{8,10},{9,11},{10,... | collective-permute-start | bytes 1179656 | tf_op jit(solution)/shard_map/ppermute | solution.py:554
  173.8 11.2 %collective-permute-start.48 = (bf16[256,768]{1,0:T(8,128)(2,1)S(1)}, bf16[256,768]{1,0:T(8,128)(2,1)S(1)}, u32[]{:S(2)}, u32[]{:S(2)}) collective-permute-start(bf16[256,768]{1,0:T(8,128)(2,1)S(1)} %get-tuple-element.214), channel_id=1, source_target_pairs={{0,4},{1,5},{2,6},{3,7},{4,0},{5,1},{6,2},{7,3},{8,12},{9,13},{10,... | collective-permute-start | bytes 1179656 | tf_op jit(solution)/shard_map/ppermute | solution.py:554
  (44 other events, 293.6 us)

commit v6 on v5

--- a/solution.py
+++ b/solution.py
@@ -666,12 +666,12 @@
         flops=2e9,
         name="attention",
     )
-    *attended, wo1, wo2, wo3, bulk_one = lax.optimization_barrier((*attended, *wo_far, bulk_one))
+    *attended, wo1, wo2, wo3 = lax.optimization_barrier((*attended, *wo_far))
     wo_all = jnp.stack([wo_z, wo1, wo2, wo3])
     wo_other = core_swap(wo_all)
-    bulk_pair = jnp.stack([bulk, bulk_one])
+    pieces = [attended[0]] + [chip_swap(attended[k], k) for k in others]
+    bulk_pair = jnp.stack([bulk, after(bulk_one, *pieces[1:])])
     bulk_two = z_swap(bulk_pair, 1)
-    pieces = [attended[0]] + [chip_swap(attended[k], k) for k in others]
     (wo,) = call(join_wo_kernel, (pos, wo_all, wo_other), [sds((768, 768), BF16)], name="join_wo")
     hidden, xhat, rstd = call(
         norm_kernel,
@@ -757,9 +757,7 @@
     )
     sx = after(sx, ff_keep)
     ff_sum = low_add(ff_keep, core_swap(ff_send))
-    ff_got = z_swap(ff_sum[2:].astype(BF16), 1)
-    ff_left = low_add(ff_sum[1], ff_got[1]).astype(BF16)
-    ff_mine = low_add(ff_sum[0], ff_got[0])
+    ff_low = ff_sum[2:].astype(BF16)
 
     *grad_att, low_one, grad_one, sums_one = call(
         norm_one_kernel,
@@ -780,7 +778,10 @@
     wo_sum = low_add(wo_keep, wo_got)
     wo_low = [wo_sum[k].astype(BF16) for k in others]
     wo_part = [chip_swap(v, k) for v, k in zip(wo_low, others)]
-    grad_pieces = lax.optimization_barrier((*grad_pieces, *wo_low))[:4]
+    *grad_pieces, ff_low = lax.optimization_barrier((*grad_pieces, ff_low, *wo_low))[:5]
+    ff_got = z_swap(ff_low, 1)
+    ff_left = low_add(ff_sum[1], ff_got[1]).astype(BF16)
+    ff_mine = low_add(ff_sum[0], ff_got[0])
 
     dq, dmine, dother = call(
         attention_back_kernel,
@@ -793,7 +794,7 @@
         flops=1e10,
         name="attention_back",
     )
-    dgot = core_swap(after(dother, *wo_part))
+    dgot = core_swap(after(dother, *wo_part, ff_got))
     ff_far = z_swap(after(ff_left, dq), 2)
     in_own, in_x, in_y, in_rest, low, sums_qv = call(
         qkv_back_kernel,
@@ -813,16 +814,19 @@
     )
     q_got = core_swap(q_send)
     wo_mine = low_add(wo_sum[0], *wo_part)
+    q_sum = low_add(q_keep, q_got)
+    q_next = z_swap(q_sum[2:].astype(BF16), 1)
+    got_x, got_y = chip_swap(in_x, 1), chip_swap(in_y, 2)
+    got_x, got_y, q_next, ff_far = lax.optimization_barrier((got_x, got_y, q_next, ff_far))
     tm = low_add(ff_mine, ff_far)
-    q_sum = low_add(q_keep, after(q_got, ff_far))
-    q_next = z_swap(q_sum[2:].astype(BF16), 1)
     wo_mine = after(wo_mine, q_next)
     wo_next = z_swap(wo_mine[48:].astype(BF16), 1)
     wo_left = low_add(wo_mine[24:48], wo_next[24:]).astype(BF16)
     uo = low_add(wo_mine[:24], wo_next[:24], z_swap(wo_left, 2))
     q_left = low_add(q_sum[1], q_next[1]).astype(BF16)
     tq = low_add(q_sum[0], q_next[0], z_swap(q_left, 2))
-    got_x, got_y, last_x, last_y = reduce_parts(in_x, in_y, in_rest[1], in_rest[0])
+    last_y = chip_swap(low_add(in_rest[0, :128], got_x[128:]).astype(BF16), 2)
+    last_x = chip_swap(low_add(in_rest[1, 128:], got_y[128:]).astype(BF16), 1)
     input_grad = low_add(
         in_own,
         grad_one,
@@ -840,7 +844,7 @@
     ]
     gqkv, gbqv, gwo, gbo, gain, shift, gwin, gbin, gwout, gbout = call(
         finish_kernel,
-        (pos, tq, tm, *final, uo),
+        (pos, after(tq, input_grad), tm, *final, uo),
         [
             sds((24, 2304), F32),
             sds((2, 24), F32),

time: 212 us -> 210 us (level)
  waiting for transfers between devices: 95.9 us -> 85.7 us
  starting transfers between devices: 66.4 us -> 72.4 us
    ppermute x41, waiting for transfers between devices: 55.1 us -> 37.8 us  [chip_swap(): return lax.ppermute(value, 'seq', [(s, s ^ 2 * k) for s in range(8)])]
    ppermute x41, starting transfers between devices: 45.1 us -> 50.7 us  [chip_swap(): return lax.ppermute(value, 'seq', [(s, s ^ 2 * k) for s in range(8)])]
    ppermute x13, waiting for transfers between devices: 38.1 us -> 43.1 us  [z_swap(): return lax.ppermute(value, 'dp', [(i, i ^ j) for i in range(4)])]
    ppermute x8, waiting for transfers between devices: 2.63 us -> 4.86 us  [core_swap(): return lax.ppermute(value, 'seq', [(s, s ^ 1) for s in range(8)])]
  transfers between devices with their start and end apart: 62 -> 62, of which waited for: 37 -> 31; matrix products, arithmetic and copies ran while one was open for 2% -> 3% of each run, Pallas kernels for 16% -> 15%
where the time goes in v6:
time: 210 us; the launch traced here: 208 us
  waiting for transfers between devices  85.7 us (41%)
  starting transfers between devices  72.4 us (34%)
  Pallas kernels  40.8 us (19%)
  other arithmetic  4.98 us (2%)
  local copies, waits for them, and re-layouts  3.02 us (1%)
    ppermute x41, starting transfers between devices, chip_swap(): return lax.ppermute(value, 'seq', [(s, s ^ 2 * k) for s in range(8)])  50.7 us
    ppermute x13, waiting for transfers between devices, z_swap(): return lax.ppermute(value, 'dp', [(i, i ^ j) for i in range(4)])  43.1 us
    pallas_call x20, Pallas kernels, call(): pl.pallas_call(kernel, out_shape=tuple(outs), in_specs=[space(i in smem_i...  40.8 us
    ppermute x41, waiting for transfers between devices, chip_swap(): return lax.ppermute(value, 'seq', [(s, s ^ 2 * k) for s in range(8)])  37.8 us
    ppermute x13, starting transfers between devices, z_swap(): return lax.ppermute(value, 'dp', [(i, i ^ j) for i in range(4)])  20.9 us
    ppermute x8, waiting for transfers between devices, core_swap(): return lax.ppermute(value, 'seq', [(s, s ^ 1) for s in range(8)])  4.86 us
  transfers between devices with their start and end apart: 62, of which 31 were waited for; matrix products, arithmetic and copies ran while one was open for 3% of the time, Pallas kernels for 15%

profile of v6, /device:TPU:0, one launch (start us, length us, event | category | flops | bytes accessed | tf_op | source)
XLA Modules:
  0.0 208.2 jit_solution(13600907558638188254)
XLA Ops:
  0.7 4.1 %collective-permute-start.3 = (bf16[24,768]{1,0:T(8,128)(2,1)}, bf16[24,768]{1,0:T(8,128)(2,1)S(1)}, u32[]{:S(2)}, u32[]{:S(2)}) collective-permute-start(bf16[24,768]{1,0:T(8,128)(2,1)} %param.18), channel_id=1, source_target_pairs={{0,16},{8,24},{16,0},{24,8},{1,17},{9,25},{17,1},{25,9},{2,18},{10... | collective-permute-start | bytes 110600 | tf_op jit(solution)/shard_map/ppermute | solution.py:566
  18.7 2.4 %collective-permute-done.4 = bf16[48,768]{1,0:T(8,128)(2,1)S(1)} collective-permute-done((bf16[48,768]{1,0:T(8,128)(2,1)S(1)}, bf16[48,768]{1,0:T(8,128)(2,1)S(1)}, u32[]{:S(2)}, u32[]{:S(2)}) %collective-permute-start.4) | collective-permute-done | bytes 73760 | tf_op jit(solution)/shard_map/ppermute | solution.py:566
  23.0 3.9 %collective-permute-done.5 = bf16[96,640]{1,0:T(8,128)(2,1)S(1)} collective-permute-done((bf16[96,640]{1,0:T(8,128)(2,1)S(1)}, bf16[96,640]{1,0:T(8,128)(2,1)S(1)}, u32[]{:S(2)}, u32[]{:S(2)}) %collective-permute-start.5) | collective-permute-done | bytes 122912 | tf_op jit(solution)/shard_map/ppermute | solution.py:566
  27.3 3.9 %collective-permute-done.6 = bf16[96,640]{1,0:T(8,128)(2,1)S(1)} collective-permute-done((bf16[96,640]{1,0:T(8,128)(2,1)S(1)}, bf16[96,640]{1,0:T(8,128)(2,1)S(1)}, u32[]{:S(2)}, u32[]{:S(2)}) %collective-permute-start.6) | collective-permute-done | bytes 122912 | tf_op jit(solution)/shard_map/ppermute | solution.py:566
  31.3 2.4 %collective-permute-done.7 = bf16[96,640]{1,0:T(8,128)(2,1)S(1)} collective-permute-done((bf16[96,640]{1,0:T(8,128)(2,1)S(1)}, bf16[96,640]{1,0:T(8,128)(2,1)S(1)}, u32[]{:S(2)}, u32[]{:S(2)}) %collective-permute-start.7) | collective-permute-done | bytes 122912 | tf_op jit(solution)/shard_map/ppermute | solution.py:566
  40.0 2.3 %collective-permute-start.15 = (bf16[96,768]{1,0:T(8,128)(2,1)S(1)}, bf16[96,768]{1,0:T(8,128)(2,1)S(1)}, u32[]{:S(2)}, u32[]{:S(2)}) collective-permute-start(bf16[96,768]{1,0:T(8,128)(2,1)S(1)} %pad_maximum_fusion.5), channel_id=1, source_target_pairs={{0,6},{1,7},{2,4},{3,5},{4,2},{5,3},{6,0},{7,1},{8,14},{9,15},{10,... | collective-permute-start | bytes 442376 | tf_op jit(solution)/shard_map/ppermute | solution.py:554
  42.3 7.8 %attention.1 = (bf16[256,192]{1,0:T(8,128)(2,1)S(1)}, bf16[256,192]{1,0:T(8,128)(2,1)S(1)}, bf16[256,192]{1,0:T(8,128)(2,1)S(1)}, bf16[256,192]{1,0:T(8,128)(2,1...) custom-call(s32[1]{0:T(128)} %bitcast.pos, s32[1]{0:T(128)} %get-tuple-element.137.nb, ...), custom_call_target="tpu_custom_call" | custom-call | flops 2000000000 | bytes 1 | tf_op jit(solution)/shard_map/attention/pallas_call | solution.py:36
  63.1 9.5 %collective-permute-done.21 = bf16[2,96,1664]{2,1,0:T(8,128)(2,1)S(1)} collective-permute-done((bf16[2,96,1664]{2,1,0:T(8,128)(2,1)S(1)}, bf16[2,96,1664]{2,1,0:T(8,128)(2,1)S(1)}, u32[]{:S(2)}, u32[]{:S(2)}) %collective-permute-start.21) | collective-permute-done | bytes 639008 | tf_op jit(solution)/shard_map/ppermute | solution.py:566
  84.8 7.9 %collective-permute-done.27.rx = bf16[256,768]{1,0:T(8,128)(2,1)S(1)} collective-permute-done((bf16[256,768]{1,0:T(8,128)(2,1)S(1)}, bf16[256,768]{1,0:T(8,128)(2,1)S(1)}, u32[]{:S(2)}, u32[]{:S(2)}) %collective-permute-start.27) | collective-permute-done | bytes 393248 | tf_op jit(solution)/shard_map/ppermute | solution.py:554
  95.4 3.0 %collective-permute-done.30.sy = bf16[128,768]{1,0:T(8,128)(2,1)S(1)} collective-permute-done((bf16[128,768]{1,0:T(8,128)(2,1)S(1)}, bf16[128,768]{1,0:T(8,128)(2,1)S(1)}, u32[]{:S(2)}, u32[]{:S(2)}) %collective-permute-start.30) | collective-permute-done | bytes 196640 | tf_op jit(solution)/shard_map/ppermute | solution.py:554
  103.2 6.7 %collective-permute-done.31.g2 = bf16[256,768]{1,0:T(8,128)(2,1)S(1)} collective-permute-done((bf16[256,768]{1,0:T(8,128)(2,1)S(1)}, bf16[256,768]{1,0:T(8,128)(2,1)S(1)}, u32[]{:S(2)}, u32[]{:S(2)}) %collective-permute-start.31) | collective-permute-done | bytes 393248 | tf_op jit(solution)/shard_map/ppermute | solution.py:554
  120.4 2.5 %collective-permute-start.36 = (bf16[256,768]{1,0:T(8,128)(2,1)S(1)}, bf16[256,768]{1,0:T(8,128)(2,1)S(1)}, u32[]{:S(2)}, u32[]{:S(2)}) collective-permute-start(bf16[256,768]{1,0:T(8,128)(2,1)S(1)} %get-tuple-element.180), channel_id=1, source_target_pairs={{0,4},{1,5},{2,6},{3,7},{4,0},{5,1},{6,2},{7,3},{8,12},{9,13},{10,... | collective-permute-start | bytes 1179656 | tf_op jit(solution)/shard_map/ppermute | solution.py:554
  122.8 6.3 %collective-permute-done.35.rx = bf16[256,768]{1,0:T(8,128)(2,1)S(1)} collective-permute-done((bf16[256,768]{1,0:T(8,128)(2,1)S(1)}, bf16[256,768]{1,0:T(8,128)(2,1)S(1)}, u32[]{:S(2)}, u32[]{:S(2)}) %collective-permute-start.35) | collective-permute-done | bytes 393248 | tf_op jit(solution)/shard_map/ppermute | solution.py:554
  129.2 2.5 %collective-permute-start.38 = (bf16[128,768]{1,0:T(8,128)(2,1)S(1)}, bf16[128,768]{1,0:T(8,128)(2,1)S(1)}, u32[]{:S(2)}, u32[]{:S(2)}) collective-permute-start(bf16[128,768]{1,0:T(8,128)(2,1)S(1)} %add_convert_fusion), channel_id=1, source_target_pairs={{0,4},{1,5},{2,6},{3,7},{4,0},{5,1},{6,2},{7,3},{8,12},{9,13},{10,... | collective-permute-start | bytes 589832 | tf_op jit(solution)/shard_map/ppermute | solution.py:554
  133.0 3.7 %ff_grad.1 = (bf16[4,96,1664]{2,1,0:T(8,128)(2,1)S(1)}, bf16[4,96,1664]{2,1,0:T(8,128)(2,1)S(1)}) custom-call(s32[1]{0:T(128)} %bitcast.pos, bf16[256,768]{1,0:T(8,128)(2,1)S(1)} %get-tuple-element.153.h.h0, bf16[256,768]{1,0:T(8,128)(2,1)S(1)} %collective-permute-done.22.h1, bf16[256,768]{1,0:T(8,128)(2,1)S(1)} %collective-permute-done.23.h2, ...), custom_call_target="tpu_custom_call" | custom-call | flops 10000000000 | bytes 1 | tf_op jit(solution)/shard_map/ff_grad/pallas_call | solution.py:36
  141.0 2.4 %collective-permute-start.41 = (bf16[256,192]{1,0:T(8,128)(2,1)S(1)}, bf16[256,192]{1,0:T(8,128)(2,1)S(1)}, u32[]{:S(2)}, u32[]{:S(2)}) collective-permute-start(bf16[256,192]{1,0:T(8,128)(2,1)S(1)} %get-tuple-element.199), channel_id=1, source_target_pairs={{0,6},{1,7},{2,4},{3,5},{4,2},{5,3},{6,0},{7,1},{8,14},{9,15},{10,... | collective-permute-start | bytes 294920 | tf_op jit(solution)/shard_map/ppermute | solution.py:554
  147.5 2.6 %collective-permute-done.40.g2 = bf16[256,192]{1,0:T(8,128)(2,1)S(1)} collective-permute-done((bf16[256,192]{1,0:T(8,128)(2,1)S(1)}, bf16[256,192]{1,0:T(8,128)(2,1)S(1)}, u32[]{:S(2)}, u32[]{:S(2)}) %collective-permute-start.40) | collective-permute-done | bytes 98336 | tf_op jit(solution)/shard_map/ppermute | solution.py:554
  151.8 9.3 %attention_back.1 = (f32[4,256,192]{2,1,0:T(8,128)S(1)}, f32[4,256,512]{2,1,0:T(8,128)S(1)}, bf16[4,256,512]{2,1,0:T(8,128)(2,1)S(1)}) custom-call(s32[1]{0:T(128)} %bitcast.pos, s32[1]{0:T(128)} %get-tuple-element.137.nb, bf16[4,256,256]{2,1,0:T(8,128)(2,1)S(1)} %get-tuple-element.138.q, bf16[4,256,512]{2,1,0:T(8,128)(2,1)S(1)} %get-tuple-element.139.mine, ...), custom_call_target="tpu_custom_call" | custom-call | flops 10000000000 | bytes 1 | tf_op jit(solution)/shard_map/attention_back/pallas_call | solution.py:36
  161.2 3.8 %collective-permute-done.47 = bf16[2,96,1664]{2,1,0:T(8,128)(2,1)S(1)} collective-permute-done((bf16[2,96,1664]{2,1,0:T(8,128)(2,1)S(1)}, bf16[2,96,1664]{2,1,0:T(8,128)(2,1)S(1)}, u32[]{:S(2)}, u32[]{:S(2)}) %collective-permute-start.47) | collective-permute-done | bytes 639008 | tf_op jit(solution)/shard_map/ppermute | solution.py:566
  165.0 2.7 %collective-permute-done.48.dother = bf16[4,256,512]{2,1,0:T(8,128)(2,1)S(1)} collective-permute-done((bf16[4,256,512]{2,1,0:T(8,128)(2,1)S(1)}, bf16[4,256,512]{2,1,0:T(8,128)(2,1)S(1)}, u32[]{:S(2)}, u32[]{:S(2)}) %collective-permute-start.48) | collective-permute-done | bytes 1048608 | tf_op jit(solution)/shard_map/ppermute | solution.py:558
  171.0 2.6 %collective-permute-start.53 = (bf16[96,1664]{1,0:T(8,128)(2,1)S(1)}, bf16[96,1664]{1,0:T(8,128)(2,1)S(1)}, u32[]{:S(2)}, u32[]{:S(2)}) collective-permute-start(bf16[96,1664]{1,0:T(8,128)(2,1)S(1)} %fusion.8), channel_id=1, source_target_pairs={{0,16},{8,24},{16,0},{24,8},{1,17},{9,25},{17,1},{25,9},{2,18},{10... | collective-permute-start | bytes 958472 | tf_op jit(solution)/shard_map/ppermute | solution.py:566
  177.6 11.0 %collective-permute-done.53 = bf16[96,1664]{1,0:T(8,128)(2,1)S(1)} collective-permute-done((bf16[96,1664]{1,0:T(8,128)(2,1)S(1)}, bf16[96,1664]{1,0:T(8,128)(2,1)S(1)}, u32[]{:S(2)}, u32[]{:S(2)}) %collective-permute-start.53) | collective-permute-done | bytes 319520 | tf_op jit(solution)/shard_map/ppermute | solution.py:566
  189.5 3.4 %collective-permute-start.56 = (bf16[96,640]{1,0:T(8,128)(2,1)S(1)}, bf16[96,640]{1,0:T(8,128)(2,1)S(1)}, u32[]{:S(2)}, u32[]{:S(2)}) collective-permute-start(bf16[96,640]{1,0:T(8,128)(2,1)S(1)} %fusion.12), channel_id=1, source_target_pairs={{0,16},{8,24},{16,0},{24,8},{1,17},{9,25},{17,1},{25,9},{2,18},{10... | collective-permute-start | bytes 368648 | tf_op jit(solution)/shard_map/ppermute | solution.py:566
  196.1 4.1 %collective-permute-done.56 = bf16[96,640]{1,0:T(8,128)(2,1)S(1)} collective-permute-done((bf16[96,640]{1,0:T(8,128)(2,1)S(1)}, bf16[96,640]{1,0:T(8,128)(2,1)S(1)}, u32[]{:S(2)}, u32[]{:S(2)}) %collective-permute-start.56) | collective-permute-done | bytes 122912 | tf_op jit(solution)/shard_map/ppermute | solution.py:566
  (189 shorter events, 96.1 us)
Async XLA Ops:
  0.7 12.1 %collective-permute-start.3 = (bf16[24,768]{1,0:T(8,128)(2,1)}, bf16[24,768]{1,0:T(8,128)(2,1)S(1)}, u32[]{:S(2)}, u32[]{:S(2)}) collective-permute-start(bf16[24,768]{1,0:T(8,128)(2,1)} %param.18), channel_id=1, source_target_pairs={{0,16},{8,24},{16,0},{24,8},{1,17},{9,25},{17,1},{25,9},{2,18},{10... | collective-permute-start | bytes 110600 | tf_op jit(solution)/shard_map/ppermute | solution.py:566
  12.8 21.0 %collective-permute-start.8 = (bf16[256,768]{1,0:T(8,128)(2,1)}, bf16[256,768]{1,0:T(8,128)(2,1)S(1)}, u32[]{:S(2)}, u32[]{:S(2)}) collective-permute-start(bf16[256,768]{1,0:T(8,128)(2,1)} %x0.3), channel_id=1, source_target_pairs={{0,2},{1,3},{2,0},{3,1},{4,6},{5,7},{6,4},{7,5},{8,10},{9,11},{10,... | collective-permute-start | bytes 1179656 | tf_op jit(solution)/shard_map/ppermute | solution.py:554
  14.3 19.5 %collective-permute-start.9 = (bf16[256,768]{1,0:T(8,128)(2,1)}, bf16[256,768]{1,0:T(8,128)(2,1)S(1)}, u32[]{:S(2)}, u32[]{:S(2)}) collective-permute-start(bf16[256,768]{1,0:T(8,128)(2,1)} %x0.3), channel_id=1, source_target_pairs={{0,4},{1,5},{2,6},{3,7},{4,0},{5,1},{6,2},{7,3},{8,12},{9,13},{10,... | collective-permute-start | bytes 1179656 | tf_op jit(solution)/shard_map/ppermute | solution.py:554
  18.2 15.5 %collective-permute-start.10 = (bf16[256,768]{1,0:T(8,128)(2,1)}, bf16[256,768]{1,0:T(8,128)(2,1)S(1)}, u32[]{:S(2)}, u32[]{:S(2)}) collective-permute-start(bf16[256,768]{1,0:T(8,128)(2,1)} %x0.3), channel_id=1, source_target_pairs={{0,6},{1,7},{2,4},{3,5},{4,2},{5,3},{6,0},{7,1},{8,14},{9,15},{10,... | collective-permute-start | bytes 1179656 | tf_op jit(solution)/shard_map/ppermute | solution.py:554
  38.1 17.6 %collective-permute-start.20 = (bf16[96,1664]{1,0:T(8,128)(2,1)S(1)}, bf16[96,1664]{1,0:T(8,128)(2,1)S(1)}, u32[]{:S(2)}, u32[]{:S(2)}) collective-permute-start(bf16[96,1664]{1,0:T(8,128)(2,1)S(1)} %pad_maximum_fusion.4), channel_id=1, source_target_pairs={{0,16},{8,24},{16,0},{24,8},{1,17},{9,25},{17,1},{25,9},{2,18},{10... | collective-permute-start | bytes 958472 | tf_op jit(solution)/shard_map/ppermute | solution.py:566
  38.7 11.4 %collective-permute-start.13 = (bf16[96,768]{1,0:T(8,128)(2,1)S(1)}, bf16[96,768]{1,0:T(8,128)(2,1)S(1)}, u32[]{:S(2)}, u32[]{:S(2)}) collective-permute-start(bf16[96,768]{1,0:T(8,128)(2,1)S(1)} %pad_maximum_fusion.5), channel_id=1, source_target_pairs={{0,2},{1,3},{2,0},{3,1},{4,6},{5,7},{6,4},{7,5},{8,10},{9,11},{10,... | collective-permute-start | bytes 442376 | tf_op jit(solution)/shard_map/ppermute | solution.py:554
  39.4 10.7 %collective-permute-start.14 = (bf16[96,768]{1,0:T(8,128)(2,1)S(1)}, bf16[96,768]{1,0:T(8,128)(2,1)S(1)}, u32[]{:S(2)}, u32[]{:S(2)}) collective-permute-start(bf16[96,768]{1,0:T(8,128)(2,1)S(1)} %pad_maximum_fusion.5), channel_id=1, source_target_pairs={{0,4},{1,5},{2,6},{3,7},{4,0},{5,1},{6,2},{7,3},{8,12},{9,13},{10,... | collective-permute-start | bytes 442376 | tf_op jit(solution)/shard_map/ppermute | solution.py:554
  40.0 10.1 %collective-permute-start.15 = (bf16[96,768]{1,0:T(8,128)(2,1)S(1)}, bf16[96,768]{1,0:T(8,128)(2,1)S(1)}, u32[]{:S(2)}, u32[]{:S(2)}) collective-permute-start(bf16[96,768]{1,0:T(8,128)(2,1)S(1)} %pad_maximum_fusion.5), channel_id=1, source_target_pairs={{0,6},{1,7},{2,4},{3,5},{4,2},{5,3},{6,0},{7,1},{8,14},{9,15},{10,... | collective-permute-start | bytes 442376 | tf_op jit(solution)/shard_map/ppermute | solution.py:554
  58.3 14.3 %collective-permute-start.21 = (bf16[2,96,1664]{2,1,0:T(8,128)(2,1)S(1)}, bf16[2,96,1664]{2,1,0:T(8,128)(2,1)S(1)}, u32[]{:S(2)}, u32[]{:S(2)}) collective-permute-start(bf16[2,96,1664]{2,1,0:T(8,128)(2,1)S(1)} %pad_maximum_fusion.1), channel_id=1, source_target_pairs={{0,8},{8,0},{16,24},{24,16},{1,9},{9,1},{17,25},{25,17},{2,10},{10... | collective-permute-start | bytes 1916936 | tf_op jit(solution)/shard_map/ppermute | solution.py:566
  60.7 12.1 %collective-permute-start.22 = (bf16[256,768]{1,0:T(8,128)(2,1)S(1)}, bf16[256,768]{1,0:T(8,128)(2,1)S(1)}, u32[]{:S(2)}, u32[]{:S(2)}) collective-permute-start(bf16[256,768]{1,0:T(8,128)(2,1)S(1)} %get-tuple-element.153.h.h0), channel_id=1, source_target_pairs={{0,2},{1,3},{2,0},{3,1},{4,6},{5,7},{6,4},{7,5},{8,10},{9,11},{10,... | collective-permute-start | bytes 1179656 | tf_op jit(solution)/shard_map/ppermute | solution.py:554
  62.0 10.7 %collective-permute-start.23 = (bf16[256,768]{1,0:T(8,128)(2,1)S(1)}, bf16[256,768]{1,0:T(8,128)(2,1)S(1)}, u32[]{:S(2)}, u32[]{:S(2)}) collective-permute-start(bf16[256,768]{1,0:T(8,128)(2,1)S(1)} %get-tuple-element.153.h.h0), channel_id=1, source_target_pairs={{0,4},{1,5},{2,6},{3,7},{4,0},{5,1},{6,2},{7,3},{8,12},{9,13},{10,... | collective-permute-start | bytes 1179656 | tf_op jit(solution)/shard_map/ppermute | solution.py:554
  82.2 10.5 %collective-permute-start.27 = (bf16[256,768]{1,0:T(8,128)(2,1)S(1)}, bf16[256,768]{1,0:T(8,128)(2,1)S(1)}, u32[]{:S(2)}, u32[]{:S(2)}) collective-permute-start(bf16[256,768]{1,0:T(8,128)(2,1)S(1)} %get-tuple-element.166), channel_id=1, source_target_pairs={{0,2},{1,3},{2,0},{3,1},{4,6},{5,7},{6,4},{7,5},{8,10},{9,11},{10,... | collective-permute-start | bytes 1179656 | tf_op jit(solution)/shard_map/ppermute | solution.py:554
  83.3 11.0 %collective-permute-start.28 = (bf16[256,768]{1,0:T(8,128)(2,1)S(1)}, bf16[256,768]{1,0:T(8,128)(2,1)S(1)}, u32[]{:S(2)}, u32[]{:S(2)}) collective-permute-start(bf16[256,768]{1,0:T(8,128)(2,1)S(1)} %get-tuple-element.167), channel_id=1, source_target_pairs={{0,4},{1,5},{2,6},{3,7},{4,0},{5,1},{6,2},{7,3},{8,12},{9,13},{10,... | collective-permute-start | bytes 1179656 | tf_op jit(solution)/shard_map/ppermute | solution.py:554
  120.4 11.4 %collective-permute-start.36 = (bf16[256,768]{1,0:T(8,128)(2,1)S(1)}, bf16[256,768]{1,0:T(8,128)(2,1)S(1)}, u32[]{:S(2)}, u32[]{:S(2)}) collective-permute-start(bf16[256,768]{1,0:T(8,128)(2,1)S(1)} %get-tuple-element.180), channel_id=1, source_target_pairs={{0,4},{1,5},{2,6},{3,7},{4,0},{5,1},{6,2},{7,3},{8,12},{9,13},{10,... | collective-permute-start | bytes 1179656 | tf_op jit(solution)/shard_map/ppermute | solution.py:554
  143.5 17.6 %collective-permute-start.44 = (bf16[96,896]{1,0:T(8,128)(2,1)S(1)}, bf16[96,896]{1,0:T(8,128)(2,1)S(1)}, u32[]{:S(2)}, u32[]{:S(2)}) collective-permute-start(bf16[96,896]{1,0:T(8,128)(2,1)S(1)} %get-tuple-element.254), channel_id=1, source_target_pairs={{0,2},{1,3},{2,0},{3,1},{4,6},{5,7},{6,4},{7,5},{8,10},{9,11},{10,... | collective-permute-start | bytes 516104 | tf_op jit(solution)/shard_map/ppermute | solution.py:554
  144.7 16.4 %collective-permute-start.45 = (bf16[96,896]{1,0:T(8,128)(2,1)S(1)}, bf16[96,896]{1,0:T(8,128)(2,1)S(1)}, u32[]{:S(2)}, u32[]{:S(2)}) collective-permute-start(bf16[96,896]{1,0:T(8,128)(2,1)S(1)} %get-tuple-element.253), channel_id=1, source_target_pairs={{0,4},{1,5},{2,6},{3,7},{4,0},{5,1},{6,2},{7,3},{8,12},{9,13},{10,... | collective-permute-start | bytes 516104 | tf_op jit(solution)/shard_map/ppermute | solution.py:554
  146.1 15.0 %collective-permute-start.46 = (bf16[96,896]{1,0:T(8,128)(2,1)S(1)}, bf16[96,896]{1,0:T(8,128)(2,1)S(1)}, u32[]{:S(2)}, u32[]{:S(2)}) collective-permute-start(bf16[96,896]{1,0:T(8,128)(2,1)S(1)} %get-tuple-element.252), channel_id=1, source_target_pairs={{0,6},{1,7},{2,4},{3,5},{4,2},{5,3},{6,0},{7,1},{8,14},{9,15},{10,... | collective-permute-start | bytes 516104 | tf_op jit(solution)/shard_map/ppermute | solution.py:554
  150.1 14.8 %collective-permute-start.47 = (bf16[2,96,1664]{2,1,0:T(8,128)(2,1)S(1)}, bf16[2,96,1664]{2,1,0:T(8,128)(2,1)S(1)}, u32[]{:S(2)}, u32[]{:S(2)}) collective-permute-start(bf16[2,96,1664]{2,1,0:T(8,128)(2,1)S(1)} %slice.310), channel_id=1, source_target_pairs={{0,8},{8,0},{16,24},{24,16},{1,9},{9,1},{17,25},{25,17},{2,10},{10... | collective-permute-start | bytes 1916936 | tf_op jit(solution)/shard_map/ppermute | solution.py:566
  171.0 17.7 %collective-permute-start.53 = (bf16[96,1664]{1,0:T(8,128)(2,1)S(1)}, bf16[96,1664]{1,0:T(8,128)(2,1)S(1)}, u32[]{:S(2)}, u32[]{:S(2)}) collective-permute-start(bf16[96,1664]{1,0:T(8,128)(2,1)S(1)} %fusion.8), channel_id=1, source_target_pairs={{0,16},{8,24},{16,0},{24,8},{1,17},{9,25},{17,1},{25,9},{2,18},{10... | collective-permute-start | bytes 958472 | tf_op jit(solution)/shard_map/ppermute | solution.py:566
  173.6 15.1 %collective-permute-start.49 = (bf16[256,768]{1,0:T(8,128)(2,1)S(1)}, bf16[256,768]{1,0:T(8,128)(2,1)S(1)}, u32[]{:S(2)}, u32[]{:S(2)}) collective-permute-start(bf16[256,768]{1,0:T(8,128)(2,1)S(1)} %get-tuple-element.220), channel_id=1, source_target_pairs={{0,2},{1,3},{2,0},{3,1},{4,6},{5,7},{6,4},{7,5},{8,10},{9,11},{10,... | collective-permute-start | bytes 1179656 | tf_op jit(solution)/shard_map/ppermute | solution.py:554
  174.4 14.3 %collective-permute-start.50 = (bf16[256,768]{1,0:T(8,128)(2,1)S(1)}, bf16[256,768]{1,0:T(8,128)(2,1)S(1)}, u32[]{:S(2)}, u32[]{:S(2)}) collective-permute-start(bf16[256,768]{1,0:T(8,128)(2,1)S(1)} %get-tuple-element.221), channel_id=1, source_target_pairs={{0,4},{1,5},{2,6},{3,7},{4,0},{5,1},{6,2},{7,3},{8,12},{9,13},{10,... | collective-permute-start | bytes 1179656 | tf_op jit(solution)/shard_map/ppermute | solution.py:554
  175.8 13.1 %collective-permute-start.52 = (bf16[2,96,640]{2,1,0:T(8,128)(2,1)S(1)}, bf16[2,96,640]{2,1,0:T(8,128)(2,1)S(1)}, u32[]{:S(2)}, u32[]{:S(2)}) collective-permute-start(bf16[2,96,640]{2,1,0:T(8,128)(2,1)S(1)} %slice.311), channel_id=1, source_target_pairs={{0,8},{8,0},{16,24},{24,16},{1,9},{9,1},{17,25},{25,17},{2,10},{10... | collective-permute-start | bytes 737288 | tf_op jit(solution)/shard_map/ppermute | solution.py:566
  189.5 10.7 %collective-permute-start.56 = (bf16[96,640]{1,0:T(8,128)(2,1)S(1)}, bf16[96,640]{1,0:T(8,128)(2,1)S(1)}, u32[]{:S(2)}, u32[]{:S(2)}) collective-permute-start(bf16[96,640]{1,0:T(8,128)(2,1)S(1)} %fusion.12), channel_id=1, source_target_pairs={{0,16},{8,24},{16,0},{24,8},{1,17},{9,25},{17,1},{25,9},{2,18},{10... | collective-permute-start | bytes 368648 | tf_op jit(solution)/shard_map/ppermute | solution.py:566
  193.1 10.9 %collective-permute-start.54 = (bf16[128,768]{1,0:T(8,128)(2,1)S(1)}, bf16[128,768]{1,0:T(8,128)(2,1)S(1)}, u32[]{:S(2)}, u32[]{:S(2)}) collective-permute-start(bf16[128,768]{1,0:T(8,128)(2,1)S(1)} %get-tuple-element.250), channel_id=1, source_target_pairs={{0,4},{1,5},{2,6},{3,7},{4,0},{5,1},{6,2},{7,3},{8,12},{9,13},{10,... | collective-permute-start | bytes 589832 | tf_op jit(solution)/shard_map/ppermute | solution.py:554
  (48 other events, 331.4 us)
